TPU v7x, 512 devices: a whole 4x8x8 slice. The times are simulated.
512 devices in a mesh: member: 8 (over z_lo, core), tile: 64 (over z_hi, x, y).
Axes of the slice: x: 4, y: 8, z: 8 (z_hi: 2, z_lo: 4; z = z_hi * 4 + z_lo), core: 2. Of those that a mesh axis runs over, the one named last changes fastest.
Arguments:
- inputs: bfloat16 [8, 32768, 512], P('member', 'tile'), may hold values from -6 to 6
- noise: bfloat16 [8, 32768, 128], P('member', 'tile'), may hold values from -6 to 6
- neighbours: int32 [8, 32768], P(None, 'tile'), may hold values from 0 to 639, as said below
- region_map: int32 [64], P('tile'), may hold values from 0 to 7, as said below
- msg_weight: bfloat16 [512, 512], replicated, may hold values from -0.25 to 0.25
- up_weight: bfloat16 [512, 1024], replicated, may hold values from -0.25 to 0.25
- down_weight: bfloat16 [1024, 512], replicated, may hold values from -0.1875 to 0.1875
- student_in: bfloat16 [512, 512], replicated, may hold values from -0.25 to 0.25
- student_noise: bfloat16 [128, 512], replicated, may hold values from -0.5 to 0.5
- student_out: bfloat16 [512, 512], replicated, may hold values from -0.25 to 0.25
Outputs:
- teacher_out: bfloat16 [8, 32768, 512], P('member', 'tile')
- region_loss: float32 [8], replicated
- grad_in: float32 [512, 512], P('tile')
- grad_noise: float32 [128, 512], P('tile')
- grad_out: float32 [512, 512], P('tile')
Inputs may be any that keep to these rules, and one draw needn't show every extreme that they name: `neighbours`: each index lies within 64 of the cell's own row (its row plus 64); the first index of a tile's first cell is 0 and that of its last cell is 639. `region_map`: each region holds 8 tiles.
All inputs are finite; a program needn't handle non-finite values.
Results may differ from a plain program's by a relative error of at most 0.0039.
The roundings to bfloat16 on the way count: a program that leaves them out, or rounds other values in their place, can miss the bound.
Values may be sent and summed in bfloat16 or wider, within the bound.
No kernel may reach another device: no remote copies, remote signals or barrier semaphores. Data moves between devices by JAX's collectives and lax.ppermute only.
A program may use at most 64 MiB of HBM per device.

v0:
```python
import math

import jax
import jax.numpy as jnp
from jax import lax
from jax.sharding import Mesh
from jax.sharding import PartitionSpec as P

D = 512
HALO = 64
REGIONS = 8
MEMBER = ("member_0", "member_1")
TILE = ("tile_0", "tile_1", "tile_2")
MEMBER_TILE = ("member_0", "member_1", "tile_0", "tile_1", "tile_2")


def with_halo(cells, sides, width):
    for axis, dim in sides:
        count = lax.axis_size(axis)
        ends = count - 1
        head = lax.slice_in_dim(cells, 0, width, axis=dim)
        tail = lax.slice_in_dim(cells, cells.shape[dim] - width, cells.shape[dim], axis=dim)
        cells = jnp.concatenate(
            [
                lax.ppermute(tail, axis, [(i, (i + 1) % count) for i in range(ends)]),
                cells,
                lax.ppermute(head, axis, [((i + 1) % count, i) for i in range(ends)]),
            ],
            axis=dim,
        )
    return cells


def one_axis_at_a_time(array, axes):
    for axis in axes:
        array = lax.psum(array, axis)
    return array


def sent_together(arrays, axis, dim, along):
    both = jnp.concatenate(arrays, axis=along)
    result, at, gathered = (lax.psum_scatter(both, axis, scatter_dimension=dim, tiled=True), 0, [])
    for a in arrays:
        gathered.append(lax.slice_in_dim(result, at, at + a.shape[along], axis=along))
        at += a.shape[along]
    return tuple(gathered)


def split_up(array, dim, devices):
    shape = array.shape
    tiles = array.reshape(*shape[:dim], devices, shape[dim] // devices, *shape[dim + 1 :])
    return jnp.moveaxis(tiles, dim, 0)


def sent_and_summed(array, axis, dim):
    tiles = split_up(array, dim, lax.axis_size(axis))
    arrived = lax.all_to_all(tiles, axis, split_axis=0, concat_axis=0, tiled=True)
    return arrived.sum(axis=0)


def gather_turned(arrays, axis, dims):
    turned = [jnp.moveaxis(a, dim, 0) for a, dim in zip(arrays, dims)]
    widths = [t[0].size for t in turned]
    both = jnp.concatenate([t.reshape(-1, w) for t, w in zip(turned, widths)], axis=1)
    result = lax.all_gather(both, axis, axis=0, tiled=True)
    tiles = jnp.split(result, [sum(widths[:k]) for k in range(1, len(widths))], axis=1)
    return tuple(
        (
            jnp.moveaxis(b.reshape(-1, *t.shape[1:]), 0, dim)
            for b, t, dim in zip(tiles, turned, dims)
        )
    )


def smooth(diff):
    return jnp.sqrt(diff * diff + 0.01) - 0.1


def smooth_grad(diff):
    return diff / jnp.sqrt(diff * diff + 0.01)


def silu_grad(value):
    sig = jax.nn.sigmoid(value)
    return sig * (1.0 + value * (1.0 - sig))


def on_device(
    inputs,
    noise,
    neighbours,
    region_map,
    msg_weight,
    up_weight,
    down_weight,
    student_in,
    student_noise,
    student_out,
):
    state = inputs[0]
    draws = noise[0]
    cells = state.shape[0]
    width = state.shape[1]
    members = lax.axis_size(MEMBER)
    tiles = lax.axis_size(TILE)
    cells_all = cells * tiles
    extended = with_halo(state, ((TILE, 0),), HALO)
    total = jnp.zeros((cells, width), jnp.float32)
    for column in range(neighbours.shape[0]):
        total = total + jnp.take(extended, neighbours[column], axis=0).astype(jnp.float32)
    gathered = (total / neighbours.shape[0]).astype(jnp.bfloat16)
    resid = state.astype(jnp.float32) + jnp.dot(
        gathered, msg_weight, preferred_element_type=jnp.float32
    )
    normed = (resid * lax.rsqrt(jnp.mean(resid * resid, axis=1, keepdims=True) + 1e-06)).astype(
        jnp.bfloat16
    )
    hidden = jax.nn.silu(jnp.dot(normed, up_weight, preferred_element_type=jnp.float32)).astype(
        jnp.bfloat16
    )
    teacher_state = (
        resid + jnp.dot(hidden, down_weight, preferred_element_type=jnp.float32)
    ).astype(jnp.bfloat16)
    preact = jnp.dot(state, student_in, preferred_element_type=jnp.float32) + jnp.dot(
        draws, student_noise, preferred_element_type=jnp.float32
    )
    shidden = jax.nn.silu(preact).astype(jnp.bfloat16)
    student = (
        state.astype(jnp.float32)
        + jnp.dot(shidden, student_out, preferred_element_type=jnp.float32)
    ).astype(jnp.bfloat16)
    block = cells // members
    scale = 1.0 / math.sqrt(cells_all)
    packed = (
        student.reshape(1, members, block, width),
        teacher_state.reshape(1, members, block, width),
    )
    own_s = lax.all_to_all(packed[0], MEMBER, split_axis=1, concat_axis=0, tiled=True)
    own_t = lax.all_to_all(packed[1], MEMBER, split_axis=1, concat_axis=0, tiled=True)
    s_all = own_s[:, 0].astype(jnp.float32)
    t_all = own_t[:, 0].astype(jnp.float32)

    def visit(carry, other):
        grads, losses = carry
        other_s, other_t = other
        cross = s_all - other_t[None]
        within = s_all - other_s[None]
        grads = (
            grads
            + smooth_grad(cross) / (members * members)
            - smooth_grad(within) / (members * (members - 1))
        )
        losses = losses + jnp.sum(
            smooth(cross) / (members * members) - smooth(within) / (2 * members * (members - 1)),
            axis=(0, 2),
        )
        return ((grads, losses), None)

    start = (jnp.zeros_like(s_all), jnp.zeros((s_all.shape[1],), jnp.float32))
    (grads, losses), _ = lax.scan(visit, start, (s_all, t_all))
    gsend = (grads * scale).astype(jnp.bfloat16)[:, None]
    returned = lax.all_to_all(gsend, MEMBER, split_axis=0, concat_axis=1, tiled=True)
    returned, cell_loss = (returned, losses[None, None, :])
    gstudent = returned.reshape(cells, width)
    local_loss = jnp.sum(cell_loss)
    onehot = (region_map[0] == jnp.arange(REGIONS, dtype=jnp.int32)).astype(
        jnp.float32
    ) * local_loss
    region_loss = one_axis_at_a_time(onehot, MEMBER_TILE) / (cells_all // REGIONS * D)
    acc_out = jnp.dot(shidden.T, gstudent, preferred_element_type=jnp.float32)
    gpre = (
        jnp.dot(gstudent, student_out.T, preferred_element_type=jnp.float32) * silu_grad(preact)
    ).astype(jnp.bfloat16)
    acc_in = jnp.dot(state.T, gpre, preferred_element_type=jnp.float32)
    acc_noise = jnp.dot(draws.T, gpre, preferred_element_type=jnp.float32)
    columns = sent_together((acc_in, acc_noise, acc_out), MEMBER, 1, 0)
    rows = (
        sent_and_summed(columns[0], TILE, 0),
        sent_and_summed(columns[1], TILE, 0),
        sent_and_summed(columns[2], TILE, 0),
    )
    grad_in, grad_noise, grad_out = gather_turned((rows[0], rows[1], rows[2]), MEMBER, (1, 1, 1))
    return (teacher_state[None], region_loss, grad_in, grad_noise, grad_out)


def solution(mesh):
    split = Mesh(
        mesh.devices.reshape(4, 2, 2, 4, 8), ("member_0", "member_1", "tile_0", "tile_1", "tile_2")
    )
    in_specs = (
        P(MEMBER, TILE, None),
        P(MEMBER, TILE, None),
        P(None, TILE),
        P(TILE),
        P(),
        P(),
        P(),
        P(),
        P(),
        P(),
    )
    out_specs = (P(MEMBER, TILE, None), P(), P(TILE, None), P(TILE, None), P(TILE, None))
    return jax.shard_map(
        on_device, mesh=split, in_specs=in_specs, out_specs=out_specs, check_vma=False
    )
```

profile of v0, /device:TPU:1, one launch (start us, length us, event | category | flops | bytes accessed | tf_op | source)
XLA Modules:
  0.0 294.8 jit_solution(13278847133362019718)
XLA Ops:
  8.2 4.0 %collective-permute-start = (bf16[64,512]{1,0:T(8,128)(2,1)S(1)}, bf16[64,512]{1,0:T(8,128)(2,1)S(1)}, u32[]{:S(2)}, u32[]{:S(2)}) collective-permute-start(bf16[64,512]{1,0:T(8,128)(2,1)S(1)} %get-tuple-element.122), channel_id=1, source_target_pairs={{0,1},{1,2},{2,3},{3,4},{4,5},{5,6},{6,7},{7,8},{8,9},{9,10},{10,1... | collective-permute-start | bytes 196616 | tf_op jit(solution)/shard_map/ppermute | solution.py:25
  16.9 8.2 %all-to-all-start.1 = ((bf16[1,8,64,512]{3,2,0,1:T(8,128)(2,1)}), bf16[1,8,64,512]{3,2,0,1:T(8,128)(2,1)S(1)}, u32[]{:S(2)}, u32[]{:S(2)}) async-start(bf16[1,8,64,512]{3,2,0,1:T(8,128)(2,1)} %bitcast.18), calls=%async_computation.1 | async-start | bytes 1048576 | tf_op jit(solution)/shard_map/all_to_all | solution.py:138
  32.7 2.6 gather_fusion.5
  35.4 2.6 gather_fusion.6
  40.6 2.6 gather_fusion
  43.2 2.6 gather_fusion.1
  45.9 4.4 %multiply_reduce_fusion = (f32[512]{0:T(512)S(1)}, f32[512,512]{1,0:T(8,128)}) fusion(bf16[512,512]{1,0:T(8,128)(2,1)} %param.18, bf16[512,512]{1,0:T(8,128)(2,1)} %gather_fusion.7, bf16[512,512]{1,0:T(8,128)(2,1)} %gather_fusion.6, bf16[512,512]{1,0:T(8,128)(2,1)} %gather_fusion.5, bf16[512,512]{1,0:T(8,128)(2,1)} %gather_fusion.4, ...), kind=kOutput, calls=%fused_computation.33 | convolution fusion | flops 276037120 | bytes 6297600 | tf_op jit(solution)/shard_map/dot_general | solution.py:112
  50.3 4.1 %fusion.2 = bf16[512,512]{1,0:T(8,128)(2,1)} fusion(f32[512,512]{1,0:T(8,128)} %get-tuple-element.137, bf16[1024,512]{1,0:T(8,128)(2,1)S(1)} %copy-done, bf16[512,1024]{1,0:T(8,128)(2,1)} %param.19, f32[512]{0:T(512)S(1)} %add_rsqrt_fusion), kind=kOutput, calls=%fused_computation.25 | convolution fusion | flops 1077411840 | bytes 3672064 | tf_op jit(solution)/shard_map/dot_general | solution.py:122
  54.4 5.1 %all-to-all-start = ((bf16[1,8,64,512]{3,2,0,1:T(8,128)(2,1)}), bf16[1,8,64,512]{3,2,0,1:T(8,128)(2,1)}, u32[]{:S(2)}, u32[]{:S(2)}) async-start(bf16[1,8,64,512]{3,2,0,1:T(8,128)(2,1)} %bitcast.14), calls=%async_computation | async-start | bytes 1048576 | tf_op jit(solution)/shard_map/all_to_all | solution.py:139
  60.7 13.3 %all-to-all-done = bf16[1,8,64,512]{3,2,0,1:T(8,128)(2,1)} async-done(((bf16[1,8,64,512]{3,2,0,1:T(8,128)(2,1)}), bf16[1,8,64,512]{3,2,0,1:T(8,128)(2,1)}, u32[]{:S(2)}, u32[]{:S(2)}) %all-to-all-start) | async-done | bytes 524320 | tf_op jit(solution)/shard_map/all_to_all | solution.py:139
  76.2 17.9 %while.16 = (s32[]{:T(128)}, f32[8,64,512]{2,1,0:T(8,128)S(1)}, f32[64]{0:T(128)S(1)}, f32[8,64,512]{2,1,0:T(8,128)}, f32[8,64,512]{2,1,0:T(8,128)S(1)}, /*index=5*/s32[]{:T(128)}, s32[]{:T(128)}) while((s32[]{:T(128)}, f32[8,64,512]{2,1,0:T(8,128)S(1)}, f32[64]{0:T(128)S(1)}, f32[8,64,512]{2,1,0:T(8,128)}, ...), condition=%wide.region_3.5_spmd.clone, body=%wide.region_1.0_spmd.clone.sunk | while | flops 4980803 | bytes 3933276 | solution.py:160
  94.2 17.8 %all_to_all.42 = bf16[8,1,64,512]{3,2,1,0:T(8,128)(2,1)S(1)} all-to-all(bf16[8,1,64,512]{3,2,1,0:T(8,128)(2,1)S(1)} %fusion.6), channel_id=1, replica_groups=mesh['member_0'=4,'member_1'=2,'tile_0'=2,'tile_1'=4,'tile_2'=8] {'membe..., dimensions={0} | all-to-all | bytes 1048576 | tf_op jit(solution)/shard_map/all_to_all | solution.py:162
  116.6 47.5 %reduce-scatter.4.cloned.1.call-done = f32[64,1152]{1,0:T(8,128)} async-done(((f32[512,1152]{1,0:T(8,128)}), f32[64,1152]{1,0:T(8,128)}) %reduce-scatter.4.cloned.1.call-update) | async-done | bytes 294928
  165.6 14.3 %all-to-all-start.4 = ((f32[64,1,128]{2,1,0:T(1,128)}), f32[64,1,128]{2,1,0:T(1,128)S(1)}, u32[]{:S(2)}, u32[]{:S(2)}) async-start(f32[64,1,128]{2,1,0:T(1,128)} %reshape.162), calls=%async_computation.4 | async-start | bytes 65536 | tf_op jit(solution)/shard_map/all_to_all | solution.py:57
  181.9 11.3 %all-to-all-done.4 = f32[64,1,128]{2,1,0:T(1,128)S(1)} async-done(((f32[64,1,128]{2,1,0:T(1,128)}), f32[64,1,128]{2,1,0:T(1,128)S(1)}, u32[]{:S(2)}, u32[]{:S(2)}) %all-to-all-start.4) | async-done | bytes 32800 | tf_op jit(solution)/shard_map/all_to_all | solution.py:57
  193.2 4.6 %all-to-all-start.3 = ((f32[64,1,512]{2,1,0:T(1,128)}), f32[64,1,512]{2,1,0:T(1,128)S(1)}, u32[]{:S(2)}, u32[]{:S(2)}) async-start(f32[64,1,512]{2,1,0:T(1,128)} %reshape.164), calls=%async_computation.3 | async-start | bytes 262144 | tf_op jit(solution)/shard_map/all_to_all | solution.py:57
  200.0 11.7 %all-to-all-done.3 = f32[64,1,512]{2,1,0:T(1,128)S(1)} async-done(((f32[64,1,512]{2,1,0:T(1,128)}), f32[64,1,512]{2,1,0:T(1,128)S(1)}, u32[]{:S(2)}, u32[]{:S(2)}) %all-to-all-start.3) | async-done | bytes 131104 | tf_op jit(solution)/shard_map/all_to_all | solution.py:57
  211.7 4.6 %all-to-all-start.5 = ((f32[64,1,512]{2,1,0:T(1,128)}), f32[64,1,512]{2,1,0:T(1,128)S(1)}, u32[]{:S(2)}, u32[]{:S(2)}) async-start(f32[64,1,512]{2,1,0:T(1,128)} %reshape.160), calls=%async_computation.5 | async-start | bytes 262144 | tf_op jit(solution)/shard_map/all_to_all | solution.py:57
  217.0 11.6 %psum.35 = f32[8]{0:T(128)S(1)} all-reduce(f32[8]{0:T(128)S(1)} %compare_select_fusion.8), channel_id=1, replica_groups=mesh['member_0'=4,'member_1'=2,'tile_0'=2,'tile_1'=4,'tile_2'=8] {'membe..., use_global_device_ids=true, to_apply=%region_5.7 | all-reduce | flops 8 | bytes 64 | tf_op jit(solution)/shard_map/psum | solution.py:36
  228.6 3.5 %psum.36 = f32[8]{0:T(128)S(1)} all-reduce(f32[8]{0:T(128)S(1)} %psum.35), channel_id=1, replica_groups=mesh['member_0'=4,'member_1'=2,'tile_0'=2,'tile_1'=4,'tile_2'=8] {'membe..., use_global_device_ids=true, to_apply=%region_6.8 | all-reduce | flops 8 | bytes 64 | tf_op jit(solution)/shard_map/psum | solution.py:36
  232.2 7.7 %psum.37 = f32[8]{0:T(128)S(1)} all-reduce(f32[8]{0:T(128)S(1)} %psum.36), channel_id=1, replica_groups=mesh['member_0'=4,'member_1'=2,'tile_0'=2,'tile_1'=4,'tile_2'=8] {'tile_0'}, use_global_device_ids=true, to_apply=%region_7.9 | all-reduce | flops 8 | bytes 64 | tf_op jit(solution)/shard_map/psum | solution.py:36
  239.8 8.5 %psum.38 = f32[8]{0:T(128)S(1)} all-reduce(f32[8]{0:T(128)S(1)} %psum.37), channel_id=1, replica_groups=mesh['member_0'=4,'member_1'=2,'tile_0'=2,'tile_1'=4,'tile_2'=8] {'tile_1'}, use_global_device_ids=true, to_apply=%region_8.10 | all-reduce | flops 8 | bytes 64 | tf_op jit(solution)/shard_map/psum | solution.py:36
  248.3 13.0 %psum.39 = f32[8]{0:T(128)S(1)} all-reduce(f32[8]{0:T(128)S(1)} %psum.38), channel_id=1, replica_groups=mesh['member_0'=4,'member_1'=2,'tile_0'=2,'tile_1'=4,'tile_2'=8] {'tile_2'}, use_global_device_ids=true, to_apply=%region_9.11 | all-reduce | flops 8 | bytes 64 | tf_op jit(solution)/shard_map/psum | solution.py:36
  265.6 21.0 %all-gather = f32[8,64,18]{1,2,0:T(8,128)S(1)} all-gather(f32[1,64,18]{1,2,0:T(8,128)S(1)} %maximum_bitcast_fusion), channel_id=1, replica_groups=mesh['member_0'=4,'member_1'=2,'tile_0'=2,'tile_1'=4,'tile_2'=8] {'membe..., dimensions={0}, use_global_device_ids=true | all-gather | bytes 41472 | tf_op jit(solution)/shard_map/all_gather | solution.py:65
  (121 shorter events, 52.6 us)
Async XLA Ops:
  7.2 43.2 %copy-start = (bf16[1024,512]{1,0:T(8,128)(2,1)S(1)}, bf16[1024,512]{1,0:T(8,128)(2,1)}, u32[]{:S(2)}) copy-start(bf16[1024,512]{1,0:T(8,128)(2,1)} %param.20) | copy-start | bytes 3145732
  7.2 8.1 %copy-start.6 = (bf16[1,512,128]{2,1,0:T(8,128)(2,1)S(1)}, bf16[1,512,128]{2,1,0:T(8,128)(2,1)}, u32[]{:S(2)}) copy-start(bf16[1,512,128]{2,1,0:T(8,128)(2,1)} %param.15) | copy-start | bytes 393220
  7.2 8.1 %copy-start.7 = (bf16[128,512]{1,0:T(8,128)(2,1)S(1)}, bf16[128,512]{1,0:T(8,128)(2,1)}, u32[]{:S(2)}) copy-start(bf16[128,512]{1,0:T(8,128)(2,1)} %param.22) | copy-start | bytes 393220
  8.2 17.2 %collective-permute-start = (bf16[64,512]{1,0:T(8,128)(2,1)S(1)}, bf16[64,512]{1,0:T(8,128)(2,1)S(1)}, u32[]{:S(2)}, u32[]{:S(2)}) collective-permute-start(bf16[64,512]{1,0:T(8,128)(2,1)S(1)} %get-tuple-element.122), channel_id=1, source_target_pairs={{0,1},{1,2},{2,3},{3,4},{4,5},{5,6},{6,7},{7,8},{8,9},{9,10},{10,1... | collective-permute-start | bytes 196616 | tf_op jit(solution)/shard_map/ppermute | solution.py:25
  12.2 3.4 %copy-start.1 = (bf16[1,512,512]{2,1,0:T(8,128)(2,1)S(1)}, bf16[1,512,512]{2,1,0:T(8,128)(2,1)}, u32[]{:S(2)}) copy-start(bf16[1,512,512]{2,1,0:T(8,128)(2,1)} %param.14) | copy-start | bytes 1572868
  12.2 3.4 %copy-start.9 = (bf16[512,512]{1,0:T(8,128)(2,1)S(1)}, bf16[512,512]{1,0:T(8,128)(2,1)}, u32[]{:S(2)}) copy-start(bf16[512,512]{1,0:T(8,128)(2,1)} %param.23) | copy-start | bytes 1572868
  12.2 13.2 %collective-permute-start.1 = (bf16[64,512]{1,0:T(8,128)(2,1)S(1)}, bf16[64,512]{1,0:T(8,128)(2,1)S(1)}, u32[]{:S(2)}, u32[]{:S(2)}) collective-permute-start(bf16[64,512]{1,0:T(8,128)(2,1)S(1)} %get-tuple-element.123), channel_id=1, source_target_pairs={{1,0},{2,1},{3,2},{4,3},{5,4},{6,5},{7,6},{8,7},{9,8},{10,9},{11,1... | collective-permute-start | bytes 196616 | tf_op jit(solution)/shard_map/ppermute | solution.py:27
  15.6 1.3 copy-start.4
  15.6 9.5 %copy-start.8 = (s32[8,512]{1,0:T(8,128)S(1)}, s32[8,512]{1,0:T(8,128)}, u32[]{:S(2)}) copy-start(s32[8,512]{1,0:T(8,128)} %param.16) | copy-start | bytes 49156
  16.9 37.5 %all-to-all-start.1 = ((bf16[1,8,64,512]{3,2,0,1:T(8,128)(2,1)}), bf16[1,8,64,512]{3,2,0,1:T(8,128)(2,1)S(1)}, u32[]{:S(2)}, u32[]{:S(2)}) async-start(bf16[1,8,64,512]{3,2,0,1:T(8,128)(2,1)} %bitcast.18), calls=%async_computation.1 | async-start | bytes 1048576 | tf_op jit(solution)/shard_map/all_to_all | solution.py:138
  54.4 5.1 %copy-start.3 = (bf16[1,8,64,512]{3,2,0,1:T(8,128)(2,1)}, bf16[1,8,64,512]{3,2,0,1:T(8,128)(2,1)S(1)}, u32[]{:S(2)}) copy-start(bf16[1,8,64,512]{3,2,0,1:T(8,128)(2,1)S(1)} %all-to-all-done.1) | copy-start | bytes 1572868
  54.4 19.6 %all-to-all-start = ((bf16[1,8,64,512]{3,2,0,1:T(8,128)(2,1)}), bf16[1,8,64,512]{3,2,0,1:T(8,128)(2,1)}, u32[]{:S(2)}, u32[]{:S(2)}) async-start(bf16[1,8,64,512]{3,2,0,1:T(8,128)(2,1)} %bitcast.14), calls=%async_computation | async-start | bytes 1048576 | tf_op jit(solution)/shard_map/all_to_all | solution.py:139
  59.5 104.5 %reduce-scatter.4.cloned.1.call-start = ((), (), s32[]{:S(2)}) async-start(), calls=%async_computation.7 | async-start | bytes 2654208
  94.1 18.0 %copy-start.5 = (f32[512,512]{1,0:T(8,128)S(1)}, f32[512,512]{1,0:T(8,128)}, u32[]{:S(2)}) copy-start(f32[512,512]{1,0:T(8,128)} %copy-done.4) | copy-start | bytes 3145732
  94.1 18.0 %copy-start.10 = (bf16[512,512]{1,0:T(8,128)(2,1)S(1)}, bf16[512,512]{1,0:T(8,128)(2,1)}, u32[]{:S(2)}) copy-start(bf16[512,512]{1,0:T(8,128)(2,1)} %param.23) | copy-start | bytes 1572868
  112.1 1.0 copy-start.2
  165.6 27.5 %all-to-all-start.4 = ((f32[64,1,128]{2,1,0:T(1,128)}), f32[64,1,128]{2,1,0:T(1,128)S(1)}, u32[]{:S(2)}, u32[]{:S(2)}) async-start(f32[64,1,128]{2,1,0:T(1,128)} %reshape.162), calls=%async_computation.4 | async-start | bytes 65536 | tf_op jit(solution)/shard_map/all_to_all | solution.py:57
  193.2 18.5 %all-to-all-start.3 = ((f32[64,1,512]{2,1,0:T(1,128)}), f32[64,1,512]{2,1,0:T(1,128)S(1)}, u32[]{:S(2)}, u32[]{:S(2)}) async-start(f32[64,1,512]{2,1,0:T(1,128)} %reshape.164), calls=%async_computation.3 | async-start | bytes 262144 | tf_op jit(solution)/shard_map/all_to_all | solution.py:57
  211.7 52.7 %all-to-all-start.5 = ((f32[64,1,512]{2,1,0:T(1,128)}), f32[64,1,512]{2,1,0:T(1,128)S(1)}, u32[]{:S(2)}, u32[]{:S(2)}) async-start(f32[64,1,512]{2,1,0:T(1,128)} %reshape.160), calls=%async_computation.5 | async-start | bytes 262144 | tf_op jit(solution)/shard_map/all_to_all | solution.py:57
Sparse Core Ops, SparseCore 0:
  116.7 47.2 reduce-scatter.3
where the time goes:
time: 296 us; the launch traced here: 295 us
  waiting for transfers between devices  83.8 us (28%)
  blocking collectives  83.2 us (28%)
  starting transfers between devices  42.3 us (14%)
  local copies, waits for them, and re-layouts  37.8 us (13%)
  other arithmetic  18.9 us (6%)
  between operations  15.2 us (5%)
  matrix products  13.6 us (5%)
    unnamed x2, waiting for transfers between devices  47.5 us
    psum x5, blocking collectives, one_axis_at_a_time(): array = lax.psum(array, axis)  44.4 us
    all_to_all x3, starting transfers between devices, sent_and_summed(): lax.all_to_all(tiles, axis, split_axis=0, concat_axis=0, tiled=True)  23.5 us
    all_to_all x3, waiting for transfers between devices, sent_and_summed(): lax.all_to_all(tiles, axis, split_axis=0, concat_axis=0, tiled=True)  23 us
    all_gather x1, blocking collectives, gather_turned(): result = lax.all_gather(both, axis, axis=0, tiled=True)  21 us
    gather x8, local copies, waits for them, and re-layouts, on_device(): jnp.take(extended, neighbours[column], axis=0).astype(jnp.float32)  20.4 us
    all_to_all x1, blocking collectives, on_device(): lax.all_to_all(gsend, MEMBER, split_axis=0, concat_axis=1, tiled=True)  17.8 us
    all_to_all x1, waiting for transfers between devices, on_device(): lax.all_to_all(packed[1], MEMBER, split_axis=1, concat_axis=0, tiled=True)  13.3 us
  transfers between devices with their start and end apart: 8, of which 4 were waited for; matrix products, arithmetic and copies ran while one was open for 14% of the time, Pallas kernels for 0%

commit v1 on v0

v1 whole, which is shorter than its diff:
```python
import math

import jax
import jax.numpy as jnp
from jax import lax
from jax.experimental import pallas as pl
from jax.experimental.pallas import tpu as pltpu
from jax.sharding import Mesh
from jax.sharding import PartitionSpec as P

D = 512
FF = 1024
H = 512
NOISE = 128
NBRS = 8
HALO = 64
REGIONS = 8
MEMBERS = 8
CELLS = 512
BLOCK = CELLS // MEMBERS
CELLS_ALL = 32768
TILES = 64
HALF = D // 2
SHARE = 40
LOSS_ROW = 36

MEMBER = ("member_0", "core")
TILE = ("tile_0", "tile_1", "tile_2")
BF16 = jnp.bfloat16
F32 = jnp.float32


def teacher_kernel(top, state, bottom, near, msg, up, down, out, ext):
    ext[0:HALO] = top[...]
    ext[HALO : HALO + CELLS] = state[...]
    ext[HALO + CELLS :] = bottom[...]
    rows = 256
    sub = 128
    for at in range(0, CELLS, rows):
        parts = []
        for start in range(at, at + rows, sub):
            picks = near[:, start : start + sub].T
            lanes = lax.broadcasted_iota(jnp.int32, (sub, 2 * sub), 1) + start
            count = jnp.zeros((sub, 2 * sub), F32)
            for k in range(NBRS):
                count = count + jnp.where(picks[:, k : k + 1] == lanes, 1.0 / NBRS, 0.0)
            parts.append(
                jnp.dot(
                    count.astype(BF16),
                    ext[start : start + 2 * sub],
                    preferred_element_type=F32,
                ).astype(BF16)
            )
        gathered = jnp.concatenate(parts, axis=0)
        resid = state[at : at + rows].astype(F32) + jnp.dot(
            gathered, msg[...], preferred_element_type=F32
        )
        power = jnp.mean(resid * resid, axis=1, keepdims=True)
        normed = (resid * lax.rsqrt(power + 1e-06)).astype(BF16)
        hidden = jax.nn.silu(jnp.dot(normed, up[...], preferred_element_type=F32)).astype(BF16)
        out[at : at + rows] = (
            resid + jnp.dot(hidden, down[...], preferred_element_type=F32)
        ).astype(BF16)


def student_kernel(both, w_in, w_noise, w_out, student, shidden, slope):
    rows = 256
    for at in range(0, CELLS, rows):
        state = both[at : at + rows, :D]
        draws = both[at : at + rows, D:]
        preact = jnp.dot(state, w_in[...], preferred_element_type=F32) + jnp.dot(
            draws, w_noise[...], preferred_element_type=F32
        )
        sig = jax.nn.sigmoid(preact)
        hid = (preact * sig).astype(BF16)
        shidden[at : at + rows] = hid
        slope[at : at + rows] = sig * (1.0 + preact * (1.0 - sig))
        student[at : at + rows] = (
            state.astype(F32) + jnp.dot(hid, w_out[...], preferred_element_type=F32)
        ).astype(BF16)


def score_kernel(student, teacher, both, shidden, slope, w_out, place, grads, gst, wide):
    step = 16
    wide[...] = jnp.zeros_like(wide)

    def block(cell, lane):
        s = [student[m, pl.ds(cell, step), lane : lane + 128].astype(F32) for m in range(MEMBERS)]
        g = [jnp.zeros((step, 128), F32) for _ in range(MEMBERS)]
        loss = jnp.zeros((step, 128), F32)
        for n in range(MEMBERS):
            t = teacher[n, pl.ds(cell, step), lane : lane + 128].astype(F32)
            for m in range(MEMBERS):
                d = s[m] - t
                q = d * d + 0.01
                inv = lax.rsqrt(q)
                loss = loss + q * inv
                g[m] = g[m] + d * inv
        ratio = (MEMBERS - 1) / MEMBERS
        loss = loss * ratio
        g = [x * ratio for x in g]
        for m in range(MEMBERS):
            for n in range(m + 1, MEMBERS):
                d = s[m] - s[n]
                q = d * d + 0.01
                inv = lax.rsqrt(q)
                r = d * inv
                loss = loss - q * inv
                g[m] = g[m] - r
                g[n] = g[n] + r
        scale = 1.0 / (MEMBERS * (MEMBERS - 1) * math.sqrt(CELLS_ALL))
        for m in range(MEMBERS):
            gst[m, pl.ds(cell, step), lane : lane + 128] = (g[m] * scale).astype(BF16)
        pairs = MEMBERS * (MEMBERS - 1)
        wide[...] += (loss - 0.1 * (pairs - pairs // 2)) * (1.0 / pairs)

    def body(i, carry):
        cell = pl.multiple_of(i * step, step)
        for lane in range(0, D, 128):
            block(cell, lane)
        return carry

    lax.fori_loop(0, BLOCK // step, body, 0)

    total = jnp.sum(jnp.sum(wide[...], axis=0, keepdims=True), axis=1, keepdims=True)
    high = total.astype(BF16).astype(F32)
    middle = (total - high).astype(BF16).astype(F32)
    low = (total - high - middle).astype(BF16).astype(F32)
    lane_ids = lax.broadcasted_iota(jnp.int32, (4, 128), 1)
    at = jnp.where(lax.broadcasted_iota(jnp.int32, (4, 128), 0) == place[1], place[0], -128)
    spread = jnp.where(lane_ids == at, high, 0.0)
    spread = spread + jnp.where(lane_ids == at + REGIONS, middle, 0.0)
    spread = spread + jnp.where(lane_ids == at + 2 * REGIONS, low, 0.0)

    back = gst[...].reshape(CELLS, D)
    tn = (((0,), (0,)), ((), ()))
    d_out = lax.dot_general(shidden[...], back, tn, preferred_element_type=F32)
    pull = lax.dot_general(
        back, w_out[...], (((1,), (1,)), ((), ())), preferred_element_type=F32
    )
    gpre = (pull * slope[...]).astype(BF16)
    d_both = lax.dot_general(both[...], gpre, tn, preferred_element_type=F32)
    for half in range(2):
        for part in range(2):
            left = half * HALF + part * 128
            grads[half, :, 8 * part : 8 * part + 8] = d_both[:D, left : left + 128].reshape(
                TILES, 8, 128
            )
            grads[half, :, 16 + 8 * part : 24 + 8 * part] = d_out[:, left : left + 128].reshape(
                TILES, 8, 128
            )
            grads[half, :, 32 + 2 * part : 34 + 2 * part] = d_both[D:, left : left + 128].reshape(
                TILES, 2, 128
            )
        grads[half, :, LOSS_ROW : LOSS_ROW + 4] = jnp.broadcast_to(
            spread[None], (TILES, 4, 128)
        )


def halos(state):
    count = TILES
    ends = count - 1
    up = lax.ppermute(state[CELLS - HALO :], TILE, [(i, i + 1) for i in range(ends)])
    down = lax.ppermute(state[:HALO], TILE, [(i + 1, i) for i in range(ends)])
    return up, down


VMEM = pl.BlockSpec(memory_space=pltpu.VMEM)


def on_device(
    inputs,
    noise,
    neighbours,
    region_map,
    msg_weight,
    up_weight,
    down_weight,
    student_in,
    student_noise,
    student_out,
):
    state = inputs[0]
    both = jnp.concatenate([state, noise[0]], axis=1).reshape(MEMBERS, BLOCK, D + NOISE)
    top, bottom = halos(state)
    mine = lax.all_to_all(both, MEMBER, split_axis=0, concat_axis=0, tiled=True)
    teacher = pl.pallas_call(
        teacher_kernel,
        out_shape=jax.ShapeDtypeStruct((CELLS, D), BF16),
        in_specs=[VMEM] * 7,
        out_specs=VMEM,
        scratch_shapes=[pltpu.VMEM((CELLS + 2 * HALO, D), BF16)],
        name="teacher",
    )(top, state, bottom, neighbours, msg_weight, up_weight, down_weight)
    every = lax.all_to_all(
        teacher.reshape(MEMBERS, BLOCK, D), MEMBER, split_axis=0, concat_axis=0, tiled=True
    )
    mine = mine.reshape(CELLS, D + NOISE)
    student, shidden, slope = pl.pallas_call(
        student_kernel,
        out_shape=(
            jax.ShapeDtypeStruct((CELLS, D), BF16),
            jax.ShapeDtypeStruct((CELLS, H), BF16),
            jax.ShapeDtypeStruct((CELLS, H), F32),
        ),
        in_specs=[VMEM] * 4,
        out_specs=[VMEM] * 3,
        name="student",
    )(mine, student_in, student_noise, student_out)
    place = jnp.stack([region_map[0], lax.axis_index("core").astype(jnp.int32)])
    grads = pl.pallas_call(
        score_kernel,
        out_shape=jax.ShapeDtypeStruct((2, TILES, SHARE, 128), F32),
        in_specs=[VMEM] * 6 + [pl.BlockSpec(memory_space=pltpu.SMEM)],
        out_specs=VMEM,
        scratch_shapes=[
            pltpu.VMEM((MEMBERS, BLOCK, D), BF16),
            pltpu.VMEM((16, 128), F32),
        ],
        name="score",
    )(student.reshape(MEMBERS, BLOCK, D), every, mine, shidden, slope, student_out, place)
    own = lax.all_to_all(grads, "core", split_axis=0, concat_axis=0, tiled=True)
    half = jnp.sum(own, axis=0).astype(BF16)
    shares = lax.all_to_all(half, TILE, split_axis=0, concat_axis=0, tiled=True)
    share = jnp.sum(shares.astype(F32), axis=0)
    copies = jnp.broadcast_to(share[None], (MEMBERS, SHARE, 128))
    parts = lax.all_to_all(copies, MEMBER, split_axis=0, concat_axis=0, tiled=True)
    sums = jnp.sum(parts.reshape(MEMBERS // 2, 2, SHARE, 128), axis=0)

    def rows(first, count):
        piece = sums[:, first : first + 2 * count].reshape(2, 2, count, 128)
        return jnp.transpose(piece, (2, 0, 1, 3)).reshape(count, D)

    losses = sums[0, LOSS_ROW : LOSS_ROW + 2, : 3 * REGIONS].reshape(6, REGIONS)
    region_loss = jnp.sum(losses, axis=0) / (CELLS_ALL // REGIONS * D)
    return (teacher[None], region_loss, rows(0, 8), rows(32, 2), rows(16, 8))


def solution(mesh):
    split = Mesh(
        mesh.devices.reshape(4, 2, 2, 4, 8), ("member_0", "core", "tile_0", "tile_1", "tile_2")
    )
    in_specs = (
        P(MEMBER, TILE, None),
        P(MEMBER, TILE, None),
        P(None, TILE),
        P(TILE),
        P(),
        P(),
        P(),
        P(),
        P(),
        P(),
    )
    out_specs = (P(MEMBER, TILE, None), P(), P(TILE, None), P(TILE, None), P(TILE, None))
    return jax.shard_map(
        on_device, mesh=split, in_specs=in_specs, out_specs=out_specs, check_vma=False
    )
```

time: 296 us -> 121 us (0.41)
  waiting for transfers between devices: 83.8 us -> 14.3 us
  local copies, waits for them, and re-layouts: 37.8 us -> 3.63 us
  blocking collectives: 83.2 us -> 59.8 us
  starting transfers between devices: 42.3 us -> 19.9 us
  Pallas kernels: 0 us -> 17.6 us
  other arithmetic: 18.9 us -> 3.48 us
  between operations: 15.2 us -> 1.33 us
  matrix products: 13.6 us -> 0 us
    unnamed x2 -> x0, waiting for transfers between devices: 47.5 us -> none
    psum x5 -> x0, blocking collectives: 44.4 us -> none  [one_axis_at_a_time(): array = lax.psum(array, axis)]
    all_to_all x1 -> x3, blocking collectives: 17.8 us -> 59.8 us  [the longest x1 40.5 us: on_device(): shares = lax.all_to_all(half, TILE, split_axis=0, concat_axis=0, tiled=True)]
    all_to_all x5 -> x2, waiting for transfers between devices: 36.3 us -> 13 us  [the longest x1 9.39 us: on_device(): lax.all_to_all(teacher.reshape(MEMBERS, BLOCK, D), MEMBER, split_axis=0,...]
    all_to_all x5 -> x2, starting transfers between devices: 36.9 us -> 14.6 us  [the longest x1 10.3 us: on_device(): mine = lax.all_to_all(both, MEMBER, split_axis=0, concat_axis=0, tiled=True)]
    all_gather x1 -> x0, blocking collectives: 21 us -> none  [gather_turned(): result = lax.all_gather(both, axis, axis=0, tiled=True)]
    gather x8 -> x0, local copies, waits for them, and re-layouts: 20.4 us -> none  [on_device(): jnp.take(extended, neighbours[column], axis=0).astype(jnp.float32)]
    pallas_call x0 -> x3, Pallas kernels: none -> 17.6 us  [the longest x1 8.34 us: on_device(): pl.pallas_call(score_kernel, out_shape=jax.ShapeDtypeStruct((2, TILES, SH...]
  transfers between devices with their start and end apart: 8 -> 4, of which waited for: 4 -> 4; matrix products, arithmetic and copies ran while one was open for 14% -> 1% of each run, Pallas kernels for 0% -> 8%
where the time goes in v1:
time: 121 us; the launch traced here: 120 us
  blocking collectives  59.8 us (49%)
  starting transfers between devices  19.9 us (16%)
  Pallas kernels  17.6 us (15%)
  waiting for transfers between devices  14.3 us (12%)
  local copies, waits for them, and re-layouts  3.63 us (3%)
  other arithmetic  3.48 us (3%)
  between operations  1.33 us (1%)
    all_to_all x1, blocking collectives, on_device(): shares = lax.all_to_all(half, TILE, split_axis=0, concat_axis=0, tiled=True)  40.5 us
    all_to_all x1, blocking collectives, on_device(): lax.all_to_all(copies, MEMBER, split_axis=0, concat_axis=0, tiled=True)  11.7 us
    all_to_all x1, starting transfers between devices, on_device(): mine = lax.all_to_all(both, MEMBER, split_axis=0, concat_axis=0, tiled=True)  10.3 us
    all_to_all x1, waiting for transfers between devices, on_device(): lax.all_to_all(teacher.reshape(MEMBERS, BLOCK, D), MEMBER, split_axis=0,...  9.39 us
    pallas_call x1, Pallas kernels, on_device(): pl.pallas_call(score_kernel, out_shape=jax.ShapeDtypeStruct((2, TILES, SH...  8.34 us
    all_to_all x1, blocking collectives, on_device(): own = lax.all_to_all(grads, 'core', split_axis=0, concat_axis=0, tiled=True)  7.68 us
    pallas_call x1, Pallas kernels, on_device(): pl.pallas_call(teacher_kernel, out_shape=jax.ShapeDtypeStruct((CELLS, D),...  5.46 us
    all_to_all x1, starting transfers between devices, on_device(): lax.all_to_all(teacher.reshape(MEMBERS, BLOCK, D), MEMBER, split_axis=0,...  4.36 us
  transfers between devices with their start and end apart: 4, of which 4 were waited for; matrix products, arithmetic and copies ran while one was open for 1% of the time, Pallas kernels for 8%

profile of v1, /device:TPU:1, one launch (start us, length us, event | category | flops | bytes accessed | tf_op | source)
XLA Modules:
  0.0 120.1 jit_solution(15294700321537259691)
XLA Ops:
  0.6 2.0 %pad_maximum_fusion = bf16[8,64,640]{2,1,0:T(8,128)(2,1)} fusion(bf16[8,64,128]{2,1,0:T(8,128)(2,1)} %bitcast.36, bf16[8,64,512]{2,1,0:T(8,128)(2,1)} %bitcast.30), kind=kLoop, calls=%fused_computation.1 | loop fusion | flops 1310720 | bytes 1310720 | tf_op jit(solution)/shard_map/concatenate | solution.py:184
  2.7 10.3 %all-to-all-start = ((bf16[8,64,640]{2,1,0:T(8,128)(2,1)}), bf16[8,64,640]{2,1,0:T(8,128)(2,1)S(1)}, u32[]{:S(2)}, u32[]{:S(2)}) async-start(bf16[8,64,640]{2,1,0:T(8,128)(2,1)} %pad_maximum_fusion), calls=%async_computation | async-start | bytes 1310720 | tf_op jit(solution)/shard_map/all_to_all | solution.py:186
  12.9 0.9 slice_bitcast_fusion
  13.8 1.3 %collective-permute-start.1 = (bf16[64,512]{1,0:T(8,128)(2,1)S(1)}, bf16[64,512]{1,0:T(8,128)(2,1)S(1)}, u32[]{:S(2)}, u32[]{:S(2)}) collective-permute-start(bf16[64,512]{1,0:T(8,128)(2,1)S(1)} %get-tuple-element.11), channel_id=1, source_target_pairs={{1,0},{2,1},{3,2},{4,3},{5,4},{6,5},{7,6},{8,7},{9,8},{10,9},{11,1... | collective-permute-start | bytes 196616 | tf_op jit(solution)/shard_map/ppermute | solution.py:164
  15.1 4.0 %collective-permute-start = (bf16[64,512]{1,0:T(8,128)(2,1)S(1)}, bf16[64,512]{1,0:T(8,128)(2,1)S(1)}, u32[]{:S(2)}, u32[]{:S(2)}) collective-permute-start(bf16[64,512]{1,0:T(8,128)(2,1)S(1)} %get-tuple-element.12), channel_id=1, source_target_pairs={{0,1},{1,2},{2,3},{3,4},{4,5},{5,6},{6,7},{7,8},{8,9},{9,10},{10,1... | collective-permute-start | bytes 196616 | tf_op jit(solution)/shard_map/ppermute | solution.py:163
  19.1 0.1 collective-permute-done.1.bottom
  19.3 1.2 collective-permute-done.top
  20.4 0.6 copy-done.3
  21.1 5.5 %teacher.1 = bf16[512,512]{1,0:T(8,128)(2,1)} custom-call(bf16[64,512]{1,0:T(8,128)(2,1)} %copy-done.3, bf16[512,512]{1,0:T(8,128)(2,1)} %bitcast.31, bf16[64,512]{1,0:T(8,128)(2,1)} %copy-done.2, s32[8,512]{1,0:T(8,128)} %near.1, bf16[512,512]{1,0:T(8,128)(2,1)} %msg.1, bf16[512,1024]{1,0:T(8,128)(2,1)} %up.1, bf16[1024,512]{1,0:T(8,128)(2,1)} %down.1), custom_call_target="tpu_custom_call" | custom-call | tf_op jit(solution)/shard_map/teacher/pallas_call | solution.py:187
  26.5 3.6 %all-to-all-done = bf16[8,64,640]{2,1,0:T(8,128)(2,1)S(1)} async-done(((bf16[8,64,640]{2,1,0:T(8,128)(2,1)}), bf16[8,64,640]{2,1,0:T(8,128)(2,1)S(1)}, u32[]{:S(2)}, u32[]{:S(2)}) %all-to-all-start) | async-done | bytes 655392 | tf_op jit(solution)/shard_map/all_to_all | solution.py:186
  30.1 4.4 %all-to-all-start.1 = ((bf16[8,64,512]{2,1,0:T(8,128)(2,1)}), bf16[8,64,512]{2,1,0:T(8,128)(2,1)S(1)}, u32[]{:S(2)}, u32[]{:S(2)}) async-start(bf16[8,64,512]{2,1,0:T(8,128)(2,1)} %bitcast.32), calls=%async_computation.1 | async-start | bytes 1048576 | tf_op jit(solution)/shard_map/all_to_all | solution.py:195
  35.2 0.6 pad_add_fusion.place
  35.7 3.8 %student.1 = (bf16[512,512]{1,0:T(8,128)(2,1)}, bf16[512,512]{1,0:T(8,128)(2,1)}, f32[512,512]{1,0:T(8,128)}) custom-call(bf16[512,640]{1,0:T(8,128)(2,1)} %bitcast.28, bf16[512,512]{1,0:T(8,128)(2,1)} %w_in.1, bf16[128,512]{1,0:T(8,128)(2,1)} %w_noise.1, bf16[512,512]{1,0:T(8,128)(2,1)} %w_out.3), custom_call_target="tpu_custom_call" | custom-call | tf_op jit(solution)/shard_map/student/pallas_call | solution.py:199
  39.5 9.4 %all-to-all-done.1.teacher = bf16[8,64,512]{2,1,0:T(8,128)(2,1)S(1)} async-done(((bf16[8,64,512]{2,1,0:T(8,128)(2,1)}), bf16[8,64,512]{2,1,0:T(8,128)(2,1)S(1)}, u32[]{:S(2)}, u32[]{:S(2)}) %all-to-all-start.1) | async-done | bytes 524320 | tf_op jit(solution)/shard_map/all_to_all | solution.py:195
  48.9 0.8 copy-done.1
  49.7 8.3 %score.1 = f32[2,64,40,128]{3,2,1,0:T(8,128)} custom-call(bf16[8,64,512]{2,1,0:T(8,128)(2,1)} %bitcast.35, bf16[8,64,512]{2,1,0:T(8,128)(2,1)} %copy-done.1, bf16[512,640]{1,0:T(8,128)(2,1)} %bitcast.29, bf16[512,512]{1,0:T(8,128)(2,1)} %get-tuple-element.9.shidden, f32[512,512]{1,0:T(8,128)} %get-tuple-element.10.slope, bf16[512,512]{1,0:T(8,128)(2,1)} %w_out.3, ...), custom_call_target="tpu_custom_call" | custom-call | tf_op jit(solution)/shard_map/score/pallas_call | solution.py:211
  58.1 7.7 %all_to_all.25 = f32[2,64,40,128]{3,2,1,0:T(8,128)S(1)} all-to-all(f32[2,64,40,128]{3,2,1,0:T(8,128)} %score.1), channel_id=1, replica_groups=mesh['member_0'=4,'core'=2,'tile_0'=2,'tile_1'=4,'tile_2'=8] {'core'}, dimensions={0} | all-to-all | bytes 5242880 | tf_op jit(solution)/shard_map/all_to_all | solution.py:222
  65.7 0.2 reduce_sum.36
  65.9 40.5 %all_to_all.26 = bf16[64,40,128]{2,1,0:T(8,128)(2,1)S(1)} all-to-all(bf16[64,40,128]{2,1,0:T(8,128)(2,1)S(1)} %reduce_sum.36), channel_id=1, replica_groups=mesh['member_0'=4,'core'=2,'tile_0'=2,'tile_1'=4,'tile_2'=8] {'tile_0','..., dimensions={0} | all-to-all | bytes 1310720 | tf_op jit(solution)/shard_map/all_to_all | solution.py:224
  106.4 0.1 convert_reduce_fusion
  106.6 11.7 %all_to_all.27 = f32[8,40,128]{2,1,0:T(8,128)S(1)} all-to-all(f32[8,40,128]{2,1,0:T(8,128)S(1)} %broadcast_in_dim.10), channel_id=1, replica_groups=mesh['member_0'=4,'core'=2,'tile_0'=2,'tile_1'=4,'tile_2'=8] {'member_0'..., dimensions={0} | all-to-all | bytes 327680 | tf_op jit(solution)/shard_map/all_to_all | solution.py:227
  118.2 0.6 slice.34
  118.8 0.6 fusion
  119.6 0.5 broadcast_multiply_fusion
  (11 shorter events, 0.1 us)
Async XLA Ops:
  2.7 27.5 %all-to-all-start = ((bf16[8,64,640]{2,1,0:T(8,128)(2,1)}), bf16[8,64,640]{2,1,0:T(8,128)(2,1)S(1)}, u32[]{:S(2)}, u32[]{:S(2)}) async-start(bf16[8,64,640]{2,1,0:T(8,128)(2,1)} %pad_maximum_fusion), calls=%async_computation | async-start | bytes 1310720 | tf_op jit(solution)/shard_map/all_to_all | solution.py:186
  13.8 5.4 %collective-permute-start.1 = (bf16[64,512]{1,0:T(8,128)(2,1)S(1)}, bf16[64,512]{1,0:T(8,128)(2,1)S(1)}, u32[]{:S(2)}, u32[]{:S(2)}) collective-permute-start(bf16[64,512]{1,0:T(8,128)(2,1)S(1)} %get-tuple-element.11), channel_id=1, source_target_pairs={{1,0},{2,1},{3,2},{4,3},{5,4},{6,5},{7,6},{8,7},{9,8},{10,9},{11,1... | collective-permute-start | bytes 196616 | tf_op jit(solution)/shard_map/ppermute | solution.py:164
  15.1 5.3 %collective-permute-start = (bf16[64,512]{1,0:T(8,128)(2,1)S(1)}, bf16[64,512]{1,0:T(8,128)(2,1)S(1)}, u32[]{:S(2)}, u32[]{:S(2)}) collective-permute-start(bf16[64,512]{1,0:T(8,128)(2,1)S(1)} %get-tuple-element.12), channel_id=1, source_target_pairs={{0,1},{1,2},{2,3},{3,4},{4,5},{5,6},{6,7},{7,8},{8,9},{9,10},{10,1... | collective-permute-start | bytes 196616 | tf_op jit(solution)/shard_map/ppermute | solution.py:163
  19.3 1.2 copy-start.2
  20.4 0.6 copy-start.3
  30.1 5.6 %copy-start = (bf16[8,64,640]{2,1,0:T(8,128)(2,1)}, bf16[8,64,640]{2,1,0:T(8,128)(2,1)S(1)}, u32[]{:S(2)}) copy-start(bf16[8,64,640]{2,1,0:T(8,128)(2,1)S(1)} %all-to-all-done) | copy-start | bytes 1966084
  30.1 18.8 %all-to-all-start.1 = ((bf16[8,64,512]{2,1,0:T(8,128)(2,1)}), bf16[8,64,512]{2,1,0:T(8,128)(2,1)S(1)}, u32[]{:S(2)}, u32[]{:S(2)}) async-start(bf16[8,64,512]{2,1,0:T(8,128)(2,1)} %bitcast.32), calls=%async_computation.1 | async-start | bytes 1048576 | tf_op jit(solution)/shard_map/all_to_all | solution.py:195
  48.9 0.8 copy-start.1

commit v2 on v1

--- a/solution.py
+++ b/solution.py
@@ -21,6 +21,7 @@
 CELLS_ALL = 32768
 TILES = 64
 HALF = D // 2
+XY = TILES // 2
 SHARE = 40
 LOSS_ROW = 36
 
@@ -63,24 +64,61 @@
         ).astype(BF16)
 
 
-def student_kernel(both, w_in, w_noise, w_out, student, shidden, slope):
+def join_kernel(state, noise, both, sem):
+    copies = [
+        pltpu.make_async_copy(state, both.at[:, :D], sem.at[0]),
+        pltpu.make_async_copy(noise, both.at[:, D:], sem.at[1]),
+    ]
+    for copy in copies:
+        copy.start()
+    for copy in copies:
+        copy.wait()
+
+
+def student_kernel(mine, w_in, w_noise, w_out, student, shidden, slope, turned):
     rows = 256
     for at in range(0, CELLS, rows):
-        state = both[at : at + rows, :D]
-        draws = both[at : at + rows, D:]
+        state = mine[at : at + rows, :D]
         preact = jnp.dot(state, w_in[...], preferred_element_type=F32) + jnp.dot(
-            draws, w_noise[...], preferred_element_type=F32
+            mine[at : at + rows, D:], w_noise[...], preferred_element_type=F32
         )
         sig = jax.nn.sigmoid(preact)
         hid = (preact * sig).astype(BF16)
-        shidden[at : at + rows] = hid
         slope[at : at + rows] = sig * (1.0 + preact * (1.0 - sig))
         student[at : at + rows] = (
             state.astype(F32) + jnp.dot(hid, w_out[...], preferred_element_type=F32)
         ).astype(BF16)
-
-
-def score_kernel(student, teacher, both, shidden, slope, w_out, place, grads, gst, wide):
+        shidden[:, at : at + rows] = hid.T
+        turned[:, at : at + rows] = mine[at : at + rows].T
+
+
+def score_kernel(
+    student,
+    teacher,
+    turned_at,
+    shidden_at,
+    slope_at,
+    w_out_at,
+    place,
+    send,
+    keep,
+    gst,
+    gpre,
+    wide,
+    turned,
+    shidden,
+    slope,
+    w_out,
+    sem,
+):
+    copies = [
+        pltpu.make_async_copy(source, target, sem.at[k])
+        for k, (source, target) in enumerate(
+            ((turned_at, turned), (shidden_at, shidden), (slope_at, slope), (w_out_at, w_out))
+        )
+    ]
+    for copy in copies:
+        copy.start()
     step = 16
     wide[...] = jnp.zeros_like(wide)
 
@@ -123,38 +161,86 @@
     lax.fori_loop(0, BLOCK // step, body, 0)
 
     total = jnp.sum(jnp.sum(wide[...], axis=0, keepdims=True), axis=1, keepdims=True)
-    high = total.astype(BF16).astype(F32)
-    middle = (total - high).astype(BF16).astype(F32)
-    low = (total - high - middle).astype(BF16).astype(F32)
     lane_ids = lax.broadcasted_iota(jnp.int32, (4, 128), 1)
     at = jnp.where(lax.broadcasted_iota(jnp.int32, (4, 128), 0) == place[1], place[0], -128)
-    spread = jnp.where(lane_ids == at, high, 0.0)
-    spread = spread + jnp.where(lane_ids == at + REGIONS, middle, 0.0)
-    spread = spread + jnp.where(lane_ids == at + 2 * REGIONS, low, 0.0)
-
+    spread = jnp.zeros((4, 128), F32)
+    for k, piece in enumerate(three(total)):
+        spread = spread + jnp.where(lane_ids == at + k * REGIONS, piece, 0.0)
+    spread = jnp.broadcast_to(spread[None], (XY, 4, 128))
+
+    for copy in copies:
+        copy.wait()
     back = gst[...].reshape(CELLS, D)
-    tn = (((0,), (0,)), ((), ()))
-    d_out = lax.dot_general(shidden[...], back, tn, preferred_element_type=F32)
     pull = lax.dot_general(
         back, w_out[...], (((1,), (1,)), ((), ())), preferred_element_type=F32
     )
-    gpre = (pull * slope[...]).astype(BF16)
-    d_both = lax.dot_general(both[...], gpre, tn, preferred_element_type=F32)
+    gpre[...] = (pull * slope[...]).astype(BF16)
+    for k, target in enumerate((send, keep)):
+        left = pl.multiple_of(jnp.where(place[1] == k, HALF, 0), HALF)
+        d_out = jnp.dot(
+            shidden[...], gst[:, :, pl.ds(left, HALF)].reshape(CELLS, HALF), preferred_element_type=F32
+        )
+        pulled = gpre[:, pl.ds(left, HALF)]
+        d_in = jnp.dot(turned[:D], pulled, preferred_element_type=F32)
+        d_noise = jnp.dot(turned[D:], pulled, preferred_element_type=F32)
+        for high in range(2):
+            pieces = []
+            for source, count in ((d_in, 8), (d_out, 8), (d_noise, 2)):
+                start = high * XY * count
+                for lane in (0, 128):
+                    pieces.append(
+                        source[start : start + XY * count, lane : lane + 128].reshape(
+                            XY, count, 128
+                        )
+                    )
+            pieces.append(spread)
+            target[:, high] = jnp.concatenate(pieces, axis=1).astype(BF16)
+
+
+def three(value):
+    high = value.astype(BF16).astype(F32)
+    middle = (value - high).astype(BF16).astype(F32)
+    return high, middle, (value - high - middle).astype(BF16).astype(F32)
+
+
+def fold_kernel(arrived, out):
+    lanes = lax.broadcasted_iota(jnp.int32, (4, 128), 1)
+    first = lax.broadcasted_iota(jnp.int32, (4, 128), 0) == 0
+    for high in range(2):
+        total = jnp.zeros((SHARE, 128), F32)
+        for k in range(XY):
+            total = total + arrived[k, high].astype(F32)
+        tail = total[LOSS_ROW:]
+        row = jnp.sum(tail, axis=0, keepdims=True)
+        loss = row[:, :REGIONS] + row[:, REGIONS : 2 * REGIONS] + row[:, 2 * REGIONS : 3 * REGIONS]
+        again = jnp.concatenate(
+            [*three(loss), jnp.zeros((1, 128 - 3 * REGIONS), F32)], axis=1
+        )
+        share = jnp.concatenate(
+            [total[:LOSS_ROW], jnp.where(first, again, jnp.zeros_like(tail))], axis=0
+        ).astype(BF16)
+        for k in range(MEMBERS):
+            out[high * MEMBERS + k] = share
+
+
+def last_kernel(arrived, region_loss, grad_in, grad_noise, grad_out):
     for half in range(2):
+        total = arrived[half].astype(F32)
+        for k in range(1, MEMBERS):
+            total = total + arrived[2 * k + half].astype(F32)
         for part in range(2):
             left = half * HALF + part * 128
-            grads[half, :, 8 * part : 8 * part + 8] = d_both[:D, left : left + 128].reshape(
-                TILES, 8, 128
+            grad_in[:, left : left + 128] = total[8 * part : 8 * part + 8]
+            grad_out[:, left : left + 128] = total[16 + 8 * part : 24 + 8 * part]
+            grad_noise[:, left : left + 128] = total[32 + 2 * part : 34 + 2 * part]
+        if half == 0:
+            row = total[LOSS_ROW : LOSS_ROW + 1]
+            loss = (
+                row[:, :REGIONS]
+                + row[:, REGIONS : 2 * REGIONS]
+                + row[:, 2 * REGIONS : 3 * REGIONS]
             )
-            grads[half, :, 16 + 8 * part : 24 + 8 * part] = d_out[:, left : left + 128].reshape(
-                TILES, 8, 128
-            )
-            grads[half, :, 32 + 2 * part : 34 + 2 * part] = d_both[D:, left : left + 128].reshape(
-                TILES, 2, 128
-            )
-        grads[half, :, LOSS_ROW : LOSS_ROW + 4] = jnp.broadcast_to(
-            spread[None], (TILES, 4, 128)
-        )
+            region_loss[...] = loss * (1.0 / (CELLS_ALL // REGIONS * D))
 
 
 def halos(state):
@@ -165,7 +251,13 @@
     return up, down
 
 
+HBM = pl.BlockSpec(memory_space=pltpu.HBM)
 VMEM = pl.BlockSpec(memory_space=pltpu.VMEM)
+PARAMS = pltpu.CompilerParams(vmem_limit_bytes=16 * 1024 * 1024)
+
+
+def in_hbm(array):
+    return pltpu.with_memory_space_constraint(array, pltpu.HBM)
 
 
 def on_device(
@@ -181,59 +273,111 @@
     student_out,
 ):
     state = inputs[0]
-    both = jnp.concatenate([state, noise[0]], axis=1).reshape(MEMBERS, BLOCK, D + NOISE)
-    top, bottom = halos(state)
-    mine = lax.all_to_all(both, MEMBER, split_axis=0, concat_axis=0, tiled=True)
-    teacher = pl.pallas_call(
+    with jax.named_scope("rows"):
+        both = pl.pallas_call(
+            join_kernel,
+            out_shape=jax.ShapeDtypeStruct((CELLS, D + NOISE), BF16),
+            in_specs=[HBM] * 2,
+            out_specs=HBM,
+            scratch_shapes=[pltpu.SemaphoreType.DMA((2,))],
+            compiler_params=PARAMS,
+            name="join",
+        )(in_hbm(state), in_hbm(noise[0]))
+        mine = lax.all_to_all(
+            both.reshape(MEMBERS, BLOCK, D + NOISE),
+            MEMBER,
+            split_axis=0,
+            concat_axis=0,
+            tiled=True,
+        )
+    with jax.named_scope("halo"):
+        top, bottom = halos(state)
+    teach = pl.pallas_call(
         teacher_kernel,
         out_shape=jax.ShapeDtypeStruct((CELLS, D), BF16),
         in_specs=[VMEM] * 7,
         out_specs=VMEM,
         scratch_shapes=[pltpu.VMEM((CELLS + 2 * HALO, D), BF16)],
+        compiler_params=PARAMS,
         name="teacher",
-    )(top, state, bottom, neighbours, msg_weight, up_weight, down_weight)
-    every = lax.all_to_all(
-        teacher.reshape(MEMBERS, BLOCK, D), MEMBER, split_axis=0, concat_axis=0, tiled=True
-    )
+    )
+    with jax.named_scope("teach"):
+        teacher = teach(top, state, bottom, neighbours, msg_weight, up_weight, down_weight)
+    with jax.named_scope("every"):
+        every = lax.all_to_all(
+            teacher.reshape(MEMBERS, BLOCK, D), MEMBER, split_axis=0, concat_axis=0, tiled=True
+        )
     mine = mine.reshape(CELLS, D + NOISE)
-    student, shidden, slope = pl.pallas_call(
+    pupil = pl.pallas_call(
         student_kernel,
         out_shape=(
             jax.ShapeDtypeStruct((CELLS, D), BF16),
-            jax.ShapeDtypeStruct((CELLS, H), BF16),
+            jax.ShapeDtypeStruct((H, CELLS), BF16),
             jax.ShapeDtypeStruct((CELLS, H), F32),
+            jax.ShapeDtypeStruct((D + NOISE, CELLS), BF16),
         ),
         in_specs=[VMEM] * 4,
-        out_specs=[VMEM] * 3,
+        out_specs=[VMEM] * 4,
+        compiler_params=PARAMS,
         name="student",
-    )(mine, student_in, student_noise, student_out)
+    )
+    with jax.named_scope("pupil"):
+        student, shidden, slope, turned = pupil(mine, student_in, student_noise, student_out)
     place = jnp.stack([region_map[0], lax.axis_index("core").astype(jnp.int32)])
-    grads = pl.pallas_call(
+    send, keep = pl.pallas_call(
         score_kernel,
-        out_shape=jax.ShapeDtypeStruct((2, TILES, SHARE, 128), F32),
-        in_specs=[VMEM] * 6 + [pl.BlockSpec(memory_space=pltpu.SMEM)],
-        out_specs=VMEM,
+        out_shape=[jax.ShapeDtypeStruct((XY, 2, SHARE, 128), BF16)] * 2,
+        in_specs=[VMEM] * 2 + [HBM] * 4 + [pl.BlockSpec(memory_space=pltpu.SMEM)],
+        out_specs=[VMEM] * 2,
         scratch_shapes=[
             pltpu.VMEM((MEMBERS, BLOCK, D), BF16),
+            pltpu.VMEM((CELLS, D), BF16),
             pltpu.VMEM((16, 128), F32),
+            pltpu.VMEM((D + NOISE, CELLS), BF16),
+            pltpu.VMEM((H, CELLS), BF16),
+            pltpu.VMEM((CELLS, H), F32),
+            pltpu.VMEM((H, D), BF16),
+            pltpu.SemaphoreType.DMA((4,)),
         ],
+        compiler_params=PARAMS,
         name="score",
-    )(student.reshape(MEMBERS, BLOCK, D), every, mine, shidden, slope, student_out, place)
-    own = lax.all_to_all(grads, "core", split_axis=0, concat_axis=0, tiled=True)
-    half = jnp.sum(own, axis=0).astype(BF16)
-    shares = lax.all_to_all(half, TILE, split_axis=0, concat_axis=0, tiled=True)
-    share = jnp.sum(shares.astype(F32), axis=0)
-    copies = jnp.broadcast_to(share[None], (MEMBERS, SHARE, 128))
-    parts = lax.all_to_all(copies, MEMBER, split_axis=0, concat_axis=0, tiled=True)
-    sums = jnp.sum(parts.reshape(MEMBERS // 2, 2, SHARE, 128), axis=0)
-
-    def rows(first, count):
-        piece = sums[:, first : first + 2 * count].reshape(2, 2, count, 128)
-        return jnp.transpose(piece, (2, 0, 1, 3)).reshape(count, D)
-
-    losses = sums[0, LOSS_ROW : LOSS_ROW + 2, : 3 * REGIONS].reshape(6, REGIONS)
-    region_loss = jnp.sum(losses, axis=0) / (CELLS_ALL // REGIONS * D)
-    return (teacher[None], region_loss, rows(0, 8), rows(32, 2), rows(16, 8))
+    )(
+        student.reshape(MEMBERS, BLOCK, D),
+        every,
+        in_hbm(turned),
+        in_hbm(shidden),
+        in_hbm(slope),
+        in_hbm(student_out),
+        place,
+    )
+    other = lax.ppermute(send, "core", [(0, 1), (1, 0)])
+    half = (keep.astype(F32) + other.astype(F32)).astype(BF16)
+    shares = lax.all_to_all(half, ("tile_1", "tile_2"), split_axis=0, concat_axis=0, tiled=True)
+    copies = pl.pallas_call(
+        fold_kernel,
+        out_shape=jax.ShapeDtypeStruct((2 * MEMBERS, SHARE, 128), BF16),
+        in_specs=[VMEM],
+        out_specs=VMEM,
+        compiler_params=PARAMS,
+        name="fold",
+    )(shares)
+    parts = lax.all_to_all(
+        copies, ("tile_0", "member_0", "core"), split_axis=0, concat_axis=0, tiled=True
+    )
+    region_loss, grad_in, grad_noise, grad_out = pl.pallas_call(
+        last_kernel,
+        out_shape=[
+            jax.ShapeDtypeStruct((1, REGIONS), F32),
+            jax.ShapeDtypeStruct((8, D), F32),
+            jax.ShapeDtypeStruct((2, D), F32),
+            jax.ShapeDtypeStruct((8, D), F32),
+        ],
+        in_specs=[VMEM],
+        out_specs=[VMEM] * 4,
+        compiler_params=PARAMS,
+        name="last",
+    )(parts)
+    return (teacher[None], region_loss.reshape(REGIONS), grad_in, grad_noise, grad_out)
 
 
 def solution(mesh):

time: 121 us -> 128 us (1.058)
  Pallas kernels: 17.6 us -> 32 us
  blocking collectives: 59.8 us -> 48.2 us
  waiting for transfers between devices: 14.3 us -> 18.9 us
  other arithmetic: 3.48 us -> 0.25 us
  starting transfers between devices: 19.9 us -> 22.9 us
    pallas_call x3 -> x6, Pallas kernels: 17.6 us -> 32 us  [the longest x1 21 us: on_device(): pl.pallas_call(join_kernel, out_shape=jax.ShapeDtypeStruct((CELLS, D + NO...]
    all_to_all x3 -> x2, blocking collectives: 59.8 us -> 48.2 us  [the longest x1 26.3 us: on_device(): lax.all_to_all(half, ('tile_1', 'tile_2'), split_axis=0, concat_axis=0, t...]
    ppermute x0 -> x1, starting transfers between devices: none -> 2.87 us  [on_device(): other = lax.ppermute(send, 'core', [(0, 1), (1, 0)])]
    all_to_all x1, waiting for transfers between devices: 3.63 us -> 6 us  [on_device(): lax.all_to_all(both.reshape(MEMBERS, BLOCK, D + NOISE), MEMBER, split_axi...]
    unnamed x8 -> x22, local copies, waits for them, and re-layouts: 1.45 us -> 3.72 us
    concatenate x1 -> x0, other arithmetic: 2.02 us -> none  [on_device(): jnp.concatenate([state, noise[0]], axis=1)]
    ppermute x0 -> x1, waiting for transfers between devices: none -> 1.7 us  [on_device(): other = lax.ppermute(send, 'core', [(0, 1), (1, 0)])]
  transfers between devices with their start and end apart: 4 -> 5, of which waited for: 4 -> 5; matrix products, arithmetic and copies ran while one was open for 1% -> 0% of each run, Pallas kernels for 8% -> 4%
where the time goes in v2:
time: 128 us; the launch traced here: 127 us
  blocking collectives  48.2 us (38%)
  Pallas kernels  32 us (25%)
  starting transfers between devices  22.9 us (18%)
  waiting for transfers between devices  18.9 us (15%)
  local copies, waits for them, and re-layouts  3.73 us (3%)
  between operations  1.4 us (1%)
    all_to_all x1, blocking collectives, on_device(): lax.all_to_all(half, ('tile_1', 'tile_2'), split_axis=0, concat_axis=0, t...  26.3 us
    all_to_all x1, blocking collectives, on_device(): lax.all_to_all(copies, ('tile_0', 'member_0', 'core'), split_axis=0, conc...  21.8 us
    pallas_call x1, Pallas kernels, on_device(): pl.pallas_call(join_kernel, out_shape=jax.ShapeDtypeStruct((CELLS, D + NO...  21 us
    all_to_all x1, starting transfers between devices, on_device(): lax.all_to_all(both.reshape(MEMBERS, BLOCK, D + NOISE), MEMBER, split_axi...  10.4 us
    all_to_all x1, waiting for transfers between devices, on_device(): lax.all_to_all(teacher.reshape(MEMBERS, BLOCK, D), MEMBER, split_axis=0,...  9.86 us
    all_to_all x1, waiting for transfers between devices, on_device(): lax.all_to_all(both.reshape(MEMBERS, BLOCK, D + NOISE), MEMBER, split_axi...  6 us
    pallas_call x1, Pallas kernels, on_device(): pl.pallas_call(score_kernel, out_shape=[jax.ShapeDtypeStruct((XY, 2, SHAR...  5.51 us
    all_to_all x1, starting transfers between devices, on_device(): lax.all_to_all(teacher.reshape(MEMBERS, BLOCK, D), MEMBER, split_axis=0,...  4.36 us
  transfers between devices with their start and end apart: 5, of which 5 were waited for; matrix products, arithmetic and copies ran while one was open for 0% of the time, Pallas kernels for 4%

profile of v2, /device:TPU:1, one launch (start us, length us, event | category | flops | bytes accessed | tf_op | source)
XLA Modules:
  0.0 127.3 jit_solution(6786805931943424288)
XLA Ops:
  0.7 21.0 %join.1 = bf16[512,640]{1,0:T(8,128)(2,1)} custom-call(bf16[512,512]{1,0:T(8,128)(2,1)} %bitcast.13, bf16[512,128]{1,0:T(8,128)(2,1)} %bitcast.19), custom_call_target="tpu_custom_call" | custom-call | tf_op jit(solution)/shard_map/rows/join/pallas_call | solution.py:277
  21.7 10.4 %all-to-all-start = ((bf16[8,64,640]{2,1,0:T(8,128)(2,1)}), bf16[8,64,640]{2,1,0:T(8,128)(2,1)S(1)}, u32[]{:S(2)}, u32[]{:S(2)}) async-start(bf16[8,64,640]{2,1,0:T(8,128)(2,1)} %bitcast.5), calls=%async_computation | async-start | bytes 1310720 | tf_op jit(solution)/shard_map/rows/all_to_all | solution.py:286
  32.1 1.3 %collective-permute-start.1 = (bf16[64,512]{1,0:T(8,128)(2,1)S(1)}, bf16[64,512]{1,0:T(8,128)(2,1)S(1)}, u32[]{:S(2)}, u32[]{:S(2)}) collective-permute-start(bf16[64,512]{1,0:T(8,128)(2,1)S(1)} %get-tuple-element.25), channel_id=1, source_target_pairs={{1,0},{2,1},{3,2},{4,3},{5,4},{6,5},{7,6},{8,7},{9,8},{10,9},{11,1... | collective-permute-start | bytes 196616 | tf_op jit(solution)/shard_map/halo/ppermute | solution.py:250
  33.4 4.0 %collective-permute-start = (bf16[64,512]{1,0:T(8,128)(2,1)S(1)}, bf16[64,512]{1,0:T(8,128)(2,1)S(1)}, u32[]{:S(2)}, u32[]{:S(2)}) collective-permute-start(bf16[64,512]{1,0:T(8,128)(2,1)S(1)} %get-tuple-element.26), channel_id=1, source_target_pairs={{0,1},{1,2},{2,3},{3,4},{4,5},{5,6},{6,7},{7,8},{8,9},{9,10},{10,1... | collective-permute-start | bytes 196616 | tf_op jit(solution)/shard_map/halo/ppermute | solution.py:249
  37.4 0.1 collective-permute-done.1.bottom
  37.5 1.2 collective-permute-done.top
  38.7 1.0 copy-done.8
  39.8 3.5 %teacher.1 = bf16[512,512]{1,0:T(8,128)(2,1)} custom-call(bf16[64,512]{1,0:T(8,128)(2,1)S(1)} %collective-permute-done.top, bf16[512,512]{1,0:T(8,128)(2,1)S(1)} %bitcast.14, bf16[64,512]{1,0:T(8,128)(2,1)S(1)} %collective-permute-done.1.bottom, s32[8,512]{1,0:T(8,128)S(1)} %copy-done.10, bf16[512,512]{1,0:T(8,128)(2,1)S(1)} %copy-done.8, ...), custom_call_target="tpu_custom_call" | custom-call | tf_op jit(solution)/shard_map/teach/teacher/pallas_call | solution.py:305
  43.3 6.0 %all-to-all-done = bf16[8,64,640]{2,1,0:T(8,128)(2,1)S(1)} async-done(((bf16[8,64,640]{2,1,0:T(8,128)(2,1)}), bf16[8,64,640]{2,1,0:T(8,128)(2,1)S(1)}, u32[]{:S(2)}, u32[]{:S(2)}) %all-to-all-start) | async-done | bytes 655392 | tf_op jit(solution)/shard_map/rows/all_to_all | solution.py:286
  49.3 4.4 %all-to-all-start.1 = ((bf16[8,64,512]{2,1,0:T(8,128)(2,1)}), bf16[8,64,512]{2,1,0:T(8,128)(2,1)S(1)}, u32[]{:S(2)}, u32[]{:S(2)}) async-start(bf16[8,64,512]{2,1,0:T(8,128)(2,1)} %bitcast.17), calls=%async_computation.1 | async-start | bytes 1048576 | tf_op jit(solution)/shard_map/every/all_to_all | solution.py:307
  54.3 0.1 pad_add_fusion.place
  54.4 1.1 student.1
  55.5 1.0 copy-done.4
  56.5 0.9 copy-done.5
  57.4 0.8 copy-done.7
  58.2 9.9 %all-to-all-done.1.teacher = bf16[8,64,512]{2,1,0:T(8,128)(2,1)S(1)} async-done(((bf16[8,64,512]{2,1,0:T(8,128)(2,1)}), bf16[8,64,512]{2,1,0:T(8,128)(2,1)S(1)}, u32[]{:S(2)}, u32[]{:S(2)}) %all-to-all-start.1) | async-done | bytes 524320 | tf_op jit(solution)/shard_map/every/all_to_all | solution.py:307
  68.0 5.5 %score.1 = (bf16[32,2,40,128]{3,2,1,0:T(8,128)(2,1)S(1)}, bf16[32,2,40,128]{3,2,1,0:T(8,128)(2,1)S(1)}) custom-call(bf16[8,64,512]{2,1,0:T(8,128)(2,1)S(1)} %bitcast.16, bf16[8,64,512]{2,1,0:T(8,128)(2,1)S(1)} %all-to-all-done.1.teacher, bf16[640,512]{1,0:T(8,128)(2,1)} %copy-done.5, bf16[512,512]{1,0:T(8,128)(2,1)} %copy-done.7, f32[512,512]{1,0:T(8,128)} %copy-done.4, ...), custom_call_target="tpu_custom_call" | custom-call | tf_op jit(solution)/shard_map/score/pallas_call | solution.py:327
  73.6 2.9 %collective-permute-start.2 = (bf16[32,2,40,128]{3,2,1,0:T(8,128)(2,1)S(1)}, bf16[32,2,40,128]{3,2,1,0:T(8,128)(2,1)S(1)}, u32[]{:S(2)}, u32[]{:S(2)}) collective-permute-start(bf16[32,2,40,128]{3,2,1,0:T(8,128)(2,1)S(1)} %get-tuple-element.20), channel_id=1, source_target_pairs={{0,64},{64,0},{1,65},{65,1},{2,66},{66,2},{3,67},{67,3},{4,68},{68... | collective-permute-start | bytes 1966088 | tf_op jit(solution)/shard_map/ppermute | solution.py:353
  76.4 1.7 %collective-permute-done.2 = bf16[32,2,40,128]{3,2,1,0:T(8,128)(2,1)S(1)} collective-permute-done((bf16[32,2,40,128]{3,2,1,0:T(8,128)(2,1)S(1)}, bf16[32,2,40,128]{3,2,1,0:T(8,128)(2,1)S(1)}, u32[]{:S(2)}, u32[]{:S(2)}) %collective-permute-start.2) | collective-permute-done | bytes 655392 | tf_op jit(solution)/shard_map/ppermute | solution.py:353
  78.1 0.2 add_convert_fusion
  78.3 26.3 %all_to_all.20.arrived = bf16[32,2,40,128]{3,2,1,0:T(8,128)(2,1)S(1)} all-to-all(bf16[32,2,40,128]{3,2,1,0:T(8,128)(2,1)S(1)} %add_convert_fusion), channel_id=1, replica_groups=mesh['member_0'=4,'core'=2,'tile_0'=2,'tile_1'=4,'tile_2'=8] {'tile_1','..., dimensions={0} | all-to-all | bytes 1310720 | tf_op jit(solution)/shard_map/all_to_all | solution.py:355
  104.6 0.2 fold.1
  104.8 21.8 %all_to_all.21.arrived = bf16[16,40,128]{2,1,0:T(8,128)(2,1)S(1)} all-to-all(bf16[16,40,128]{2,1,0:T(8,128)(2,1)S(1)} %fold.1), channel_id=1, replica_groups=mesh['member_0'=4,'core'=2,'tile_0'=2,'tile_1'=4,'tile_2'=8] {'tile_0','..., dimensions={0} | all-to-all | bytes 327680 | tf_op jit(solution)/shard_map/all_to_all | solution.py:364
  126.7 0.6 last.1
  (19 shorter events, 0.0 us)
Async XLA Ops:
  0.6 31.5 %copy-start = (bf16[1,512,512]{2,1,0:T(8,128)(2,1)S(1)}, bf16[1,512,512]{2,1,0:T(8,128)(2,1)}, u32[]{:S(2)}) copy-start(bf16[1,512,512]{2,1,0:T(8,128)(2,1)} %param.10) | copy-start | bytes 1572868
  0.6 38.1 %copy-start.3 = (bf16[1024,512]{1,0:T(8,128)(2,1)S(1)}, bf16[1024,512]{1,0:T(8,128)(2,1)}, u32[]{:S(2)}) copy-start(bf16[1024,512]{1,0:T(8,128)(2,1)} %down.1) | copy-start | bytes 3145732
  21.6 17.1 %copy-start.2 = (bf16[512,1024]{1,0:T(8,128)(2,1)S(1)}, bf16[512,1024]{1,0:T(8,128)(2,1)}, u32[]{:S(2)}) copy-start(bf16[512,1024]{1,0:T(8,128)(2,1)} %up.1) | copy-start | bytes 3145732
  21.6 17.1 %copy-start.10 = (s32[8,512]{1,0:T(8,128)S(1)}, s32[8,512]{1,0:T(8,128)}, u32[]{:S(2)}) copy-start(s32[8,512]{1,0:T(8,128)} %near.1) | copy-start | bytes 49156
  21.7 27.6 %all-to-all-start = ((bf16[8,64,640]{2,1,0:T(8,128)(2,1)}), bf16[8,64,640]{2,1,0:T(8,128)(2,1)S(1)}, u32[]{:S(2)}, u32[]{:S(2)}) async-start(bf16[8,64,640]{2,1,0:T(8,128)(2,1)} %bitcast.5), calls=%async_computation | async-start | bytes 1310720 | tf_op jit(solution)/shard_map/rows/all_to_all | solution.py:286
  32.1 5.4 %collective-permute-start.1 = (bf16[64,512]{1,0:T(8,128)(2,1)S(1)}, bf16[64,512]{1,0:T(8,128)(2,1)S(1)}, u32[]{:S(2)}, u32[]{:S(2)}) collective-permute-start(bf16[64,512]{1,0:T(8,128)(2,1)S(1)} %get-tuple-element.25), channel_id=1, source_target_pairs={{1,0},{2,1},{3,2},{4,3},{5,4},{6,5},{7,6},{8,7},{9,8},{10,9},{11,1... | collective-permute-start | bytes 196616 | tf_op jit(solution)/shard_map/halo/ppermute | solution.py:250
  33.4 5.3 %collective-permute-start = (bf16[64,512]{1,0:T(8,128)(2,1)S(1)}, bf16[64,512]{1,0:T(8,128)(2,1)S(1)}, u32[]{:S(2)}, u32[]{:S(2)}) collective-permute-start(bf16[64,512]{1,0:T(8,128)(2,1)S(1)} %get-tuple-element.26), channel_id=1, source_target_pairs={{0,1},{1,2},{2,3},{3,4},{4,5},{5,6},{6,7},{7,8},{8,9},{9,10},{10,1... | collective-permute-start | bytes 196616 | tf_op jit(solution)/shard_map/halo/ppermute | solution.py:249
  38.7 1.0 copy-start.8
  39.8 14.6 %copy-start.9 = (bf16[128,512]{1,0:T(8,128)(2,1)S(1)}, bf16[128,512]{1,0:T(8,128)(2,1)}, u32[]{:S(2)}) copy-start(bf16[128,512]{1,0:T(8,128)(2,1)} %w_noise.1) | copy-start | bytes 393220
  43.3 11.1 %copy-start.1 = (bf16[512,512]{1,0:T(8,128)(2,1)S(1)}, bf16[512,512]{1,0:T(8,128)(2,1)}, u32[]{:S(2)}) copy-start(bf16[512,512]{1,0:T(8,128)(2,1)} %w_out_at.1) | copy-start | bytes 1572868
  43.3 11.1 %copy-start.6 = (bf16[512,512]{1,0:T(8,128)(2,1)S(1)}, bf16[512,512]{1,0:T(8,128)(2,1)}, u32[]{:S(2)}) copy-start(bf16[512,512]{1,0:T(8,128)(2,1)} %w_in.1) | copy-start | bytes 1572868
  49.3 18.8 %all-to-all-start.1 = ((bf16[8,64,512]{2,1,0:T(8,128)(2,1)}), bf16[8,64,512]{2,1,0:T(8,128)(2,1)S(1)}, u32[]{:S(2)}, u32[]{:S(2)}) async-start(bf16[8,64,512]{2,1,0:T(8,128)(2,1)} %bitcast.17), calls=%async_computation.1 | async-start | bytes 1048576 | tf_op jit(solution)/shard_map/every/all_to_all | solution.py:307
  55.5 1.0 copy-start.4
  56.5 0.9 copy-start.5
  57.4 0.8 copy-start.7
  73.6 4.6 %collective-permute-start.2 = (bf16[32,2,40,128]{3,2,1,0:T(8,128)(2,1)S(1)}, bf16[32,2,40,128]{3,2,1,0:T(8,128)(2,1)S(1)}, u32[]{:S(2)}, u32[]{:S(2)}) collective-permute-start(bf16[32,2,40,128]{3,2,1,0:T(8,128)(2,1)S(1)} %get-tuple-element.20), channel_id=1, source_target_pairs={{0,64},{64,0},{1,65},{65,1},{2,66},{66,2},{3,67},{67,3},{4,68},{68... | collective-permute-start | bytes 1966088 | tf_op jit(solution)/shard_map/ppermute | solution.py:353

commit v3 on v2

--- a/solution.py
+++ b/solution.py
@@ -9,7 +9,6 @@
 from jax.sharding import PartitionSpec as P
 
 D = 512
-FF = 1024
 H = 512
 NOISE = 128
 NBRS = 8
@@ -31,10 +30,14 @@
 F32 = jnp.float32
 
 
-def teacher_kernel(top, state, bottom, near, msg, up, down, out, ext):
-    ext[0:HALO] = top[...]
+def teacher_kernel(
+    top, top_far, state, bottom, bottom_far, near, msg_at, up, down, out, ext, msg, sem
+):
+    copy = pltpu.make_async_copy(msg_at, msg, sem)
+    copy.start()
+    ext[0:HALO] = top[...] + top_far[...]
     ext[HALO : HALO + CELLS] = state[...]
-    ext[HALO + CELLS :] = bottom[...]
+    ext[HALO + CELLS :] = bottom[...] + bottom_far[...]
     rows = 256
     sub = 128
     for at in range(0, CELLS, rows):
@@ -53,6 +56,8 @@
                 ).astype(BF16)
             )
         gathered = jnp.concatenate(parts, axis=0)
+        if at == 0:
+            copy.wait()
         resid = state[at : at + rows].astype(F32) + jnp.dot(
             gathered, msg[...], preferred_element_type=F32
         )
@@ -243,11 +248,9 @@
             region_loss[...] = loss * (1.0 / (CELLS_ALL // REGIONS * D))
 
 
-def halos(state):
-    count = TILES
-    ends = count - 1
-    up = lax.ppermute(state[CELLS - HALO :], TILE, [(i, i + 1) for i in range(ends)])
-    down = lax.ppermute(state[:HALO], TILE, [(i + 1, i) for i in range(ends)])
+def halos(state, links):
+    up = lax.ppermute(state[CELLS - HALO :], TILE, [(i, i + 1) for i in links])
+    down = lax.ppermute(state[:HALO], TILE, [(i + 1, i) for i in links])
     return up, down
 
 
@@ -260,7 +263,7 @@
     return pltpu.with_memory_space_constraint(array, pltpu.HBM)
 
 
-def on_device(
+def step(
     inputs,
     noise,
     neighbours,
@@ -273,40 +276,51 @@
     student_out,
 ):
     state = inputs[0]
-    with jax.named_scope("rows"):
-        both = pl.pallas_call(
-            join_kernel,
-            out_shape=jax.ShapeDtypeStruct((CELLS, D + NOISE), BF16),
-            in_specs=[HBM] * 2,
-            out_specs=HBM,
-            scratch_shapes=[pltpu.SemaphoreType.DMA((2,))],
-            compiler_params=PARAMS,
-            name="join",
-        )(in_hbm(state), in_hbm(noise[0]))
-        mine = lax.all_to_all(
-            both.reshape(MEMBERS, BLOCK, D + NOISE),
-            MEMBER,
-            split_axis=0,
-            concat_axis=0,
-            tiled=True,
-        )
-    with jax.named_scope("halo"):
-        top, bottom = halos(state)
+    both = pl.pallas_call(
+        join_kernel,
+        out_shape=jax.ShapeDtypeStruct((CELLS, D + NOISE), BF16),
+        in_specs=[HBM] * 2,
+        out_specs=VMEM,
+        scratch_shapes=[pltpu.SemaphoreType.DMA((2,))],
+        compiler_params=PARAMS,
+        name="join",
+    )(in_hbm(state), in_hbm(noise[0]))
+    mine = lax.all_to_all(
+        both.reshape(MEMBERS, BLOCK, D + NOISE),
+        MEMBER,
+        split_axis=0,
+        concat_axis=0,
+        tiled=True,
+    )
+    top_far, bottom_far = halos(state, [XY - 1])
+    top, bottom = halos(state, [i for i in range(TILES - 1) if i != XY - 1])
     teach = pl.pallas_call(
         teacher_kernel,
         out_shape=jax.ShapeDtypeStruct((CELLS, D), BF16),
-        in_specs=[VMEM] * 7,
+        in_specs=[VMEM] * 6 + [HBM] + [VMEM] * 2,
         out_specs=VMEM,
-        scratch_shapes=[pltpu.VMEM((CELLS + 2 * HALO, D), BF16)],
+        scratch_shapes=[
+            pltpu.VMEM((CELLS + 2 * HALO, D), BF16),
+            pltpu.VMEM((D, D), BF16),
+            pltpu.SemaphoreType.DMA,
+        ],
         compiler_params=PARAMS,
         name="teacher",
     )
-    with jax.named_scope("teach"):
-        teacher = teach(top, state, bottom, neighbours, msg_weight, up_weight, down_weight)
-    with jax.named_scope("every"):
-        every = lax.all_to_all(
-            teacher.reshape(MEMBERS, BLOCK, D), MEMBER, split_axis=0, concat_axis=0, tiled=True
-        )
+    teacher = teach(
+        top,
+        top_far,
+        state,
+        bottom,
+        bottom_far,
+        neighbours,
+        in_hbm(msg_weight),
+        up_weight,
+        down_weight,
+    )
+    every = lax.all_to_all(
+        teacher.reshape(MEMBERS, BLOCK, D), MEMBER, split_axis=0, concat_axis=0, tiled=True
+    )
     mine = mine.reshape(CELLS, D + NOISE)
     pupil = pl.pallas_call(
         student_kernel,
@@ -321,8 +335,7 @@
         compiler_params=PARAMS,
         name="student",
     )
-    with jax.named_scope("pupil"):
-        student, shidden, slope, turned = pupil(mine, student_in, student_noise, student_out)
+    student, shidden, slope, turned = pupil(mine, student_in, student_noise, student_out)
     place = jnp.stack([region_map[0], lax.axis_index("core").astype(jnp.int32)])
     send, keep = pl.pallas_call(
         score_kernel,
@@ -397,6 +410,4 @@
         P(),
     )
     out_specs = (P(MEMBER, TILE, None), P(), P(TILE, None), P(TILE, None), P(TILE, None))
-    return jax.shard_map(
-        on_device, mesh=split, in_specs=in_specs, out_specs=out_specs, check_vma=False
-    )
+    return jax.shard_map(step, mesh=split, in_specs=in_specs, out_specs=out_specs, check_vma=False)

time: 128 us -> 110 us (0.86)
  Pallas kernels: 32 us -> 13.5 us
  starting transfers between devices: 22.9 us -> 24.3 us
    pallas_call x6, Pallas kernels: 32 us -> 13.5 us  [the longest x1 5.51 us: step(): pl.pallas_call(score_kernel, out_shape=[jax.ShapeDtypeStruct((XY, 2, SHAR...]
    ppermute x3 -> x5, starting transfers between devices: 8.15 us -> 9.48 us  [the longest x2 4.65 us: halos(): up = lax.ppermute(state[CELLS - HALO:], TILE, [(i, i + 1) for i in links])]
    unnamed x22 -> x20, local copies, waits for them, and re-layouts: 3.72 us -> 2.7 us
    ppermute x3 -> x5, waiting for transfers between devices: 3.01 us -> 2.99 us  [the longest x1 1.7 us: step(): other = lax.ppermute(send, 'core', [(0, 1), (1, 0)])]
  transfers between devices with their start and end apart: 5 -> 7, of which waited for: 5 -> 4; matrix products, arithmetic and copies ran while one was open for 0% -> 0% of each run, Pallas kernels for 4% -> 5%
where the time goes in v3:
time: 110 us; the launch traced here: 109 us
  blocking collectives  48.9 us (44%)
  starting transfers between devices  24.3 us (22%)
  waiting for transfers between devices  18 us (16%)
  Pallas kernels  13.5 us (12%)
  local copies, waits for them, and re-layouts  2.71 us (2%)
  between operations  1.46 us (1%)
    all_to_all x1, blocking collectives, step(): lax.all_to_all(half, ('tile_1', 'tile_2'), split_axis=0, concat_axis=0, t...  31.4 us
    all_to_all x1, blocking collectives, step(): lax.all_to_all(copies, ('tile_0', 'member_0', 'core'), split_axis=0, conc...  17.6 us
    all_to_all x1, starting transfers between devices, step(): lax.all_to_all(both.reshape(MEMBERS, BLOCK, D + NOISE), MEMBER, split_axi...  10.4 us
    all_to_all x1, waiting for transfers between devices, step(): lax.all_to_all(teacher.reshape(MEMBERS, BLOCK, D), MEMBER, split_axis=0,...  9.84 us
    pallas_call x1, Pallas kernels, step(): pl.pallas_call(score_kernel, out_shape=[jax.ShapeDtypeStruct((XY, 2, SHAR...  5.51 us
    all_to_all x1, waiting for transfers between devices, step(): lax.all_to_all(both.reshape(MEMBERS, BLOCK, D + NOISE), MEMBER, split_axi...  5.21 us
    ppermute x2, starting transfers between devices, halos(): up = lax.ppermute(state[CELLS - HALO:], TILE, [(i, i + 1) for i in links])  4.65 us
    all_to_all x1, starting transfers between devices, step(): lax.all_to_all(teacher.reshape(MEMBERS, BLOCK, D), MEMBER, split_axis=0,...  4.36 us
  transfers between devices with their start and end apart: 7, of which 4 were waited for; matrix products, arithmetic and copies ran while one was open for 0% of the time, Pallas kernels for 5%

profile of v3, /device:TPU:1, one launch (start us, length us, event | category | flops | bytes accessed | tf_op | source)
XLA Modules:
  0.0 109.2 jit_solution(16793077470272029953)
XLA Ops:
  0.7 2.1 %join.1 = bf16[512,640]{1,0:T(8,128)(2,1)} custom-call(bf16[512,512]{1,0:T(8,128)(2,1)} %bitcast.13, bf16[512,128]{1,0:T(8,128)(2,1)} %bitcast.19), custom_call_target="tpu_custom_call" | custom-call | tf_op jit(solution)/shard_map/join/pallas_call | solution.py:279
  2.8 10.4 %all-to-all-start = ((bf16[8,64,640]{2,1,0:T(8,128)(2,1)}), bf16[8,64,640]{2,1,0:T(8,128)(2,1)S(1)}, u32[]{:S(2)}, u32[]{:S(2)}) async-start(bf16[8,64,640]{2,1,0:T(8,128)(2,1)} %bitcast.5), calls=%async_computation | async-start | bytes 1310720 | tf_op jit(solution)/shard_map/all_to_all | solution.py:288
  13.2 0.7 collective-permute-start.3
  13.9 1.3 %collective-permute-start.2 = (bf16[64,512]{1,0:T(8,128)(2,1)S(1)}, bf16[64,512]{1,0:T(8,128)(2,1)S(1)}, u32[]{:S(2)}, u32[]{:S(2)}) collective-permute-start(bf16[64,512]{1,0:T(8,128)(2,1)S(1)} %get-tuple-element.25), channel_id=1, source_target_pairs={{1,0},{2,1},{3,2},{4,3},{5,4},{6,5},{7,6},{8,7},{9,8},{10,9},{11,1... | collective-permute-start | bytes 196616 | tf_op jit(solution)/shard_map/ppermute | solution.py:253
  15.2 0.7 collective-permute-start.1
  15.8 4.0 %collective-permute-start = (bf16[64,512]{1,0:T(8,128)(2,1)S(1)}, bf16[64,512]{1,0:T(8,128)(2,1)S(1)}, u32[]{:S(2)}, u32[]{:S(2)}) collective-permute-start(bf16[64,512]{1,0:T(8,128)(2,1)S(1)} %get-tuple-element.26), channel_id=1, source_target_pairs={{0,1},{1,2},{2,3},{3,4},{4,5},{5,6},{6,7},{7,8},{8,9},{9,10},{10,1... | collective-permute-start | bytes 196616 | tf_op jit(solution)/shard_map/ppermute | solution.py:252
  19.9 1.3 %collective-permute-done.top = bf16[64,512]{1,0:T(8,128)(2,1)S(1)} collective-permute-done((bf16[64,512]{1,0:T(8,128)(2,1)S(1)}, bf16[64,512]{1,0:T(8,128)(2,1)S(1)}, u32[]{:S(2)}, u32[]{:S(2)}) %collective-permute-start) | collective-permute-done | bytes 65568 | tf_op jit(solution)/shard_map/ppermute | solution.py:252
  21.2 4.0 %teacher.1 = bf16[512,512]{1,0:T(8,128)(2,1)} custom-call(bf16[64,512]{1,0:T(8,128)(2,1)S(1)} %collective-permute-done.top, bf16[64,512]{1,0:T(8,128)(2,1)S(1)} %collective-permute-done.1.top_far, bf16[512,512]{1,0:T(8,128)(2,1)S(1)} %bitcast.14, bf16[64,512]{1,0:T(8,128)(2,1)S(1)} %collective-permute-done.2.bottom, ...), custom_call_target="tpu_custom_call" | custom-call | tf_op jit(solution)/shard_map/teacher/pallas_call | solution.py:310
  25.2 5.2 %all-to-all-done = bf16[8,64,640]{2,1,0:T(8,128)(2,1)S(1)} async-done(((bf16[8,64,640]{2,1,0:T(8,128)(2,1)}), bf16[8,64,640]{2,1,0:T(8,128)(2,1)S(1)}, u32[]{:S(2)}, u32[]{:S(2)}) %all-to-all-start) | async-done | bytes 655392 | tf_op jit(solution)/shard_map/all_to_all | solution.py:288
  30.4 4.4 %all-to-all-start.1 = ((bf16[8,64,512]{2,1,0:T(8,128)(2,1)}), bf16[8,64,512]{2,1,0:T(8,128)(2,1)S(1)}, u32[]{:S(2)}, u32[]{:S(2)}) async-start(bf16[8,64,512]{2,1,0:T(8,128)(2,1)} %bitcast.17), calls=%async_computation.1 | async-start | bytes 1048576 | tf_op jit(solution)/shard_map/all_to_all | solution.py:321
  35.4 0.1 pad_add_fusion.place
  35.5 1.1 %student.1 = (bf16[512,512]{1,0:T(8,128)(2,1)S(1)}, bf16[512,512]{1,0:T(8,128)(2,1)S(1)}, f32[512,512]{1,0:T(8,128)S(1)}, bf16[640,512]{1,0:T(8,128)(2,1)S(1)}) custom-call(bf16[512,640]{1,0:T(8,128)(2,1)S(1)} %bitcast.15, bf16[512,512]{1,0:T(8,128)(2,1)S(1)} %copy-done.6, bf16[128,512]{1,0:T(8,128)(2,1)S(1)} %copy-done.8, bf16[512,512]{1,0:T(8,128)(2,1)S(1)} %copy-done.1), custom_call_target="tpu_custom_call" | custom-call | tf_op jit(solution)/shard_map/student/pallas_call | solution.py:338
  36.6 1.0 copy-done.4
  37.6 0.9 copy-done.5
  38.5 0.8 copy-done.7
  39.3 9.8 %all-to-all-done.1.teacher = bf16[8,64,512]{2,1,0:T(8,128)(2,1)S(1)} async-done(((bf16[8,64,512]{2,1,0:T(8,128)(2,1)}), bf16[8,64,512]{2,1,0:T(8,128)(2,1)S(1)}, u32[]{:S(2)}, u32[]{:S(2)}) %all-to-all-start.1) | async-done | bytes 524320 | tf_op jit(solution)/shard_map/all_to_all | solution.py:321
  49.1 5.5 %score.1 = (bf16[32,2,40,128]{3,2,1,0:T(8,128)(2,1)S(1)}, bf16[32,2,40,128]{3,2,1,0:T(8,128)(2,1)S(1)}) custom-call(bf16[8,64,512]{2,1,0:T(8,128)(2,1)S(1)} %bitcast.16, bf16[8,64,512]{2,1,0:T(8,128)(2,1)S(1)} %all-to-all-done.1.teacher, bf16[640,512]{1,0:T(8,128)(2,1)} %copy-done.5, bf16[512,512]{1,0:T(8,128)(2,1)} %copy-done.7, f32[512,512]{1,0:T(8,128)} %copy-done.4, ...), custom_call_target="tpu_custom_call" | custom-call | tf_op jit(solution)/shard_map/score/pallas_call | solution.py:340
  54.6 2.9 %collective-permute-start.4 = (bf16[32,2,40,128]{3,2,1,0:T(8,128)(2,1)S(1)}, bf16[32,2,40,128]{3,2,1,0:T(8,128)(2,1)S(1)}, u32[]{:S(2)}, u32[]{:S(2)}) collective-permute-start(bf16[32,2,40,128]{3,2,1,0:T(8,128)(2,1)S(1)} %get-tuple-element.20), channel_id=1, source_target_pairs={{0,64},{64,0},{1,65},{65,1},{2,66},{66,2},{3,67},{67,3},{4,68},{68... | collective-permute-start | bytes 1966088 | tf_op jit(solution)/shard_map/ppermute | solution.py:366
  57.5 1.7 %collective-permute-done.4 = bf16[32,2,40,128]{3,2,1,0:T(8,128)(2,1)S(1)} collective-permute-done((bf16[32,2,40,128]{3,2,1,0:T(8,128)(2,1)S(1)}, bf16[32,2,40,128]{3,2,1,0:T(8,128)(2,1)S(1)}, u32[]{:S(2)}, u32[]{:S(2)}) %collective-permute-start.4) | collective-permute-done | bytes 655392 | tf_op jit(solution)/shard_map/ppermute | solution.py:366
  59.2 0.2 add_convert_fusion
  59.4 31.4 %all_to_all.20.arrived = bf16[32,2,40,128]{3,2,1,0:T(8,128)(2,1)S(1)} all-to-all(bf16[32,2,40,128]{3,2,1,0:T(8,128)(2,1)S(1)} %add_convert_fusion), channel_id=1, replica_groups=mesh['member_0'=4,'core'=2,'tile_0'=2,'tile_1'=4,'tile_2'=8] {'tile_1','..., dimensions={0} | all-to-all | bytes 1310720 | tf_op jit(solution)/shard_map/all_to_all | solution.py:368
  90.8 0.2 fold.1
  91.0 17.6 %all_to_all.21.arrived = bf16[16,40,128]{2,1,0:T(8,128)(2,1)S(1)} all-to-all(bf16[16,40,128]{2,1,0:T(8,128)(2,1)S(1)} %fold.1), channel_id=1, replica_groups=mesh['member_0'=4,'core'=2,'tile_0'=2,'tile_1'=4,'tile_2'=8] {'tile_0','..., dimensions={0} | all-to-all | bytes 327680 | tf_op jit(solution)/shard_map/all_to_all | solution.py:377
  108.5 0.6 last.1
  (21 shorter events, 0.1 us)
Async XLA Ops:
  0.6 12.5 %copy-start = (bf16[1,512,512]{2,1,0:T(8,128)(2,1)S(1)}, bf16[1,512,512]{2,1,0:T(8,128)(2,1)}, u32[]{:S(2)}) copy-start(bf16[1,512,512]{2,1,0:T(8,128)(2,1)} %param.10) | copy-start | bytes 1572868
  0.6 20.5 %copy-start.3 = (bf16[1024,512]{1,0:T(8,128)(2,1)S(1)}, bf16[1024,512]{1,0:T(8,128)(2,1)}, u32[]{:S(2)}) copy-start(bf16[1024,512]{1,0:T(8,128)(2,1)} %down.1) | copy-start | bytes 3145732
  2.7 18.4 %copy-start.2 = (bf16[512,1024]{1,0:T(8,128)(2,1)S(1)}, bf16[512,1024]{1,0:T(8,128)(2,1)}, u32[]{:S(2)}) copy-start(bf16[512,1024]{1,0:T(8,128)(2,1)} %up.1) | copy-start | bytes 3145732
  2.7 18.4 %copy-start.9 = (s32[8,512]{1,0:T(8,128)S(1)}, s32[8,512]{1,0:T(8,128)}, u32[]{:S(2)}) copy-start(s32[8,512]{1,0:T(8,128)} %near.1) | copy-start | bytes 49156
  2.8 27.6 %all-to-all-start = ((bf16[8,64,640]{2,1,0:T(8,128)(2,1)}), bf16[8,64,640]{2,1,0:T(8,128)(2,1)S(1)}, u32[]{:S(2)}, u32[]{:S(2)}) async-start(bf16[8,64,640]{2,1,0:T(8,128)(2,1)} %bitcast.5), calls=%async_computation | async-start | bytes 1310720 | tf_op jit(solution)/shard_map/all_to_all | solution.py:288
  13.2 6.6 %collective-permute-start.3 = (bf16[64,512]{1,0:T(8,128)(2,1)S(1)}, bf16[64,512]{1,0:T(8,128)(2,1)S(1)}, u32[]{:S(2)}, u32[]{:S(2)}) collective-permute-start(bf16[64,512]{1,0:T(8,128)(2,1)S(1)} %get-tuple-element.25), channel_id=1, source_target_pairs={{32,31},{96,95},{160,159},{224,223},{288,287},{352,351},{416,415},... | collective-permute-start | bytes 196616 | tf_op jit(solution)/shard_map/ppermute | solution.py:253
  13.9 6.0 %collective-permute-start.2 = (bf16[64,512]{1,0:T(8,128)(2,1)S(1)}, bf16[64,512]{1,0:T(8,128)(2,1)S(1)}, u32[]{:S(2)}, u32[]{:S(2)}) collective-permute-start(bf16[64,512]{1,0:T(8,128)(2,1)S(1)} %get-tuple-element.25), channel_id=1, source_target_pairs={{1,0},{2,1},{3,2},{4,3},{5,4},{6,5},{7,6},{8,7},{9,8},{10,9},{11,1... | collective-permute-start | bytes 196616 | tf_op jit(solution)/shard_map/ppermute | solution.py:253
  15.2 4.7 %collective-permute-start.1 = (bf16[64,512]{1,0:T(8,128)(2,1)S(1)}, bf16[64,512]{1,0:T(8,128)(2,1)S(1)}, u32[]{:S(2)}, u32[]{:S(2)}) collective-permute-start(bf16[64,512]{1,0:T(8,128)(2,1)S(1)} %get-tuple-element.26), channel_id=1, source_target_pairs={{31,32},{95,96},{159,160},{223,224},{287,288},{351,352},{415,416},... | collective-permute-start | bytes 196616 | tf_op jit(solution)/shard_map/ppermute | solution.py:252
  15.8 5.3 %collective-permute-start = (bf16[64,512]{1,0:T(8,128)(2,1)S(1)}, bf16[64,512]{1,0:T(8,128)(2,1)S(1)}, u32[]{:S(2)}, u32[]{:S(2)}) collective-permute-start(bf16[64,512]{1,0:T(8,128)(2,1)S(1)} %get-tuple-element.26), channel_id=1, source_target_pairs={{0,1},{1,2},{2,3},{3,4},{4,5},{5,6},{6,7},{7,8},{8,9},{9,10},{10,1... | collective-permute-start | bytes 196616 | tf_op jit(solution)/shard_map/ppermute | solution.py:252
  21.2 14.3 %copy-start.8 = (bf16[128,512]{1,0:T(8,128)(2,1)S(1)}, bf16[128,512]{1,0:T(8,128)(2,1)}, u32[]{:S(2)}) copy-start(bf16[128,512]{1,0:T(8,128)(2,1)} %w_noise.1) | copy-start | bytes 393220
  25.1 10.3 %copy-start.1 = (bf16[512,512]{1,0:T(8,128)(2,1)S(1)}, bf16[512,512]{1,0:T(8,128)(2,1)}, u32[]{:S(2)}) copy-start(bf16[512,512]{1,0:T(8,128)(2,1)} %w_out_at.1) | copy-start | bytes 1572868
  25.2 10.3 %copy-start.6 = (bf16[512,512]{1,0:T(8,128)(2,1)S(1)}, bf16[512,512]{1,0:T(8,128)(2,1)}, u32[]{:S(2)}) copy-start(bf16[512,512]{1,0:T(8,128)(2,1)} %w_in.1) | copy-start | bytes 1572868
  30.4 18.8 %all-to-all-start.1 = ((bf16[8,64,512]{2,1,0:T(8,128)(2,1)}), bf16[8,64,512]{2,1,0:T(8,128)(2,1)S(1)}, u32[]{:S(2)}, u32[]{:S(2)}) async-start(bf16[8,64,512]{2,1,0:T(8,128)(2,1)} %bitcast.17), calls=%async_computation.1 | async-start | bytes 1048576 | tf_op jit(solution)/shard_map/all_to_all | solution.py:321
  36.6 1.0 copy-start.4
  37.6 0.9 copy-start.5
  38.5 0.8 copy-start.7
  54.6 4.6 %collective-permute-start.4 = (bf16[32,2,40,128]{3,2,1,0:T(8,128)(2,1)S(1)}, bf16[32,2,40,128]{3,2,1,0:T(8,128)(2,1)S(1)}, u32[]{:S(2)}, u32[]{:S(2)}) collective-permute-start(bf16[32,2,40,128]{3,2,1,0:T(8,128)(2,1)S(1)} %get-tuple-element.20), channel_id=1, source_target_pairs={{0,64},{64,0},{1,65},{65,1},{2,66},{66,2},{3,67},{67,3},{4,68},{68... | collective-permute-start | bytes 1966088 | tf_op jit(solution)/shard_map/ppermute | solution.py:366

commit v4 on v3

--- a/solution.py
+++ b/solution.py
@@ -21,6 +21,7 @@
 TILES = 64
 HALF = D // 2
 XY = TILES // 2
+JOINS = 4
 SHARE = 40
 LOSS_ROW = 36
 
@@ -30,53 +31,106 @@
 F32 = jnp.float32
 
 
-def teacher_kernel(
-    top, top_far, state, bottom, bottom_far, near, msg_at, up, down, out, ext, msg, sem
-):
+def counts(picks, start, rows, width):
+    lanes = lax.broadcasted_iota(jnp.int32, (rows, width), 1) + start
+    count = jnp.zeros((rows, width), F32)
+    for k in range(NBRS):
+        count = count + jnp.where(picks[:, k : k + 1] == lanes, 1.0 / NBRS, 0.0)
+    return count.astype(BF16)
+
+
+def teach(state, gathered, msg, up, down):
+    resid = state.astype(F32) + jnp.dot(gathered, msg, preferred_element_type=F32)
+    power = jnp.mean(resid * resid, axis=1, keepdims=True)
+    normed = (resid * lax.rsqrt(power + 1e-06)).astype(BF16)
+    hidden = jax.nn.silu(jnp.dot(normed, up, preferred_element_type=F32)).astype(BF16)
+    return (resid + jnp.dot(hidden, down, preferred_element_type=F32)).astype(BF16)
+
+
+def middle_kernel(state, near, msg_at, up, down, out, msg, held, sem, out_sem):
     copy = pltpu.make_async_copy(msg_at, msg, sem)
     copy.start()
-    ext[0:HALO] = top[...] + top_far[...]
-    ext[HALO : HALO + CELLS] = state[...]
-    ext[HALO + CELLS :] = bottom[...] + bottom_far[...]
-    rows = 256
     sub = 128
-    for at in range(0, CELLS, rows):
-        parts = []
-        for start in range(at, at + rows, sub):
-            picks = near[:, start : start + sub].T
-            lanes = lax.broadcasted_iota(jnp.int32, (sub, 2 * sub), 1) + start
-            count = jnp.zeros((sub, 2 * sub), F32)
-            for k in range(NBRS):
-                count = count + jnp.where(picks[:, k : k + 1] == lanes, 1.0 / NBRS, 0.0)
-            parts.append(
-                jnp.dot(
-                    count.astype(BF16),
-                    ext[start : start + 2 * sub],
-                    preferred_element_type=F32,
-                ).astype(BF16)
+    parts = []
+    for at in range(0, CELLS - 2 * HALO, sub):
+        picks = near[:, HALO + at : HALO + at + sub].T
+        parts.append(
+            jnp.dot(
+                counts(picks, HALO + at, sub, 2 * sub),
+                state[at : at + 2 * sub],
+                preferred_element_type=F32,
+            ).astype(BF16)
+        )
+    copy.wait()
+    half = (CELLS - 2 * HALO) // 2
+    gathered = jnp.concatenate(parts, axis=0)
+    writes = []
+    for k, at in enumerate((0, half)):
+        held[at : at + half] = teach(
+            state[HALO + at : HALO + at + half],
+            gathered[at : at + half],
+            msg[...],
+            up[...],
+            down[...],
+        )
+        writes.append(
+            pltpu.make_async_copy(
+                held.at[at : at + half], out.at[HALO + at : HALO + at + half], out_sem.at[k]
             )
-        gathered = jnp.concatenate(parts, axis=0)
-        if at == 0:
+        )
+        writes[-1].start()
+    for copy in writes:
+        copy.wait()
+
+
+def edges_kernel(top, top_far, state, bottom, bottom_far, near, msg, up, down, partly, out, held, sem):
+    reach = 3 * HALO
+    above = jnp.concatenate([top[...] + top_far[...], state[: 2 * HALO]], axis=0)
+    below = jnp.concatenate([state[CELLS - 2 * HALO :], bottom[...] + bottom_far[...]], axis=0)
+    first = near[:, : 2 * HALO].T[:HALO]
+    last = near[:, CELLS - 2 * HALO :].T[HALO:]
+    gathered = jnp.concatenate(
+        [
+            jnp.dot(counts(first, 0, HALO, reach), above, preferred_element_type=F32),
+            jnp.dot(
+                counts(last, CELLS - HALO, HALO, reach), below, preferred_element_type=F32
+            ),
+        ],
+        axis=0,
+    ).astype(BF16)
+    ends = jnp.concatenate([state[:HALO], state[CELLS - HALO :]], axis=0)
+    held[...] = teach(ends, gathered, msg[...], up[...], down[...])
+    writes = [
+        pltpu.make_async_copy(held.at[:HALO], out.at[:HALO], sem.at[0]),
+        pltpu.make_async_copy(held.at[HALO:], out.at[CELLS - HALO :], sem.at[1]),
+    ]
+    for copy in writes:
+        copy.start()
+    for copy in writes:
+        copy.wait()
+
+
+def join_kernel(state, noise, both, held, sem, out_sem):
+    rows = CELLS // JOINS
+    reads = []
+    for k in range(JOINS):
+        at = pl.ds(k * rows, rows)
+        reads.append(
+            (
+                pltpu.make_async_copy(state.at[at], held.at[at, :D], sem.at[2 * k]),
+                pltpu.make_async_copy(noise.at[at], held.at[at, D:], sem.at[2 * k + 1]),
+            )
+        )
+        for copy in reads[-1]:
+            copy.start()
+    writes = []
+    for k in range(JOINS):
+        at = pl.ds(k * rows, rows)
+        for copy in reads[k]:
             copy.wait()
-        resid = state[at : at + rows].astype(F32) + jnp.dot(
-            gathered, msg[...], preferred_element_type=F32
-        )
-        power = jnp.mean(resid * resid, axis=1, keepdims=True)
-        normed = (resid * lax.rsqrt(power + 1e-06)).astype(BF16)
-        hidden = jax.nn.silu(jnp.dot(normed, up[...], preferred_element_type=F32)).astype(BF16)
-        out[at : at + rows] = (
-            resid + jnp.dot(hidden, down[...], preferred_element_type=F32)
-        ).astype(BF16)
-
-
-def join_kernel(state, noise, both, sem):
-    copies = [
-        pltpu.make_async_copy(state, both.at[:, :D], sem.at[0]),
-        pltpu.make_async_copy(noise, both.at[:, D:], sem.at[1]),
-    ]
-    for copy in copies:
-        copy.start()
-    for copy in copies:
+        writes.append(pltpu.make_async_copy(held.at[at], both.at[at], out_sem.at[k]))
+        writes[-1].start()
+    for copy in writes:
         copy.wait()
 
 
@@ -280,8 +334,12 @@
         join_kernel,
         out_shape=jax.ShapeDtypeStruct((CELLS, D + NOISE), BF16),
         in_specs=[HBM] * 2,
-        out_specs=VMEM,
-        scratch_shapes=[pltpu.SemaphoreType.DMA((2,))],
+        out_specs=HBM,
+        scratch_shapes=[
+            pltpu.VMEM((CELLS, D + NOISE), BF16),
+            pltpu.SemaphoreType.DMA((2 * JOINS,)),
+            pltpu.SemaphoreType.DMA((JOINS,)),
+        ],
         compiler_params=PARAMS,
         name="join",
     )(in_hbm(state), in_hbm(noise[0]))
@@ -294,29 +352,42 @@
     )
     top_far, bottom_far = halos(state, [XY - 1])
     top, bottom = halos(state, [i for i in range(TILES - 1) if i != XY - 1])
-    teach = pl.pallas_call(
-        teacher_kernel,
+    middle = pl.pallas_call(
+        middle_kernel,
         out_shape=jax.ShapeDtypeStruct((CELLS, D), BF16),
-        in_specs=[VMEM] * 6 + [HBM] + [VMEM] * 2,
-        out_specs=VMEM,
+        in_specs=[VMEM] * 2 + [HBM] + [VMEM] * 2,
+        out_specs=HBM,
         scratch_shapes=[
-            pltpu.VMEM((CELLS + 2 * HALO, D), BF16),
             pltpu.VMEM((D, D), BF16),
+            pltpu.VMEM((CELLS - 2 * HALO, D), BF16),
             pltpu.SemaphoreType.DMA,
+            pltpu.SemaphoreType.DMA((2,)),
         ],
         compiler_params=PARAMS,
-        name="teacher",
-    )
-    teacher = teach(
+        name="middle",
+    )
+    edges = pl.pallas_call(
+        edges_kernel,
+        out_shape=jax.ShapeDtypeStruct((CELLS, D), BF16),
+        in_specs=[VMEM] * 9 + [HBM],
+        out_specs=HBM,
+        input_output_aliases={9: 0},
+        scratch_shapes=[pltpu.VMEM((2 * HALO, D), BF16), pltpu.SemaphoreType.DMA((2,))],
+        compiler_params=PARAMS,
+        name="edges",
+    )
+    partly = middle(state, neighbours, in_hbm(msg_weight), up_weight, down_weight)
+    teacher = edges(
         top,
         top_far,
         state,
         bottom,
         bottom_far,
         neighbours,
-        in_hbm(msg_weight),
+        msg_weight,
         up_weight,
         down_weight,
+        partly,
     )
     every = lax.all_to_all(
         teacher.reshape(MEMBERS, BLOCK, D), MEMBER, split_axis=0, concat_axis=0, tiled=True

time: 110 us -> 108 us (0.982)
  blocking collectives: 48.9 us -> 46.9 us
  waiting for transfers between devices: 18 us -> 16.5 us
  Pallas kernels: 13.5 us -> 14.8 us
    pallas_call x1 -> x2, Pallas kernels: 3.97 us -> 5.37 us  [the longest x1 3.52 us: step(): middle(state, neighbours, in_hbm(msg_weight), up_weight, down_weight)]
    ppermute x2, waiting for transfers between devices: 1.28 us -> 0.01 us  [halos(): up = lax.ppermute(state[CELLS - HALO:], TILE, [(i, i + 1) for i in links])]
    all_to_all x1, blocking collectives: 31.4 us -> 30.2 us  [step(): lax.all_to_all(half, ('tile_1', 'tile_2'), split_axis=0, concat_axis=0, t...]
    unnamed x20 -> x24, local copies, waits for them, and re-layouts: 2.7 us -> 3.54 us
  transfers between devices with their start and end apart: 7 -> 7, of which waited for: 4 -> 3; matrix products, arithmetic and copies ran while one was open for 0% -> 0% of each run, Pallas kernels for 5% -> 6%
where the time goes in v4:
time: 108 us
  blocking collectives  46.9 us (43%)
  starting transfers between devices  24.4 us (23%)
  waiting for transfers between devices  16.5 us (15%)
  Pallas kernels  14.8 us (14%)
  local copies, waits for them, and re-layouts  3.55 us (3%)
  between operations  1.51 us (1%)
    all_to_all x1, blocking collectives, step(): lax.all_to_all(half, ('tile_1', 'tile_2'), split_axis=0, concat_axis=0, t...  30.2 us
    all_to_all x1, blocking collectives, step(): lax.all_to_all(copies, ('tile_0', 'member_0', 'core'), split_axis=0, conc...  16.7 us
    all_to_all x1, starting transfers between devices, step(): lax.all_to_all(both.reshape(MEMBERS, BLOCK, D + NOISE), MEMBER, split_axi...  10.4 us
    all_to_all x1, waiting for transfers between devices, step(): lax.all_to_all(teacher.reshape(MEMBERS, BLOCK, D), MEMBER, split_axis=0,...  9.87 us
    pallas_call x1, Pallas kernels, step(): pl.pallas_call(score_kernel, out_shape=[jax.ShapeDtypeStruct((XY, 2, SHAR...  5.51 us
    all_to_all x1, waiting for transfers between devices, step(): lax.all_to_all(both.reshape(MEMBERS, BLOCK, D + NOISE), MEMBER, split_axi...  4.9 us
    ppermute x2, starting transfers between devices, halos(): up = lax.ppermute(state[CELLS - HALO:], TILE, [(i, i + 1) for i in links])  4.79 us
    all_to_all x1, starting transfers between devices, step(): lax.all_to_all(teacher.reshape(MEMBERS, BLOCK, D), MEMBER, split_axis=0,...  4.36 us
  transfers between devices with their start and end apart: 7, of which 3 were waited for; matrix products, arithmetic and copies ran while one was open for 0% of the time, Pallas kernels for 6%

profile of v4, /device:TPU:1, one launch (start us, length us, event | category | flops | bytes accessed | tf_op | source)
XLA Modules:
  0.0 107.9 jit_solution(1165066904938361196)
XLA Ops:
  0.7 2.0 %join.1 = bf16[512,640]{1,0:T(8,128)(2,1)S(1)} custom-call(bf16[512,512]{1,0:T(8,128)(2,1)} %bitcast.13, bf16[512,128]{1,0:T(8,128)(2,1)} %bitcast.21), custom_call_target="tpu_custom_call" | custom-call | tf_op jit(solution)/shard_map/join/pallas_call | solution.py:333
  2.6 0.9 copy-done.3
  3.5 10.4 %all-to-all-start = ((bf16[8,64,640]{2,1,0:T(8,128)(2,1)}), bf16[8,64,640]{2,1,0:T(8,128)(2,1)S(1)}, u32[]{:S(2)}, u32[]{:S(2)}) async-start(bf16[8,64,640]{2,1,0:T(8,128)(2,1)} %bitcast.17), calls=%async_computation | async-start | bytes 1310720 | tf_op jit(solution)/shard_map/all_to_all | solution.py:346
  13.9 0.7 collective-permute-start.3
  14.6 1.3 %collective-permute-start.2 = (bf16[64,512]{1,0:T(8,128)(2,1)S(1)}, bf16[64,512]{1,0:T(8,128)(2,1)S(1)}, u32[]{:S(2)}, u32[]{:S(2)}) collective-permute-start(bf16[64,512]{1,0:T(8,128)(2,1)S(1)} %get-tuple-element.25), channel_id=1, source_target_pairs={{1,0},{2,1},{3,2},{4,3},{5,4},{6,5},{7,6},{8,7},{9,8},{10,9},{11,1... | collective-permute-start | bytes 196616 | tf_op jit(solution)/shard_map/ppermute | solution.py:307
  15.9 0.8 collective-permute-start.1
  16.7 4.0 %collective-permute-start = (bf16[64,512]{1,0:T(8,128)(2,1)S(1)}, bf16[64,512]{1,0:T(8,128)(2,1)S(1)}, u32[]{:S(2)}, u32[]{:S(2)}) collective-permute-start(bf16[64,512]{1,0:T(8,128)(2,1)S(1)} %get-tuple-element.26), channel_id=1, source_target_pairs={{0,1},{1,2},{2,3},{3,4},{4,5},{5,6},{6,7},{7,8},{8,9},{9,10},{10,1... | collective-permute-start | bytes 196616 | tf_op jit(solution)/shard_map/ppermute | solution.py:306
  20.7 3.5 %middle.1.partly = bf16[512,512]{1,0:T(8,128)(2,1)} custom-call(bf16[512,512]{1,0:T(8,128)(2,1)S(1)} %bitcast.14, s32[8,512]{1,0:T(8,128)S(1)} %copy-done.11, bf16[512,512]{1,0:T(8,128)(2,1)} %msg.1, bf16[512,1024]{1,0:T(8,128)(2,1)S(1)} %copy-done.1, bf16[1024,512]{1,0:T(8,128)(2,1)S(1)} %copy-done.2), custom_call_target="tpu_custom_call" | custom-call | tf_op jit(solution)/shard_map/middle/pallas_call | solution.py:379
  24.3 1.9 %edges.1 = bf16[512,512]{1,0:T(8,128)(2,1)} custom-call(bf16[64,512]{1,0:T(8,128)(2,1)S(1)} %collective-permute-done.top, bf16[64,512]{1,0:T(8,128)(2,1)S(1)} %collective-permute-done.1.top_far, bf16[512,512]{1,0:T(8,128)(2,1)S(1)} %bitcast.15, bf16[64,512]{1,0:T(8,128)(2,1)S(1)} %collective-permute-done.2.bottom, ...), custom_call_target="tpu_custom_call", output_to_operand_aliasing={{}: (9, {})} | custom-call | tf_op jit(solution)/shard_map/edges/pallas_call | solution.py:380
  26.2 4.9 %all-to-all-done = bf16[8,64,640]{2,1,0:T(8,128)(2,1)S(1)} async-done(((bf16[8,64,640]{2,1,0:T(8,128)(2,1)}), bf16[8,64,640]{2,1,0:T(8,128)(2,1)S(1)}, u32[]{:S(2)}, u32[]{:S(2)}) %all-to-all-start) | async-done | bytes 655392 | tf_op jit(solution)/shard_map/all_to_all | solution.py:346
  31.1 4.4 %all-to-all-start.1 = ((bf16[8,64,512]{2,1,0:T(8,128)(2,1)}), bf16[8,64,512]{2,1,0:T(8,128)(2,1)S(1)}, u32[]{:S(2)}, u32[]{:S(2)}) async-start(bf16[8,64,512]{2,1,0:T(8,128)(2,1)} %bitcast.19), calls=%async_computation.1 | async-start | bytes 1048576 | tf_op jit(solution)/shard_map/all_to_all | solution.py:392
  36.2 1.1 %student.1 = (bf16[512,512]{1,0:T(8,128)(2,1)S(1)}, bf16[512,512]{1,0:T(8,128)(2,1)S(1)}, f32[512,512]{1,0:T(8,128)S(1)}, bf16[640,512]{1,0:T(8,128)(2,1)S(1)}) custom-call(bf16[512,640]{1,0:T(8,128)(2,1)S(1)} %bitcast.16, bf16[512,512]{1,0:T(8,128)(2,1)S(1)} %copy-done.8, bf16[128,512]{1,0:T(8,128)(2,1)S(1)} %copy-done.10, bf16[512,512]{1,0:T(8,128)(2,1)S(1)} %copy-done.5), custom_call_target="tpu_custom_call" | custom-call | tf_op jit(solution)/shard_map/student/pallas_call | solution.py:409
  37.3 1.0 copy-done.6
  38.3 0.9 copy-done.7
  39.2 0.8 copy-done.9
  40.0 9.9 %all-to-all-done.1.teacher = bf16[8,64,512]{2,1,0:T(8,128)(2,1)S(1)} async-done(((bf16[8,64,512]{2,1,0:T(8,128)(2,1)}), bf16[8,64,512]{2,1,0:T(8,128)(2,1)S(1)}, u32[]{:S(2)}, u32[]{:S(2)}) %all-to-all-start.1) | async-done | bytes 524320 | tf_op jit(solution)/shard_map/all_to_all | solution.py:392
  49.8 5.5 %score.1 = (bf16[32,2,40,128]{3,2,1,0:T(8,128)(2,1)S(1)}, bf16[32,2,40,128]{3,2,1,0:T(8,128)(2,1)S(1)}) custom-call(bf16[8,64,512]{2,1,0:T(8,128)(2,1)S(1)} %bitcast.18, bf16[8,64,512]{2,1,0:T(8,128)(2,1)S(1)} %all-to-all-done.1.teacher, bf16[640,512]{1,0:T(8,128)(2,1)} %copy-done.7, bf16[512,512]{1,0:T(8,128)(2,1)} %copy-done.9, f32[512,512]{1,0:T(8,128)} %copy-done.6, ...), custom_call_target="tpu_custom_call" | custom-call | tf_op jit(solution)/shard_map/score/pallas_call | solution.py:411
  55.4 2.9 %collective-permute-start.4 = (bf16[32,2,40,128]{3,2,1,0:T(8,128)(2,1)S(1)}, bf16[32,2,40,128]{3,2,1,0:T(8,128)(2,1)S(1)}, u32[]{:S(2)}, u32[]{:S(2)}) collective-permute-start(bf16[32,2,40,128]{3,2,1,0:T(8,128)(2,1)S(1)} %get-tuple-element.20), channel_id=1, source_target_pairs={{0,64},{64,0},{1,65},{65,1},{2,66},{66,2},{3,67},{67,3},{4,68},{68... | collective-permute-start | bytes 1966088 | tf_op jit(solution)/shard_map/ppermute | solution.py:437
  58.2 1.7 %collective-permute-done.4 = bf16[32,2,40,128]{3,2,1,0:T(8,128)(2,1)S(1)} collective-permute-done((bf16[32,2,40,128]{3,2,1,0:T(8,128)(2,1)S(1)}, bf16[32,2,40,128]{3,2,1,0:T(8,128)(2,1)S(1)}, u32[]{:S(2)}, u32[]{:S(2)}) %collective-permute-start.4) | collective-permute-done | bytes 655392 | tf_op jit(solution)/shard_map/ppermute | solution.py:437
  59.9 0.2 add_convert_fusion
  60.1 30.2 %all_to_all.20.arrived = bf16[32,2,40,128]{3,2,1,0:T(8,128)(2,1)S(1)} all-to-all(bf16[32,2,40,128]{3,2,1,0:T(8,128)(2,1)S(1)} %add_convert_fusion), channel_id=1, replica_groups=mesh['member_0'=4,'core'=2,'tile_0'=2,'tile_1'=4,'tile_2'=8] {'tile_1','..., dimensions={0} | all-to-all | bytes 1310720 | tf_op jit(solution)/shard_map/all_to_all | solution.py:439
  90.3 0.2 fold.1
  90.5 16.7 %all_to_all.21.arrived = bf16[16,40,128]{2,1,0:T(8,128)(2,1)S(1)} all-to-all(bf16[16,40,128]{2,1,0:T(8,128)(2,1)S(1)} %fold.1), channel_id=1, replica_groups=mesh['member_0'=4,'core'=2,'tile_0'=2,'tile_1'=4,'tile_2'=8] {'tile_0','..., dimensions={0} | all-to-all | bytes 327680 | tf_op jit(solution)/shard_map/all_to_all | solution.py:448
  107.3 0.6 last.1
  (26 shorter events, 0.1 us)
Async XLA Ops:
  0.6 13.3 %copy-start = (bf16[1,512,512]{2,1,0:T(8,128)(2,1)S(1)}, bf16[1,512,512]{2,1,0:T(8,128)(2,1)}, u32[]{:S(2)}) copy-start(bf16[1,512,512]{2,1,0:T(8,128)(2,1)} %param.10) | copy-start | bytes 1572868
  0.6 20.1 %copy-start.2 = (bf16[1024,512]{1,0:T(8,128)(2,1)S(1)}, bf16[1024,512]{1,0:T(8,128)(2,1)}, u32[]{:S(2)}) copy-start(bf16[1024,512]{1,0:T(8,128)(2,1)} %down.3) | copy-start | bytes 3145732
  2.6 0.9 copy-start.3
  3.5 17.2 %copy-start.1 = (bf16[512,1024]{1,0:T(8,128)(2,1)S(1)}, bf16[512,1024]{1,0:T(8,128)(2,1)}, u32[]{:S(2)}) copy-start(bf16[512,1024]{1,0:T(8,128)(2,1)} %up.3) | copy-start | bytes 3145732
  3.5 17.2 %copy-start.11 = (s32[8,512]{1,0:T(8,128)S(1)}, s32[8,512]{1,0:T(8,128)}, u32[]{:S(2)}) copy-start(s32[8,512]{1,0:T(8,128)} %near.3) | copy-start | bytes 49156
  3.5 27.6 %all-to-all-start = ((bf16[8,64,640]{2,1,0:T(8,128)(2,1)}), bf16[8,64,640]{2,1,0:T(8,128)(2,1)S(1)}, u32[]{:S(2)}, u32[]{:S(2)}) async-start(bf16[8,64,640]{2,1,0:T(8,128)(2,1)} %bitcast.17), calls=%async_computation | async-start | bytes 1310720 | tf_op jit(solution)/shard_map/all_to_all | solution.py:346
  13.9 10.3 %collective-permute-start.3 = (bf16[64,512]{1,0:T(8,128)(2,1)S(1)}, bf16[64,512]{1,0:T(8,128)(2,1)S(1)}, u32[]{:S(2)}, u32[]{:S(2)}) collective-permute-start(bf16[64,512]{1,0:T(8,128)(2,1)S(1)} %get-tuple-element.25), channel_id=1, source_target_pairs={{32,31},{96,95},{160,159},{224,223},{288,287},{352,351},{416,415},... | collective-permute-start | bytes 196616 | tf_op jit(solution)/shard_map/ppermute | solution.py:307
  14.6 9.7 %collective-permute-start.2 = (bf16[64,512]{1,0:T(8,128)(2,1)S(1)}, bf16[64,512]{1,0:T(8,128)(2,1)S(1)}, u32[]{:S(2)}, u32[]{:S(2)}) collective-permute-start(bf16[64,512]{1,0:T(8,128)(2,1)S(1)} %get-tuple-element.25), channel_id=1, source_target_pairs={{1,0},{2,1},{3,2},{4,3},{5,4},{6,5},{7,6},{8,7},{9,8},{10,9},{11,1... | collective-permute-start | bytes 196616 | tf_op jit(solution)/shard_map/ppermute | solution.py:307
  15.9 8.4 %copy-start.4 = (bf16[512,512]{1,0:T(8,128)(2,1)S(1)}, bf16[512,512]{1,0:T(8,128)(2,1)}, u32[]{:S(2)}) copy-start(bf16[512,512]{1,0:T(8,128)(2,1)} %msg.1) | copy-start | bytes 1572868
  15.9 8.4 %collective-permute-start.1 = (bf16[64,512]{1,0:T(8,128)(2,1)S(1)}, bf16[64,512]{1,0:T(8,128)(2,1)S(1)}, u32[]{:S(2)}, u32[]{:S(2)}) collective-permute-start(bf16[64,512]{1,0:T(8,128)(2,1)S(1)} %get-tuple-element.26), channel_id=1, source_target_pairs={{31,32},{95,96},{159,160},{223,224},{287,288},{351,352},{415,416},... | collective-permute-start | bytes 196616 | tf_op jit(solution)/shard_map/ppermute | solution.py:306
  16.7 7.6 %collective-permute-start = (bf16[64,512]{1,0:T(8,128)(2,1)S(1)}, bf16[64,512]{1,0:T(8,128)(2,1)S(1)}, u32[]{:S(2)}, u32[]{:S(2)}) collective-permute-start(bf16[64,512]{1,0:T(8,128)(2,1)S(1)} %get-tuple-element.26), channel_id=1, source_target_pairs={{0,1},{1,2},{2,3},{3,4},{4,5},{5,6},{6,7},{7,8},{8,9},{9,10},{10,1... | collective-permute-start | bytes 196616 | tf_op jit(solution)/shard_map/ppermute | solution.py:306
  24.3 11.9 %copy-start.10 = (bf16[128,512]{1,0:T(8,128)(2,1)S(1)}, bf16[128,512]{1,0:T(8,128)(2,1)}, u32[]{:S(2)}) copy-start(bf16[128,512]{1,0:T(8,128)(2,1)} %w_noise.1) | copy-start | bytes 393220
  26.2 10.0 %copy-start.5 = (bf16[512,512]{1,0:T(8,128)(2,1)S(1)}, bf16[512,512]{1,0:T(8,128)(2,1)}, u32[]{:S(2)}) copy-start(bf16[512,512]{1,0:T(8,128)(2,1)} %w_out_at.1) | copy-start | bytes 1572868
  26.2 10.0 %copy-start.8 = (bf16[512,512]{1,0:T(8,128)(2,1)S(1)}, bf16[512,512]{1,0:T(8,128)(2,1)}, u32[]{:S(2)}) copy-start(bf16[512,512]{1,0:T(8,128)(2,1)} %w_in.1) | copy-start | bytes 1572868
  31.1 18.8 %all-to-all-start.1 = ((bf16[8,64,512]{2,1,0:T(8,128)(2,1)}), bf16[8,64,512]{2,1,0:T(8,128)(2,1)S(1)}, u32[]{:S(2)}, u32[]{:S(2)}) async-start(bf16[8,64,512]{2,1,0:T(8,128)(2,1)} %bitcast.19), calls=%async_computation.1 | async-start | bytes 1048576 | tf_op jit(solution)/shard_map/all_to_all | solution.py:392
  37.3 1.0 copy-start.6
  38.3 0.9 copy-start.7
  39.2 0.8 copy-start.9
  55.4 4.6 %collective-permute-start.4 = (bf16[32,2,40,128]{3,2,1,0:T(8,128)(2,1)S(1)}, bf16[32,2,40,128]{3,2,1,0:T(8,128)(2,1)S(1)}, u32[]{:S(2)}, u32[]{:S(2)}) collective-permute-start(bf16[32,2,40,128]{3,2,1,0:T(8,128)(2,1)S(1)} %get-tuple-element.20), channel_id=1, source_target_pairs={{0,64},{64,0},{1,65},{65,1},{2,66},{66,2},{3,67},{67,3},{4,68},{68... | collective-permute-start | bytes 1966088 | tf_op jit(solution)/shard_map/ppermute | solution.py:437

commit v5 on v4

--- a/solution.py
+++ b/solution.py
@@ -83,10 +83,15 @@
         copy.wait()
 
 
-def edges_kernel(top, top_far, state, bottom, bottom_far, near, msg, up, down, partly, out, held, sem):
+def edges_kernel(odd_swap, even_swap, state, near, msg, up, down, partly, odd, out, held, sem):
     reach = 3 * HALO
-    above = jnp.concatenate([top[...] + top_far[...], state[: 2 * HALO]], axis=0)
-    below = jnp.concatenate([state[CELLS - 2 * HALO :], bottom[...] + bottom_far[...]], axis=0)
+    is_odd = jnp.full((HALO, D), odd[0], jnp.int32) == 1
+    after_odd = odd_swap[...].astype(F32)
+    after_even = even_swap[...].astype(F32)
+    top = jnp.where(is_odd, after_even, after_odd).astype(BF16)
+    bottom = jnp.where(is_odd, after_odd, after_even).astype(BF16)
+    above = jnp.concatenate([top, state[: 2 * HALO]], axis=0)
+    below = jnp.concatenate([state[CELLS - 2 * HALO :], bottom], axis=0)
     first = near[:, : 2 * HALO].T[:HALO]
     last = near[:, CELLS - 2 * HALO :].T[HALO:]
     gathered = jnp.concatenate(
@@ -302,10 +307,11 @@
             region_loss[...] = loss * (1.0 / (CELLS_ALL // REGIONS * D))
 
 
-def halos(state, links):
-    up = lax.ppermute(state[CELLS - HALO :], TILE, [(i, i + 1) for i in links])
-    down = lax.ppermute(state[:HALO], TILE, [(i + 1, i) for i in links])
-    return up, down
+def exchanged(state, odd, first):
+    ahead = odd if first else 1 - odd
+    edge = lax.dynamic_slice_in_dim(state, ahead * (CELLS - HALO), HALO, axis=0)
+    pairs = [(i, i + 1) for i in range(first, TILES - 1, 2)]
+    return lax.ppermute(edge, TILE, pairs + [(b, a) for a, b in pairs])
 
 
 HBM = pl.BlockSpec(memory_space=pltpu.HBM)
@@ -340,7 +346,7 @@
             pltpu.SemaphoreType.DMA((2 * JOINS,)),
             pltpu.SemaphoreType.DMA((JOINS,)),
         ],
-        compiler_params=PARAMS,
+        compiler_params=pltpu.CompilerParams(vmem_limit_bytes=60 * 1024 * 1024),
         name="join",
     )(in_hbm(state), in_hbm(noise[0]))
     mine = lax.all_to_all(
@@ -350,8 +356,9 @@
         concat_axis=0,
         tiled=True,
     )
-    top_far, bottom_far = halos(state, [XY - 1])
-    top, bottom = halos(state, [i for i in range(TILES - 1) if i != XY - 1])
+    odd = lax.axis_index("tile_2") % 2
+    far = exchanged(state, odd, 1)
+    near = exchanged(state, odd, 0)
     middle = pl.pallas_call(
         middle_kernel,
         out_shape=jax.ShapeDtypeStruct((CELLS, D), BF16),
@@ -369,25 +376,24 @@
     edges = pl.pallas_call(
         edges_kernel,
         out_shape=jax.ShapeDtypeStruct((CELLS, D), BF16),
-        in_specs=[VMEM] * 9 + [HBM],
+        in_specs=[VMEM] * 7 + [HBM, pl.BlockSpec(memory_space=pltpu.SMEM)],
         out_specs=HBM,
-        input_output_aliases={9: 0},
+        input_output_aliases={7: 0},
         scratch_shapes=[pltpu.VMEM((2 * HALO, D), BF16), pltpu.SemaphoreType.DMA((2,))],
         compiler_params=PARAMS,
         name="edges",
     )
     partly = middle(state, neighbours, in_hbm(msg_weight), up_weight, down_weight)
     teacher = edges(
-        top,
-        top_far,
+        far,
+        near,
         state,
-        bottom,
-        bottom_far,
         neighbours,
         msg_weight,
         up_weight,
         down_weight,
         partly,
+        odd.astype(jnp.int32).reshape(1),
     )
     every = lax.all_to_all(
         teacher.reshape(MEMBERS, BLOCK, D), MEMBER, split_axis=0, concat_axis=0, tiled=True

time: 108 us -> 106 us (0.981)
  starting transfers between devices: 24.4 us -> 20.4 us
  waiting for transfers between devices: 16.5 us -> 20.5 us
  blocking collectives: 46.9 us -> 45.4 us
    all_to_all x1, blocking collectives: 30.2 us -> 26 us  [step(): lax.all_to_all(half, ('tile_1', 'tile_2'), split_axis=0, concat_axis=0, t...]
    all_to_all x1, waiting for transfers between devices: 4.9 us -> 8.96 us  [step(): lax.all_to_all(both.reshape(MEMBERS, BLOCK, D + NOISE), MEMBER, split_axi...]
    ppermute x4 -> x2, starting transfers between devices: 6.74 us -> 2.72 us  [exchanged(): return lax.ppermute(edge, TILE, pairs + [(b, a) for a, b in pairs])]
    all_to_all x1, blocking collectives: 16.7 us -> 19.4 us  [step(): lax.all_to_all(copies, ('tile_0', 'member_0', 'core'), split_axis=0, conc...]
    unnamed x24 -> x22, local copies, waits for them, and re-layouts: 3.54 us -> 2.69 us
  transfers between devices with their start and end apart: 7 -> 5, of which waited for: 3 -> 3; matrix products, arithmetic and copies ran while one was open for 0% -> 0% of each run, Pallas kernels for 6% -> 6%
where the time goes in v5:
time: 106 us
  blocking collectives  45.4 us (43%)
  waiting for transfers between devices  20.5 us (19%)
  starting transfers between devices  20.4 us (19%)
  Pallas kernels  14.9 us (14%)
  local copies, waits for them, and re-layouts  2.7 us (3%)
  between operations  1.48 us (1%)
    all_to_all x1, blocking collectives, step(): lax.all_to_all(half, ('tile_1', 'tile_2'), split_axis=0, concat_axis=0, t...  26 us
    all_to_all x1, blocking collectives, step(): lax.all_to_all(copies, ('tile_0', 'member_0', 'core'), split_axis=0, conc...  19.4 us
    all_to_all x1, starting transfers between devices, step(): lax.all_to_all(both.reshape(MEMBERS, BLOCK, D + NOISE), MEMBER, split_axi...  10.4 us
    all_to_all x1, waiting for transfers between devices, step(): lax.all_to_all(teacher.reshape(MEMBERS, BLOCK, D), MEMBER, split_axis=0,...  9.86 us
    all_to_all x1, waiting for transfers between devices, step(): lax.all_to_all(both.reshape(MEMBERS, BLOCK, D + NOISE), MEMBER, split_axi...  8.96 us
    pallas_call x1, Pallas kernels, step(): pl.pallas_call(score_kernel, out_shape=[jax.ShapeDtypeStruct((XY, 2, SHAR...  5.5 us
    all_to_all x1, starting transfers between devices, step(): lax.all_to_all(teacher.reshape(MEMBERS, BLOCK, D), MEMBER, split_axis=0,...  4.36 us
    pallas_call x1, Pallas kernels, step(): middle(state, neighbours, in_hbm(msg_weight), up_weight, down_weight)  3.52 us
  transfers between devices with their start and end apart: 5, of which 3 were waited for; matrix products, arithmetic and copies ran while one was open for 0% of the time, Pallas kernels for 6%

profile of v5, /device:TPU:1, one launch (start us, length us, event | category | flops | bytes accessed | tf_op | source)
XLA Modules:
  0.0 105.6 jit_solution(8270342495705186827)
XLA Ops:
  0.7 2.0 %join.1 = bf16[512,640]{1,0:T(8,128)(2,1)} custom-call(bf16[512,512]{1,0:T(8,128)(2,1)} %bitcast.14, bf16[512,128]{1,0:T(8,128)(2,1)} %bitcast.22), custom_call_target="tpu_custom_call" | custom-call | tf_op jit(solution)/shard_map/join/pallas_call | solution.py:339
  2.7 10.4 %all-to-all-start = ((bf16[8,64,640]{2,1,0:T(8,128)(2,1)}), bf16[8,64,640]{2,1,0:T(8,128)(2,1)S(1)}, u32[]{:S(2)}, u32[]{:S(2)}) async-start(bf16[8,64,640]{2,1,0:T(8,128)(2,1)} %bitcast.21), calls=%async_computation | async-start | bytes 1310720 | tf_op jit(solution)/shard_map/all_to_all | solution.py:352
  13.2 1.9 %collective-permute-start.1 = (bf16[64,512]{1,0:T(8,128)(2,1)S(1)}, bf16[64,512]{1,0:T(8,128)(2,1)S(1)}, u32[]{:S(2)}, u32[]{:S(2)}) collective-permute-start(bf16[64,512]{1,0:T(8,128)(2,1)S(1)} %get-tuple-element.25), channel_id=1, source_target_pairs={{0,1},{2,3},{4,5},{6,7},{8,9},{10,11},{12,13},{14,15},{16,17},{18,... | collective-permute-start | bytes 196616 | tf_op jit(solution)/shard_map/ppermute | solution.py:314
  15.1 0.0 copy-start.3
  15.1 0.8 collective-permute-start
  15.9 3.5 %middle.1.partly = bf16[512,512]{1,0:T(8,128)(2,1)} custom-call(bf16[512,512]{1,0:T(8,128)(2,1)S(1)} %bitcast.15, s32[8,512]{1,0:T(8,128)S(1)} %copy-done.10, bf16[512,512]{1,0:T(8,128)(2,1)} %msg.1, bf16[512,1024]{1,0:T(8,128)(2,1)S(1)} %copy-done.1, bf16[1024,512]{1,0:T(8,128)(2,1)S(1)} %copy-done.2), custom_call_target="tpu_custom_call" | custom-call | tf_op jit(solution)/shard_map/middle/pallas_call | solution.py:386
  19.5 1.8 %edges.1 = bf16[512,512]{1,0:T(8,128)(2,1)} custom-call(bf16[64,512]{1,0:T(8,128)(2,1)S(1)} %collective-permute-done.odd_swap, bf16[64,512]{1,0:T(8,128)(2,1)S(1)} %collective-permute-done.1.even_swap, bf16[512,512]{1,0:T(8,128)(2,1)S(1)} %bitcast.16, s32[8,512]{1,0:T(8,128)S(1)} %copy-done.10, ...), custom_call_target="tpu_custom_call", output_to_operand_aliasing={{}: (7, {})} | custom-call | tf_op jit(solution)/shard_map/edges/pallas_call | solution.py:387
  21.4 0.0 copy-start.4
  21.4 9.0 %all-to-all-done = bf16[8,64,640]{2,1,0:T(8,128)(2,1)S(1)} async-done(((bf16[8,64,640]{2,1,0:T(8,128)(2,1)}), bf16[8,64,640]{2,1,0:T(8,128)(2,1)S(1)}, u32[]{:S(2)}, u32[]{:S(2)}) %all-to-all-start) | async-done | bytes 655392 | tf_op jit(solution)/shard_map/all_to_all | solution.py:352
  30.3 4.4 %all-to-all-start.1 = ((bf16[8,64,512]{2,1,0:T(8,128)(2,1)}), bf16[8,64,512]{2,1,0:T(8,128)(2,1)S(1)}, u32[]{:S(2)}, u32[]{:S(2)}) async-start(bf16[8,64,512]{2,1,0:T(8,128)(2,1)} %bitcast.19), calls=%async_computation.1 | async-start | bytes 1048576 | tf_op jit(solution)/shard_map/all_to_all | solution.py:398
  35.3 0.1 pad_add_fusion.place
  35.4 1.1 %student.1 = (bf16[512,512]{1,0:T(8,128)(2,1)S(1)}, bf16[512,512]{1,0:T(8,128)(2,1)S(1)}, f32[512,512]{1,0:T(8,128)S(1)}, bf16[640,512]{1,0:T(8,128)(2,1)S(1)}) custom-call(bf16[512,640]{1,0:T(8,128)(2,1)S(1)} %bitcast.17, bf16[512,512]{1,0:T(8,128)(2,1)S(1)} %copy-done.7, bf16[128,512]{1,0:T(8,128)(2,1)S(1)} %copy-done.9, bf16[512,512]{1,0:T(8,128)(2,1)S(1)} %copy-done.4), custom_call_target="tpu_custom_call" | custom-call | tf_op jit(solution)/shard_map/student/pallas_call | solution.py:415
  36.6 1.0 copy-done.5
  37.6 0.9 copy-done.6
  38.4 0.8 copy-done.8
  39.2 9.9 %all-to-all-done.1.teacher = bf16[8,64,512]{2,1,0:T(8,128)(2,1)S(1)} async-done(((bf16[8,64,512]{2,1,0:T(8,128)(2,1)}), bf16[8,64,512]{2,1,0:T(8,128)(2,1)S(1)}, u32[]{:S(2)}, u32[]{:S(2)}) %all-to-all-start.1) | async-done | bytes 524320 | tf_op jit(solution)/shard_map/all_to_all | solution.py:398
  49.1 5.5 %score.1 = (bf16[32,2,40,128]{3,2,1,0:T(8,128)(2,1)S(1)}, bf16[32,2,40,128]{3,2,1,0:T(8,128)(2,1)S(1)}) custom-call(bf16[8,64,512]{2,1,0:T(8,128)(2,1)S(1)} %bitcast.18, bf16[8,64,512]{2,1,0:T(8,128)(2,1)S(1)} %all-to-all-done.1.teacher, bf16[640,512]{1,0:T(8,128)(2,1)} %copy-done.6, bf16[512,512]{1,0:T(8,128)(2,1)} %copy-done.8, f32[512,512]{1,0:T(8,128)} %copy-done.5, ...), custom_call_target="tpu_custom_call" | custom-call | tf_op jit(solution)/shard_map/score/pallas_call | solution.py:417
  54.6 2.9 %collective-permute-start.2 = (bf16[32,2,40,128]{3,2,1,0:T(8,128)(2,1)S(1)}, bf16[32,2,40,128]{3,2,1,0:T(8,128)(2,1)S(1)}, u32[]{:S(2)}, u32[]{:S(2)}) collective-permute-start(bf16[32,2,40,128]{3,2,1,0:T(8,128)(2,1)S(1)} %get-tuple-element.20), channel_id=1, source_target_pairs={{0,64},{64,0},{1,65},{65,1},{2,66},{66,2},{3,67},{67,3},{4,68},{68... | collective-permute-start | bytes 1966088 | tf_op jit(solution)/shard_map/ppermute | solution.py:443
  57.5 1.7 %collective-permute-done.2 = bf16[32,2,40,128]{3,2,1,0:T(8,128)(2,1)S(1)} collective-permute-done((bf16[32,2,40,128]{3,2,1,0:T(8,128)(2,1)S(1)}, bf16[32,2,40,128]{3,2,1,0:T(8,128)(2,1)S(1)}, u32[]{:S(2)}, u32[]{:S(2)}) %collective-permute-start.2) | collective-permute-done | bytes 655392 | tf_op jit(solution)/shard_map/ppermute | solution.py:443
  59.2 0.2 add_convert_fusion
  59.4 26.0 %all_to_all.20.arrived = bf16[32,2,40,128]{3,2,1,0:T(8,128)(2,1)S(1)} all-to-all(bf16[32,2,40,128]{3,2,1,0:T(8,128)(2,1)S(1)} %add_convert_fusion), channel_id=1, replica_groups=mesh['member_0'=4,'core'=2,'tile_0'=2,'tile_1'=4,'tile_2'=8] {'tile_1','..., dimensions={0} | all-to-all | bytes 1310720 | tf_op jit(solution)/shard_map/all_to_all | solution.py:445
  85.4 0.2 fold.1
  85.6 19.4 %all_to_all.21.arrived = bf16[16,40,128]{2,1,0:T(8,128)(2,1)S(1)} all-to-all(bf16[16,40,128]{2,1,0:T(8,128)(2,1)S(1)} %fold.1), channel_id=1, replica_groups=mesh['member_0'=4,'core'=2,'tile_0'=2,'tile_1'=4,'tile_2'=8] {'tile_0','..., dimensions={0} | all-to-all | bytes 327680 | tf_op jit(solution)/shard_map/all_to_all | solution.py:454
  105.0 0.6 last.1
  (20 shorter events, 0.1 us)
Async XLA Ops:
  0.6 12.5 %copy-start = (bf16[1,512,512]{2,1,0:T(8,128)(2,1)S(1)}, bf16[1,512,512]{2,1,0:T(8,128)(2,1)}, u32[]{:S(2)}) copy-start(bf16[1,512,512]{2,1,0:T(8,128)(2,1)} %param.10) | copy-start | bytes 1572868
  0.6 15.3 %copy-start.2 = (bf16[1024,512]{1,0:T(8,128)(2,1)S(1)}, bf16[1024,512]{1,0:T(8,128)(2,1)}, u32[]{:S(2)}) copy-start(bf16[1024,512]{1,0:T(8,128)(2,1)} %down.3) | copy-start | bytes 3145732
  2.7 13.2 %copy-start.1 = (bf16[512,1024]{1,0:T(8,128)(2,1)S(1)}, bf16[512,1024]{1,0:T(8,128)(2,1)}, u32[]{:S(2)}) copy-start(bf16[512,1024]{1,0:T(8,128)(2,1)} %up.3) | copy-start | bytes 3145732
  2.7 13.2 %copy-start.10 = (s32[8,512]{1,0:T(8,128)S(1)}, s32[8,512]{1,0:T(8,128)}, u32[]{:S(2)}) copy-start(s32[8,512]{1,0:T(8,128)} %near.3) | copy-start | bytes 49156
  2.7 27.6 %all-to-all-start = ((bf16[8,64,640]{2,1,0:T(8,128)(2,1)}), bf16[8,64,640]{2,1,0:T(8,128)(2,1)S(1)}, u32[]{:S(2)}, u32[]{:S(2)}) async-start(bf16[8,64,640]{2,1,0:T(8,128)(2,1)} %bitcast.21), calls=%async_computation | async-start | bytes 1310720 | tf_op jit(solution)/shard_map/all_to_all | solution.py:352
  13.2 6.3 %collective-permute-start.1 = (bf16[64,512]{1,0:T(8,128)(2,1)S(1)}, bf16[64,512]{1,0:T(8,128)(2,1)S(1)}, u32[]{:S(2)}, u32[]{:S(2)}) collective-permute-start(bf16[64,512]{1,0:T(8,128)(2,1)S(1)} %get-tuple-element.25), channel_id=1, source_target_pairs={{0,1},{2,3},{4,5},{6,7},{8,9},{10,11},{12,13},{14,15},{16,17},{18,... | collective-permute-start | bytes 196616 | tf_op jit(solution)/shard_map/ppermute | solution.py:314
  15.1 4.4 %copy-start.3 = (bf16[512,512]{1,0:T(8,128)(2,1)S(1)}, bf16[512,512]{1,0:T(8,128)(2,1)}, u32[]{:S(2)}) copy-start(bf16[512,512]{1,0:T(8,128)(2,1)} %msg.1) | copy-start | bytes 1572868
  15.1 4.4 %collective-permute-start = (bf16[64,512]{1,0:T(8,128)(2,1)S(1)}, bf16[64,512]{1,0:T(8,128)(2,1)S(1)}, u32[]{:S(2)}, u32[]{:S(2)}) collective-permute-start(bf16[64,512]{1,0:T(8,128)(2,1)S(1)} %get-tuple-element.26), channel_id=1, source_target_pairs={{1,2},{3,4},{5,6},{7,8},{9,10},{11,12},{13,14},{15,16},{17,18},{19... | collective-permute-start | bytes 196616 | tf_op jit(solution)/shard_map/ppermute | solution.py:314
  19.5 15.9 %copy-start.9 = (bf16[128,512]{1,0:T(8,128)(2,1)S(1)}, bf16[128,512]{1,0:T(8,128)(2,1)}, u32[]{:S(2)}) copy-start(bf16[128,512]{1,0:T(8,128)(2,1)} %w_noise.1) | copy-start | bytes 393220
  21.4 14.1 %copy-start.4 = (bf16[512,512]{1,0:T(8,128)(2,1)S(1)}, bf16[512,512]{1,0:T(8,128)(2,1)}, u32[]{:S(2)}) copy-start(bf16[512,512]{1,0:T(8,128)(2,1)} %w_out_at.1) | copy-start | bytes 1572868
  21.4 14.1 %copy-start.7 = (bf16[512,512]{1,0:T(8,128)(2,1)S(1)}, bf16[512,512]{1,0:T(8,128)(2,1)}, u32[]{:S(2)}) copy-start(bf16[512,512]{1,0:T(8,128)(2,1)} %w_in.1) | copy-start | bytes 1572868
  30.3 18.8 %all-to-all-start.1 = ((bf16[8,64,512]{2,1,0:T(8,128)(2,1)}), bf16[8,64,512]{2,1,0:T(8,128)(2,1)S(1)}, u32[]{:S(2)}, u32[]{:S(2)}) async-start(bf16[8,64,512]{2,1,0:T(8,128)(2,1)} %bitcast.19), calls=%async_computation.1 | async-start | bytes 1048576 | tf_op jit(solution)/shard_map/all_to_all | solution.py:398
  36.6 1.0 copy-start.5
  37.6 0.9 copy-start.6
  38.4 0.8 copy-start.8
  54.6 4.6 %collective-permute-start.2 = (bf16[32,2,40,128]{3,2,1,0:T(8,128)(2,1)S(1)}, bf16[32,2,40,128]{3,2,1,0:T(8,128)(2,1)S(1)}, u32[]{:S(2)}, u32[]{:S(2)}) collective-permute-start(bf16[32,2,40,128]{3,2,1,0:T(8,128)(2,1)S(1)} %get-tuple-element.20), channel_id=1, source_target_pairs={{0,64},{64,0},{1,65},{65,1},{2,66},{66,2},{3,67},{67,3},{4,68},{68... | collective-permute-start | bytes 1966088 | tf_op jit(solution)/shard_map/ppermute | solution.py:443

commit v6 on v5

--- a/solution.py
+++ b/solution.py
@@ -22,6 +22,7 @@
 HALF = D // 2
 XY = TILES // 2
 JOINS = 4
+STEP = 16
 SHARE = 40
 LOSS_ROW = 36
 
@@ -139,7 +140,9 @@
         copy.wait()
 
 
-def student_kernel(mine, w_in, w_noise, w_out, student, shidden, slope, turned):
+def student_kernel(
+    mine, w_in, w_noise, w_out, shidden, slope, turned, held, within_loss
+):
     rows = 256
     for at in range(0, CELLS, rows):
         state = mine[at : at + rows, :D]
@@ -149,16 +152,44 @@
         sig = jax.nn.sigmoid(preact)
         hid = (preact * sig).astype(BF16)
         slope[at : at + rows] = sig * (1.0 + preact * (1.0 - sig))
-        student[at : at + rows] = (
+        made = (
             state.astype(F32) + jnp.dot(hid, w_out[...], preferred_element_type=F32)
-        ).astype(BF16)
+        ).astype(BF16).astype(F32)
+        for k in range(rows // BLOCK):
+            held[0, at // BLOCK + k] = made[k * BLOCK : (k + 1) * BLOCK]
         shidden[:, at : at + rows] = hid.T
         turned[:, at : at + rows] = mine[at : at + rows].T
 
+    within_loss[...] = jnp.zeros_like(within_loss)
+
+    def body(i, carry):
+        cell = pl.multiple_of(i * STEP, STEP)
+        for lane in range(0, D, 128):
+            at = (pl.ds(cell, STEP), slice(lane, lane + 128))
+            s = [held[0, m, at[0], at[1]] for m in range(MEMBERS)]
+            g = [jnp.zeros((STEP, 128), F32) for _ in range(MEMBERS)]
+            loss = jnp.zeros((STEP, 128), F32)
+            for m in range(MEMBERS):
+                for n in range(m + 1, MEMBERS):
+                    d = s[m] - s[n]
+                    q = d * d + 0.01
+                    inv = lax.rsqrt(q)
+                    r = d * inv
+                    loss = loss + q * inv
+                    g[m] = g[m] - r
+                    g[n] = g[n] + r
+            for m in range(MEMBERS):
+                held[1, m, at[0], at[1]] = g[m]
+            within_loss[...] += loss
+        return carry
+
+    lax.fori_loop(0, BLOCK // STEP, body, 0)
+
 
 def score_kernel(
-    student,
+    held,
     teacher,
+    within_loss,
     turned_at,
     shidden_at,
     slope_at,
@@ -183,46 +214,35 @@
     ]
     for copy in copies:
         copy.start()
-    step = 16
-    wide[...] = jnp.zeros_like(wide)
+    ratio = (MEMBERS - 1) / MEMBERS
+    pairs = MEMBERS * (MEMBERS - 1)
+    scale = 1.0 / (pairs * math.sqrt(CELLS_ALL))
+    wide[...] = -within_loss[...] * (1.0 / pairs)
 
     def block(cell, lane):
-        s = [student[m, pl.ds(cell, step), lane : lane + 128].astype(F32) for m in range(MEMBERS)]
-        g = [jnp.zeros((step, 128), F32) for _ in range(MEMBERS)]
-        loss = jnp.zeros((step, 128), F32)
+        s = [held[0, m, pl.ds(cell, STEP), lane : lane + 128] for m in range(MEMBERS)]
+        g = [jnp.zeros((STEP, 128), F32) for _ in range(MEMBERS)]
+        loss = jnp.zeros((STEP, 128), F32)
         for n in range(MEMBERS):
-            t = teacher[n, pl.ds(cell, step), lane : lane + 128].astype(F32)
+            t = teacher[n, pl.ds(cell, STEP), lane : lane + 128].astype(F32)
             for m in range(MEMBERS):
                 d = s[m] - t
                 q = d * d + 0.01
                 inv = lax.rsqrt(q)
                 loss = loss + q * inv
                 g[m] = g[m] + d * inv
-        ratio = (MEMBERS - 1) / MEMBERS
-        loss = loss * ratio
-        g = [x * ratio for x in g]
         for m in range(MEMBERS):
-            for n in range(m + 1, MEMBERS):
-                d = s[m] - s[n]
-                q = d * d + 0.01
-                inv = lax.rsqrt(q)
-                r = d * inv
-                loss = loss - q * inv
-                g[m] = g[m] - r
-                g[n] = g[n] + r
-        scale = 1.0 / (MEMBERS * (MEMBERS - 1) * math.sqrt(CELLS_ALL))
-        for m in range(MEMBERS):
-            gst[m, pl.ds(cell, step), lane : lane + 128] = (g[m] * scale).astype(BF16)
-        pairs = MEMBERS * (MEMBERS - 1)
-        wide[...] += (loss - 0.1 * (pairs - pairs // 2)) * (1.0 / pairs)
+            total = g[m] * ratio + held[1, m, pl.ds(cell, STEP), lane : lane + 128]
+            gst[m, pl.ds(cell, STEP), lane : lane + 128] = (total * scale).astype(BF16)
+        wide[...] += (loss * ratio - 0.1 * (pairs - pairs // 2)) * (1.0 / pairs)
 
     def body(i, carry):
-        cell = pl.multiple_of(i * step, step)
+        cell = pl.multiple_of(i * STEP, STEP)
         for lane in range(0, D, 128):
             block(cell, lane)
         return carry
 
-    lax.fori_loop(0, BLOCK // step, body, 0)
+    lax.fori_loop(0, BLOCK // STEP, body, 0)
 
     total = jnp.sum(jnp.sum(wide[...], axis=0, keepdims=True), axis=1, keepdims=True)
     lane_ids = lax.broadcasted_iota(jnp.int32, (4, 128), 1)
@@ -402,27 +422,28 @@
     pupil = pl.pallas_call(
         student_kernel,
         out_shape=(
-            jax.ShapeDtypeStruct((CELLS, D), BF16),
             jax.ShapeDtypeStruct((H, CELLS), BF16),
             jax.ShapeDtypeStruct((CELLS, H), F32),
             jax.ShapeDtypeStruct((D + NOISE, CELLS), BF16),
+            jax.ShapeDtypeStruct((2, MEMBERS, BLOCK, D), F32),
+            jax.ShapeDtypeStruct((STEP, 128), F32),
         ),
         in_specs=[VMEM] * 4,
-        out_specs=[VMEM] * 4,
+        out_specs=[VMEM] * 5,
         compiler_params=PARAMS,
         name="student",
     )
-    student, shidden, slope, turned = pupil(mine, student_in, student_noise, student_out)
+    shidden, slope, turned, held, within_loss = pupil(mine, student_in, student_noise, student_out)
     place = jnp.stack([region_map[0], lax.axis_index("core").astype(jnp.int32)])
     send, keep = pl.pallas_call(
         score_kernel,
         out_shape=[jax.ShapeDtypeStruct((XY, 2, SHARE, 128), BF16)] * 2,
-        in_specs=[VMEM] * 2 + [HBM] * 4 + [pl.BlockSpec(memory_space=pltpu.SMEM)],
+        in_specs=[VMEM] * 3 + [HBM] * 4 + [pl.BlockSpec(memory_space=pltpu.SMEM)],
         out_specs=[VMEM] * 2,
         scratch_shapes=[
             pltpu.VMEM((MEMBERS, BLOCK, D), BF16),
             pltpu.VMEM((CELLS, D), BF16),
-            pltpu.VMEM((16, 128), F32),
+            pltpu.VMEM((STEP, 128), F32),
             pltpu.VMEM((D + NOISE, CELLS), BF16),
             pltpu.VMEM((H, CELLS), BF16),
             pltpu.VMEM((CELLS, H), F32),
@@ -432,8 +453,9 @@
         compiler_params=PARAMS,
         name="score",
     )(
-        student.reshape(MEMBERS, BLOCK, D),
+        held,
         every,
+        within_loss,
         in_hbm(turned),
         in_hbm(shidden),
         in_hbm(slope),

time: 106 us -> 106 us (level)
  waiting for transfers between devices: 20.5 us -> 18.5 us
    all_to_all x1, waiting for transfers between devices: 9.86 us -> 7.79 us  [step(): lax.all_to_all(teacher.reshape(MEMBERS, BLOCK, D), MEMBER, split_axis=0,...]
    pallas_call x1, Pallas kernels: 1.13 us -> 2.25 us  [step(): pupil(mine, student_in, student_noise, student_out)]
  transfers between devices with their start and end apart: 5 -> 5, of which waited for: 3 -> 3; matrix products, arithmetic and copies ran while one was open for 0% -> 0% of each run, Pallas kernels for 6% -> 7%
where the time goes in v6:
time: 106 us
  blocking collectives  45.4 us (43%)
  starting transfers between devices  20.9 us (20%)
  waiting for transfers between devices  18.5 us (17%)
  Pallas kernels  15.4 us (15%)
  local copies, waits for them, and re-layouts  3.75 us (4%)
  between operations  1.48 us (1%)
    all_to_all x1, blocking collectives, step(): lax.all_to_all(half, ('tile_1', 'tile_2'), split_axis=0, concat_axis=0, t...  25.4 us
    all_to_all x1, blocking collectives, step(): lax.all_to_all(copies, ('tile_0', 'member_0', 'core'), split_axis=0, conc...  20 us
    all_to_all x1, starting transfers between devices, step(): lax.all_to_all(both.reshape(MEMBERS, BLOCK, D + NOISE), MEMBER, split_axi...  10.3 us
    all_to_all x1, waiting for transfers between devices, step(): lax.all_to_all(both.reshape(MEMBERS, BLOCK, D + NOISE), MEMBER, split_axi...  8.97 us
    all_to_all x1, waiting for transfers between devices, step(): lax.all_to_all(teacher.reshape(MEMBERS, BLOCK, D), MEMBER, split_axis=0,...  7.79 us
    all_to_all x1, starting transfers between devices, step(): lax.all_to_all(teacher.reshape(MEMBERS, BLOCK, D), MEMBER, split_axis=0,...  4.98 us
    pallas_call x1, Pallas kernels, step(): pl.pallas_call(score_kernel, out_shape=[jax.ShapeDtypeStruct((XY, 2, SHAR...  4.91 us
    unnamed x22, local copies, waits for them, and re-layouts  3.74 us
  transfers between devices with their start and end apart: 5, of which 3 were waited for; matrix products, arithmetic and copies ran while one was open for 0% of the time, Pallas kernels for 7%

profile of v6, /device:TPU:1, one launch (start us, length us, event | category | flops | bytes accessed | tf_op | source)
XLA Modules:
  0.0 105.6 jit_solution(14455427917773612629)
XLA Ops:
  0.7 2.1 %join.1 = bf16[512,640]{1,0:T(8,128)(2,1)} custom-call(bf16[512,512]{1,0:T(8,128)(2,1)} %bitcast.13, bf16[512,128]{1,0:T(8,128)(2,1)} %bitcast.20), custom_call_target="tpu_custom_call" | custom-call | tf_op jit(solution)/shard_map/join/pallas_call | solution.py:359
  2.7 10.3 %all-to-all-start = ((bf16[8,64,640]{2,1,0:T(8,128)(2,1)}), bf16[8,64,640]{2,1,0:T(8,128)(2,1)S(1)}, u32[]{:S(2)}, u32[]{:S(2)}) async-start(bf16[8,64,640]{2,1,0:T(8,128)(2,1)} %bitcast.19), calls=%async_computation | async-start | bytes 1310720 | tf_op jit(solution)/shard_map/all_to_all | solution.py:372
  13.0 1.9 %collective-permute-start.1 = (bf16[64,512]{1,0:T(8,128)(2,1)S(1)}, bf16[64,512]{1,0:T(8,128)(2,1)S(1)}, u32[]{:S(2)}, u32[]{:S(2)}) collective-permute-start(bf16[64,512]{1,0:T(8,128)(2,1)S(1)} %get-tuple-element.27), channel_id=1, source_target_pairs={{0,1},{2,3},{4,5},{6,7},{8,9},{10,11},{12,13},{14,15},{16,17},{18,... | collective-permute-start | bytes 196616 | tf_op jit(solution)/shard_map/ppermute | solution.py:334
  15.0 0.8 collective-permute-start
  15.8 3.5 %middle.1.partly = bf16[512,512]{1,0:T(8,128)(2,1)} custom-call(bf16[512,512]{1,0:T(8,128)(2,1)S(1)} %bitcast.14, s32[8,512]{1,0:T(8,128)S(1)} %copy-done.10, bf16[512,512]{1,0:T(8,128)(2,1)} %msg.1, bf16[512,1024]{1,0:T(8,128)(2,1)S(1)} %copy-done.1, bf16[1024,512]{1,0:T(8,128)(2,1)S(1)} %copy-done.2), custom_call_target="tpu_custom_call" | custom-call | tf_op jit(solution)/shard_map/middle/pallas_call | solution.py:406
  19.4 0.0 copy-start.9
  19.4 1.8 %edges.1 = bf16[512,512]{1,0:T(8,128)(2,1)} custom-call(bf16[64,512]{1,0:T(8,128)(2,1)S(1)} %collective-permute-done.odd_swap, bf16[64,512]{1,0:T(8,128)(2,1)S(1)} %collective-permute-done.1.even_swap, bf16[512,512]{1,0:T(8,128)(2,1)S(1)} %bitcast.15, s32[8,512]{1,0:T(8,128)S(1)} %copy-done.10, ...), custom_call_target="tpu_custom_call", output_to_operand_aliasing={{}: (7, {})} | custom-call | tf_op jit(solution)/shard_map/edges/pallas_call | solution.py:407
  21.3 9.0 %all-to-all-done = bf16[8,64,640]{2,1,0:T(8,128)(2,1)S(1)} async-done(((bf16[8,64,640]{2,1,0:T(8,128)(2,1)}), bf16[8,64,640]{2,1,0:T(8,128)(2,1)S(1)}, u32[]{:S(2)}, u32[]{:S(2)}) %all-to-all-start) | async-done | bytes 655392 | tf_op jit(solution)/shard_map/all_to_all | solution.py:372
  30.2 5.0 %all-to-all-start.1 = ((bf16[8,64,512]{2,1,0:T(8,128)(2,1)}), bf16[8,64,512]{2,1,0:T(8,128)(2,1)}, u32[]{:S(2)}, u32[]{:S(2)}) async-start(bf16[8,64,512]{2,1,0:T(8,128)(2,1)} %bitcast.17), calls=%async_computation.1 | async-start | bytes 1048576 | tf_op jit(solution)/shard_map/all_to_all | solution.py:418
  35.9 0.1 pad_add_fusion.place
  36.0 1.0 copy-done.7
  37.0 2.3 %student.1 = (bf16[512,512]{1,0:T(8,128)(2,1)S(1)}, f32[512,512]{1,0:T(8,128)S(1)}, bf16[640,512]{1,0:T(8,128)(2,1)S(1)}, f32[2,8,64,512]{3,2,1,0:T(8,128)S(1)}, f32[16,128]{1,0:T(8,128)S(1)}) custom-call(bf16[512,640]{1,0:T(8,128)(2,1)S(1)} %bitcast.16, bf16[512,512]{1,0:T(8,128)(2,1)S(1)} %copy-done.7, bf16[128,512]{1,0:T(8,128)(2,1)S(1)} %copy-done.9, ...), custom_call_target="tpu_custom_call" | custom-call | tf_op jit(solution)/shard_map/student/pallas_call | solution.py:436
  39.3 1.0 copy-done.5
  40.2 0.9 copy-done.6
  41.1 0.8 copy-done.8
  41.9 7.8 %all-to-all-done.1.teacher = bf16[8,64,512]{2,1,0:T(8,128)(2,1)} async-done(((bf16[8,64,512]{2,1,0:T(8,128)(2,1)}), bf16[8,64,512]{2,1,0:T(8,128)(2,1)}, u32[]{:S(2)}, u32[]{:S(2)}) %all-to-all-start.1) | async-done | bytes 524320 | tf_op jit(solution)/shard_map/all_to_all | solution.py:418
  49.7 4.9 %score.1 = (bf16[32,2,40,128]{3,2,1,0:T(8,128)(2,1)S(1)}, bf16[32,2,40,128]{3,2,1,0:T(8,128)(2,1)S(1)}) custom-call(f32[2,8,64,512]{3,2,1,0:T(8,128)S(1)} %get-tuple-element.16.held, bf16[8,64,512]{2,1,0:T(8,128)(2,1)} %all-to-all-done.1.teacher, f32[16,128]{1,0:T(8,128)S(1)} %get-tuple-element.17.within_loss, bf16[640,512]{1,0:T(8,128)(2,1)} %copy-done.6, ...), custom_call_target="tpu_custom_call" | custom-call | tf_op jit(solution)/shard_map/score/pallas_call | solution.py:438
  54.6 2.9 %collective-permute-start.2 = (bf16[32,2,40,128]{3,2,1,0:T(8,128)(2,1)S(1)}, bf16[32,2,40,128]{3,2,1,0:T(8,128)(2,1)S(1)}, u32[]{:S(2)}, u32[]{:S(2)}) collective-permute-start(bf16[32,2,40,128]{3,2,1,0:T(8,128)(2,1)S(1)} %get-tuple-element.22), channel_id=1, source_target_pairs={{0,64},{64,0},{1,65},{65,1},{2,66},{66,2},{3,67},{67,3},{4,68},{68... | collective-permute-start | bytes 1966088 | tf_op jit(solution)/shard_map/ppermute | solution.py:465
  57.5 1.7 %collective-permute-done.2 = bf16[32,2,40,128]{3,2,1,0:T(8,128)(2,1)S(1)} collective-permute-done((bf16[32,2,40,128]{3,2,1,0:T(8,128)(2,1)S(1)}, bf16[32,2,40,128]{3,2,1,0:T(8,128)(2,1)S(1)}, u32[]{:S(2)}, u32[]{:S(2)}) %collective-permute-start.2) | collective-permute-done | bytes 655392 | tf_op jit(solution)/shard_map/ppermute | solution.py:465
  59.2 0.2 add_convert_fusion
  59.4 25.4 %all_to_all.20.arrived = bf16[32,2,40,128]{3,2,1,0:T(8,128)(2,1)S(1)} all-to-all(bf16[32,2,40,128]{3,2,1,0:T(8,128)(2,1)S(1)} %add_convert_fusion), channel_id=1, replica_groups=mesh['member_0'=4,'core'=2,'tile_0'=2,'tile_1'=4,'tile_2'=8] {'tile_1','..., dimensions={0} | all-to-all | bytes 1310720 | tf_op jit(solution)/shard_map/all_to_all | solution.py:467
  84.8 0.2 fold.1
  85.0 20.0 %all_to_all.21.arrived = bf16[16,40,128]{2,1,0:T(8,128)(2,1)S(1)} all-to-all(bf16[16,40,128]{2,1,0:T(8,128)(2,1)S(1)} %fold.1), channel_id=1, replica_groups=mesh['member_0'=4,'core'=2,'tile_0'=2,'tile_1'=4,'tile_2'=8] {'tile_0','..., dimensions={0} | all-to-all | bytes 327680 | tf_op jit(solution)/shard_map/all_to_all | solution.py:476
  105.0 0.6 last.1
  (20 shorter events, 0.1 us)
Async XLA Ops:
  0.6 12.4 %copy-start = (bf16[1,512,512]{2,1,0:T(8,128)(2,1)S(1)}, bf16[1,512,512]{2,1,0:T(8,128)(2,1)}, u32[]{:S(2)}) copy-start(bf16[1,512,512]{2,1,0:T(8,128)(2,1)} %param.10) | copy-start | bytes 1572868
  0.6 15.2 %copy-start.1 = (bf16[512,1024]{1,0:T(8,128)(2,1)S(1)}, bf16[512,1024]{1,0:T(8,128)(2,1)}, u32[]{:S(2)}) copy-start(bf16[512,1024]{1,0:T(8,128)(2,1)} %up.3) | copy-start | bytes 3145732
  0.7 15.2 %copy-start.2 = (bf16[1024,512]{1,0:T(8,128)(2,1)S(1)}, bf16[1024,512]{1,0:T(8,128)(2,1)}, u32[]{:S(2)}) copy-start(bf16[1024,512]{1,0:T(8,128)(2,1)} %down.3) | copy-start | bytes 3145732
  0.7 15.2 %copy-start.10 = (s32[8,512]{1,0:T(8,128)S(1)}, s32[8,512]{1,0:T(8,128)}, u32[]{:S(2)}) copy-start(s32[8,512]{1,0:T(8,128)} %near.3) | copy-start | bytes 49156
  2.7 27.5 %all-to-all-start = ((bf16[8,64,640]{2,1,0:T(8,128)(2,1)}), bf16[8,64,640]{2,1,0:T(8,128)(2,1)S(1)}, u32[]{:S(2)}, u32[]{:S(2)}) async-start(bf16[8,64,640]{2,1,0:T(8,128)(2,1)} %bitcast.19), calls=%async_computation | async-start | bytes 1310720 | tf_op jit(solution)/shard_map/all_to_all | solution.py:372
  13.0 6.3 %collective-permute-start.1 = (bf16[64,512]{1,0:T(8,128)(2,1)S(1)}, bf16[64,512]{1,0:T(8,128)(2,1)S(1)}, u32[]{:S(2)}, u32[]{:S(2)}) collective-permute-start(bf16[64,512]{1,0:T(8,128)(2,1)S(1)} %get-tuple-element.27), channel_id=1, source_target_pairs={{0,1},{2,3},{4,5},{6,7},{8,9},{10,11},{12,13},{14,15},{16,17},{18,... | collective-permute-start | bytes 196616 | tf_op jit(solution)/shard_map/ppermute | solution.py:334
  15.0 4.4 %copy-start.3 = (bf16[512,512]{1,0:T(8,128)(2,1)S(1)}, bf16[512,512]{1,0:T(8,128)(2,1)}, u32[]{:S(2)}) copy-start(bf16[512,512]{1,0:T(8,128)(2,1)} %msg.1) | copy-start | bytes 1572868
  15.0 4.4 %collective-permute-start = (bf16[64,512]{1,0:T(8,128)(2,1)S(1)}, bf16[64,512]{1,0:T(8,128)(2,1)S(1)}, u32[]{:S(2)}, u32[]{:S(2)}) collective-permute-start(bf16[64,512]{1,0:T(8,128)(2,1)S(1)} %get-tuple-element.28), channel_id=1, source_target_pairs={{1,2},{3,4},{5,6},{7,8},{9,10},{11,12},{13,14},{15,16},{17,18},{19... | collective-permute-start | bytes 196616 | tf_op jit(solution)/shard_map/ppermute | solution.py:334
  19.4 16.6 %copy-start.9 = (bf16[128,512]{1,0:T(8,128)(2,1)S(1)}, bf16[128,512]{1,0:T(8,128)(2,1)}, u32[]{:S(2)}) copy-start(bf16[128,512]{1,0:T(8,128)(2,1)} %w_noise.1) | copy-start | bytes 393220
  21.2 14.7 %copy-start.4 = (bf16[512,512]{1,0:T(8,128)(2,1)S(1)}, bf16[512,512]{1,0:T(8,128)(2,1)}, u32[]{:S(2)}) copy-start(bf16[512,512]{1,0:T(8,128)(2,1)} %w_out_at.1) | copy-start | bytes 1572868
  30.2 19.5 %all-to-all-start.1 = ((bf16[8,64,512]{2,1,0:T(8,128)(2,1)}), bf16[8,64,512]{2,1,0:T(8,128)(2,1)}, u32[]{:S(2)}, u32[]{:S(2)}) async-start(bf16[8,64,512]{2,1,0:T(8,128)(2,1)} %bitcast.17), calls=%async_computation.1 | async-start | bytes 1048576 | tf_op jit(solution)/shard_map/all_to_all | solution.py:418
  35.9 1.0 copy-start.7
  39.3 1.0 copy-start.5
  40.2 0.9 copy-start.6
  41.1 0.8 copy-start.8
  54.6 4.6 %collective-permute-start.2 = (bf16[32,2,40,128]{3,2,1,0:T(8,128)(2,1)S(1)}, bf16[32,2,40,128]{3,2,1,0:T(8,128)(2,1)S(1)}, u32[]{:S(2)}, u32[]{:S(2)}) collective-permute-start(bf16[32,2,40,128]{3,2,1,0:T(8,128)(2,1)S(1)} %get-tuple-element.22), channel_id=1, source_target_pairs={{0,64},{64,0},{1,65},{65,1},{2,66},{66,2},{3,67},{67,3},{4,68},{68... | collective-permute-start | bytes 1966088 | tf_op jit(solution)/shard_map/ppermute | solution.py:465

commit v7 on v5

--- a/solution.py
+++ b/solution.py
@@ -9,6 +9,7 @@
 from jax.sharding import PartitionSpec as P
 
 D = 512
+FF = 1024
 H = 512
 NOISE = 128
 NBRS = 8
@@ -21,7 +22,6 @@
 TILES = 64
 HALF = D // 2
 XY = TILES // 2
-JOINS = 4
 SHARE = 40
 LOSS_ROW = 36
 
@@ -47,9 +47,31 @@
     return (resid + jnp.dot(hidden, down, preferred_element_type=F32)).astype(BF16)
 
 
-def middle_kernel(state, near, msg_at, up, down, out, msg, held, sem, out_sem):
-    copy = pltpu.make_async_copy(msg_at, msg, sem)
-    copy.start()
+def middle_kernel(
+    state,
+    noise,
+    near,
+    msg_at,
+    up_at,
+    down_at,
+    out,
+    sent,
+    msg,
+    up,
+    down,
+    held,
+    sem,
+    out_sem,
+    noise_sem,
+):
+    loads = [
+        pltpu.make_async_copy(source, target, sem.at[k])
+        for k, (source, target) in enumerate(((msg_at, msg), (up_at, up), (down_at, down)))
+    ]
+    for copy in loads:
+        copy.start()
+    beside = pltpu.make_async_copy(noise, sent.at[:, D:], noise_sem)
+    beside.start()
     sub = 128
     parts = []
     for at in range(0, CELLS - 2 * HALO, sub):
@@ -61,7 +83,8 @@
                 preferred_element_type=F32,
             ).astype(BF16)
         )
-    copy.wait()
+    for copy in loads:
+        copy.wait()
     half = (CELLS - 2 * HALO) // 2
     gathered = jnp.concatenate(parts, axis=0)
     writes = []
@@ -73,17 +96,33 @@
             up[...],
             down[...],
         )
-        writes.append(
-            pltpu.make_async_copy(
-                held.at[at : at + half], out.at[HALO + at : HALO + at + half], out_sem.at[k]
+        rows = pl.ds(HALO + at, half)
+        for target, wait in ((out.at[rows], 2 * k), (sent.at[rows, :D], 2 * k + 1)):
+            writes.append(
+                pltpu.make_async_copy(held.at[at : at + half], target, out_sem.at[wait])
             )
-        )
-        writes[-1].start()
+            writes[-1].start()
+    beside.wait()
     for copy in writes:
         copy.wait()
 
 
-def edges_kernel(odd_swap, even_swap, state, near, msg, up, down, partly, odd, out, held, sem):
+def edges_kernel(
+    odd_swap,
+    even_swap,
+    state,
+    near,
+    msg,
+    up,
+    down,
+    partly,
+    partly_sent,
+    odd,
+    out,
+    sent,
+    held,
+    sem,
+):
     reach = 3 * HALO
     is_odd = jnp.full((HALO, D), odd[0], jnp.int32) == 1
     after_odd = odd_swap[...].astype(F32)
@@ -108,6 +147,8 @@
     writes = [
         pltpu.make_async_copy(held.at[:HALO], out.at[:HALO], sem.at[0]),
         pltpu.make_async_copy(held.at[HALO:], out.at[CELLS - HALO :], sem.at[1]),
+        pltpu.make_async_copy(held.at[:HALO], sent.at[:HALO, :D], sem.at[2]),
+        pltpu.make_async_copy(held.at[HALO:], sent.at[CELLS - HALO :, :D], sem.at[3]),
     ]
     for copy in writes:
         copy.start()
@@ -115,54 +156,21 @@
         copy.wait()
 
 
-def join_kernel(state, noise, both, held, sem, out_sem):
-    rows = CELLS // JOINS
-    reads = []
-    for k in range(JOINS):
-        at = pl.ds(k * rows, rows)
-        reads.append(
-            (
-                pltpu.make_async_copy(state.at[at], held.at[at, :D], sem.at[2 * k]),
-                pltpu.make_async_copy(noise.at[at], held.at[at, D:], sem.at[2 * k + 1]),
-            )
-        )
-        for copy in reads[-1]:
-            copy.start()
-    writes = []
-    for k in range(JOINS):
-        at = pl.ds(k * rows, rows)
-        for copy in reads[k]:
-            copy.wait()
-        writes.append(pltpu.make_async_copy(held.at[at], both.at[at], out_sem.at[k]))
-        writes[-1].start()
-    for copy in writes:
-        copy.wait()
-
-
-def student_kernel(mine, w_in, w_noise, w_out, student, shidden, slope, turned):
+def student_kernel(mine, w_in, early, turned):
     rows = 256
     for at in range(0, CELLS, rows):
-        state = mine[at : at + rows, :D]
-        preact = jnp.dot(state, w_in[...], preferred_element_type=F32) + jnp.dot(
-            mine[at : at + rows, D:], w_noise[...], preferred_element_type=F32
-        )
-        sig = jax.nn.sigmoid(preact)
-        hid = (preact * sig).astype(BF16)
-        slope[at : at + rows] = sig * (1.0 + preact * (1.0 - sig))
-        student[at : at + rows] = (
-            state.astype(F32) + jnp.dot(hid, w_out[...], preferred_element_type=F32)
-        ).astype(BF16)
-        shidden[:, at : at + rows] = hid.T
-        turned[:, at : at + rows] = mine[at : at + rows].T
+        state = mine[at : at + rows]
+        early[at : at + rows] = jnp.dot(state, w_in[...], preferred_element_type=F32)
+        turned[:, at : at + rows] = state.T
 
 
 def score_kernel(
-    student,
-    teacher,
+    early,
+    mine,
+    every,
+    w_noise,
+    w_out,
     turned_at,
-    shidden_at,
-    slope_at,
-    w_out_at,
     place,
     send,
     keep,
@@ -170,28 +178,42 @@
     gpre,
     wide,
     turned,
+    turned_noise,
     shidden,
     slope,
-    w_out,
+    student,
     sem,
 ):
-    copies = [
-        pltpu.make_async_copy(source, target, sem.at[k])
-        for k, (source, target) in enumerate(
-            ((turned_at, turned), (shidden_at, shidden), (slope_at, slope), (w_out_at, w_out))
+    copy = pltpu.make_async_copy(turned_at, turned, sem)
+    copy.start()
+    rows = 256
+    for at in range(0, CELLS, rows):
+        draws = every[at // BLOCK : (at + rows) // BLOCK, :, D:].reshape(rows, NOISE)
+        preact = early[at : at + rows] + jnp.dot(
+            draws, w_noise[...], preferred_element_type=F32
         )
-    ]
-    for copy in copies:
-        copy.start()
+        sig = jax.nn.sigmoid(preact)
+        hid = (preact * sig).astype(BF16)
+        slope[at : at + rows] = sig * (1.0 + preact * (1.0 - sig))
+        student[at : at + rows] = (
+            mine[at : at + rows].astype(F32)
+            + jnp.dot(hid, w_out[...], preferred_element_type=F32)
+        ).astype(BF16)
+        shidden[:, at : at + rows] = hid.T
+        turned_noise[:, at : at + rows] = draws.T
+
     step = 16
     wide[...] = jnp.zeros_like(wide)
 
     def block(cell, lane):
-        s = [student[m, pl.ds(cell, step), lane : lane + 128].astype(F32) for m in range(MEMBERS)]
+        s = [
+            student[pl.ds(cell + m * BLOCK, step), lane : lane + 128].astype(F32)
+            for m in range(MEMBERS)
+        ]
         g = [jnp.zeros((step, 128), F32) for _ in range(MEMBERS)]
         loss = jnp.zeros((step, 128), F32)
         for n in range(MEMBERS):
-            t = teacher[n, pl.ds(cell, step), lane : lane + 128].astype(F32)
+            t = every[n, pl.ds(cell, step), lane : lane + 128].astype(F32)
             for m in range(MEMBERS):
                 d = s[m] - t
                 q = d * d + 0.01
@@ -232,8 +254,7 @@
         spread = spread + jnp.where(lane_ids == at + k * REGIONS, piece, 0.0)
     spread = jnp.broadcast_to(spread[None], (XY, 4, 128))
 
-    for copy in copies:
-        copy.wait()
+    copy.wait()
     back = gst[...].reshape(CELLS, D)
     pull = lax.dot_general(
         back, w_out[...], (((1,), (1,)), ((), ())), preferred_element_type=F32
@@ -245,8 +266,8 @@
             shidden[...], gst[:, :, pl.ds(left, HALF)].reshape(CELLS, HALF), preferred_element_type=F32
         )
         pulled = gpre[:, pl.ds(left, HALF)]
-        d_in = jnp.dot(turned[:D], pulled, preferred_element_type=F32)
-        d_noise = jnp.dot(turned[D:], pulled, preferred_element_type=F32)
+        d_in = jnp.dot(turned[...], pulled, preferred_element_type=F32)
+        d_noise = jnp.dot(turned_noise[...], pulled, preferred_element_type=F32)
         for high in range(2):
             pieces = []
             for source, count in ((d_in, 8), (d_out, 8), (d_noise, 2)):
@@ -336,55 +357,52 @@
     student_out,
 ):
     state = inputs[0]
-    both = pl.pallas_call(
-        join_kernel,
-        out_shape=jax.ShapeDtypeStruct((CELLS, D + NOISE), BF16),
-        in_specs=[HBM] * 2,
-        out_specs=HBM,
-        scratch_shapes=[
-            pltpu.VMEM((CELLS, D + NOISE), BF16),
-            pltpu.SemaphoreType.DMA((2 * JOINS,)),
-            pltpu.SemaphoreType.DMA((JOINS,)),
-        ],
-        compiler_params=pltpu.CompilerParams(vmem_limit_bytes=60 * 1024 * 1024),
-        name="join",
-    )(in_hbm(state), in_hbm(noise[0]))
     mine = lax.all_to_all(
-        both.reshape(MEMBERS, BLOCK, D + NOISE),
-        MEMBER,
-        split_axis=0,
-        concat_axis=0,
-        tiled=True,
+        state.reshape(MEMBERS, BLOCK, D), MEMBER, split_axis=0, concat_axis=0, tiled=True
     )
     odd = lax.axis_index("tile_2") % 2
     far = exchanged(state, odd, 1)
     near = exchanged(state, odd, 0)
+    shapes = (
+        jax.ShapeDtypeStruct((CELLS, D), BF16),
+        jax.ShapeDtypeStruct((CELLS, D + NOISE), BF16),
+    )
     middle = pl.pallas_call(
         middle_kernel,
-        out_shape=jax.ShapeDtypeStruct((CELLS, D), BF16),
-        in_specs=[VMEM] * 2 + [HBM] + [VMEM] * 2,
-        out_specs=HBM,
+        out_shape=shapes,
+        in_specs=[VMEM] * 3 + [HBM] * 3,
+        out_specs=[HBM] * 2,
         scratch_shapes=[
             pltpu.VMEM((D, D), BF16),
+            pltpu.VMEM((D, FF), BF16),
+            pltpu.VMEM((FF, D), BF16),
             pltpu.VMEM((CELLS - 2 * HALO, D), BF16),
+            pltpu.SemaphoreType.DMA((3,)),
+            pltpu.SemaphoreType.DMA((4,)),
             pltpu.SemaphoreType.DMA,
-            pltpu.SemaphoreType.DMA((2,)),
         ],
         compiler_params=PARAMS,
         name="middle",
     )
     edges = pl.pallas_call(
         edges_kernel,
-        out_shape=jax.ShapeDtypeStruct((CELLS, D), BF16),
-        in_specs=[VMEM] * 7 + [HBM, pl.BlockSpec(memory_space=pltpu.SMEM)],
-        out_specs=HBM,
-        input_output_aliases={7: 0},
-        scratch_shapes=[pltpu.VMEM((2 * HALO, D), BF16), pltpu.SemaphoreType.DMA((2,))],
+        out_shape=shapes,
+        in_specs=[VMEM] * 7 + [HBM] * 2 + [pl.BlockSpec(memory_space=pltpu.SMEM)],
+        out_specs=[HBM] * 2,
+        input_output_aliases={7: 0, 8: 1},
+        scratch_shapes=[pltpu.VMEM((2 * HALO, D), BF16), pltpu.SemaphoreType.DMA((4,))],
         compiler_params=PARAMS,
         name="edges",
     )
-    partly = middle(state, neighbours, in_hbm(msg_weight), up_weight, down_weight)
-    teacher = edges(
+    partly, partly_sent = middle(
+        state,
+        noise[0],
+        neighbours,
+        in_hbm(msg_weight),
+        in_hbm(up_weight),
+        in_hbm(down_weight),
+    )
+    teacher, sent = edges(
         far,
         near,
         state,
@@ -393,53 +411,49 @@
         up_weight,
         down_weight,
         partly,
+        partly_sent,
         odd.astype(jnp.int32).reshape(1),
     )
     every = lax.all_to_all(
-        teacher.reshape(MEMBERS, BLOCK, D), MEMBER, split_axis=0, concat_axis=0, tiled=True
-    )
-    mine = mine.reshape(CELLS, D + NOISE)
+        sent.reshape(MEMBERS, BLOCK, D + NOISE),
+        MEMBER,
+        split_axis=0,
+        concat_axis=0,
+        tiled=True,
+    )
+    mine = mine.reshape(CELLS, D)
     pupil = pl.pallas_call(
         student_kernel,
         out_shape=(
-            jax.ShapeDtypeStruct((CELLS, D), BF16),
-            jax.ShapeDtypeStruct((H, CELLS), BF16),
             jax.ShapeDtypeStruct((CELLS, H), F32),
-            jax.ShapeDtypeStruct((D + NOISE, CELLS), BF16),
+            jax.ShapeDtypeStruct((D, CELLS), BF16),
         ),
-        in_specs=[VMEM] * 4,
-        out_specs=[VMEM] * 4,
+        in_specs=[VMEM] * 2,
+        out_specs=[VMEM] * 2,
         compiler_params=PARAMS,
         name="student",
     )
-    student, shidden, slope, turned = pupil(mine, student_in, student_noise, student_out)
+    early, turned = pupil(mine, student_in)
     place = jnp.stack([region_map[0], lax.axis_index("core").astype(jnp.int32)])
     send, keep = pl.pallas_call(
         score_kernel,
         out_shape=[jax.ShapeDtypeStruct((XY, 2, SHARE, 128), BF16)] * 2,
-        in_specs=[VMEM] * 2 + [HBM] * 4 + [pl.BlockSpec(memory_space=pltpu.SMEM)],
+        in_specs=[VMEM] * 5 + [HBM, pl.BlockSpec(memory_space=pltpu.SMEM)],
         out_specs=[VMEM] * 2,
         scratch_shapes=[
             pltpu.VMEM((MEMBERS, BLOCK, D), BF16),
             pltpu.VMEM((CELLS, D), BF16),
             pltpu.VMEM((16, 128), F32),
-            pltpu.VMEM((D + NOISE, CELLS), BF16),
+            pltpu.VMEM((D, CELLS), BF16),
+            pltpu.VMEM((NOISE, CELLS), BF16),
             pltpu.VMEM((H, CELLS), BF16),
             pltpu.VMEM((CELLS, H), F32),
-            pltpu.VMEM((H, D), BF16),
-            pltpu.SemaphoreType.DMA((4,)),
+            pltpu.VMEM((CELLS, D), BF16),
+            pltpu.SemaphoreType.DMA,
         ],
         compiler_params=PARAMS,
         name="score",
-    )(
-        student.reshape(MEMBERS, BLOCK, D),
-        every,
-        in_hbm(turned),
-        in_hbm(shidden),
-        in_hbm(slope),
-        in_hbm(student_out),
-        place,
-    )
+    )(early, mine, every, student_noise, student_out, in_hbm(turned), place)
     other = lax.ppermute(send, "core", [(0, 1), (1, 0)])
     half = (keep.astype(F32) + other.astype(F32)).astype(BF16)
     shares = lax.all_to_all(half, ("tile_1", "tile_2"), split_axis=0, concat_axis=0, tiled=True)

time: 106 us -> 105 us (level)
  local copies, waits for them, and re-layouts: 2.7 us -> 0.85 us
  waiting for transfers between devices: 20.5 us -> 22 us
    all_to_all x1, blocking collectives: 26 us -> 28.2 us  [step(): lax.all_to_all(half, ('tile_1', 'tile_2'), split_axis=0, concat_axis=0, t...]
    all_to_all x1, blocking collectives: 19.4 us -> 17.3 us  [step(): lax.all_to_all(copies, ('tile_0', 'member_0', 'core'), split_axis=0, conc...]
    unnamed x22 -> x20, local copies, waits for them, and re-layouts: 2.69 us -> 0.84 us
    pallas_call x3 -> x2, Pallas kernels: 6.68 us -> 5.08 us  [the longest x1 4.65 us: step(): middle(state, noise[0], neighbours, in_hbm(msg_weight), in_hbm(up_weight)...]
    all_to_all x2, waiting for transfers between devices: 18.8 us -> 20.3 us  [the longest x1 15.2 us: step(): lax.all_to_all(sent.reshape(MEMBERS, BLOCK, D + NOISE), MEMBER, split_axi...]
  transfers between devices with their start and end apart: 5 -> 5, of which waited for: 3 -> 3; matrix products, arithmetic and copies ran while one was open for 0% -> 0% of each run, Pallas kernels for 6% -> 7%
where the time goes in v7:
time: 105 us
  blocking collectives  45.5 us (43%)
  waiting for transfers between devices  22 us (21%)
  starting transfers between devices  20.4 us (19%)
  Pallas kernels  14.1 us (13%)
  between operations  1.47 us (1%)
    all_to_all x1, blocking collectives, step(): lax.all_to_all(half, ('tile_1', 'tile_2'), split_axis=0, concat_axis=0, t...  28.2 us
    all_to_all x1, blocking collectives, step(): lax.all_to_all(copies, ('tile_0', 'member_0', 'core'), split_axis=0, conc...  17.3 us
    all_to_all x1, waiting for transfers between devices, step(): lax.all_to_all(sent.reshape(MEMBERS, BLOCK, D + NOISE), MEMBER, split_axi...  15.2 us
    all_to_all x1, starting transfers between devices, step(): lax.all_to_all(state.reshape(MEMBERS, BLOCK, D), MEMBER, split_axis=0, co...  10.4 us
    pallas_call x1, Pallas kernels, step(): pl.pallas_call(score_kernel, out_shape=[jax.ShapeDtypeStruct((XY, 2, SHAR...  6.28 us
    all_to_all x1, waiting for transfers between devices, step(): lax.all_to_all(state.reshape(MEMBERS, BLOCK, D), MEMBER, split_axis=0, co...  5.08 us
    pallas_call x1, Pallas kernels, step(): middle(state, noise[0], neighbours, in_hbm(msg_weight), in_hbm(up_weight)...  4.65 us
    all_to_all x1, starting transfers between devices, step(): lax.all_to_all(sent.reshape(MEMBERS, BLOCK, D + NOISE), MEMBER, split_axi...  4.54 us
  transfers between devices with their start and end apart: 5, of which 3 were waited for; matrix products, arithmetic and copies ran while one was open for 0% of the time, Pallas kernels for 7%

profile of v7, /device:TPU:1, one launch (start us, length us, event | category | flops | bytes accessed | tf_op | source)
XLA Modules:
  0.0 104.5 jit_solution(12640178805528008445)
XLA Ops:
  0.7 10.4 %all-to-all-start = ((bf16[8,64,512]{2,1,0:T(8,128)(2,1)}), bf16[8,64,512]{2,1,0:T(8,128)(2,1)S(1)}, u32[]{:S(2)}, u32[]{:S(2)}) async-start(bf16[8,64,512]{2,1,0:T(8,128)(2,1)} %bitcast.13), calls=%async_computation | async-start | bytes 1048576 | tf_op jit(solution)/shard_map/all_to_all | solution.py:360
  11.1 1.9 %collective-permute-start.1 = (bf16[64,512]{1,0:T(8,128)(2,1)S(1)}, bf16[64,512]{1,0:T(8,128)(2,1)S(1)}, u32[]{:S(2)}, u32[]{:S(2)}) collective-permute-start(bf16[64,512]{1,0:T(8,128)(2,1)S(1)} %get-tuple-element.29), channel_id=1, source_target_pairs={{0,1},{2,3},{4,5},{6,7},{8,9},{10,11},{12,13},{14,15},{16,17},{18,... | collective-permute-start | bytes 196616 | tf_op jit(solution)/shard_map/ppermute | solution.py:335
  13.0 0.7 collective-permute-start
  13.7 0.0 copy-start.1
  13.7 0.0 copy-start.2
  13.7 0.0 copy-start.3
  13.7 4.6 %middle.1 = (bf16[512,512]{1,0:T(8,128)(2,1)}, bf16[512,640]{1,0:T(8,128)(2,1)}) custom-call(bf16[512,512]{1,0:T(8,128)(2,1)S(1)} %bitcast.14, bf16[512,128]{1,0:T(8,128)(2,1)S(1)} %bitcast.18, s32[8,512]{1,0:T(8,128)S(1)} %copy-done.9, bf16[512,512]{1,0:T(8,128)(2,1)} %msg.1, bf16[512,1024]{1,0:T(8,128)(2,1)} %up.1, bf16[1024,512]{1,0:T(8,128)(2,1)} %down.1), custom_call_target="tpu_custom_call" | custom-call | tf_op jit(solution)/shard_map/middle/pallas_call | solution.py:397
  18.4 0.0 collective-permute-done.1.even_swap
  18.4 1.9 %edges.1 = (bf16[512,512]{1,0:T(8,128)(2,1)}, bf16[512,640]{1,0:T(8,128)(2,1)}) custom-call(bf16[64,512]{1,0:T(8,128)(2,1)S(1)} %collective-permute-done.odd_swap, bf16[64,512]{1,0:T(8,128)(2,1)S(1)} %collective-permute-done.1.even_swap, bf16[512,512]{1,0:T(8,128)(2,1)S(1)} %bitcast.15, ...), custom_call_target="tpu_custom_call", output_to_operand_aliasing={{0}: (7, {}), {1}: (8, {})} | custom-call | tf_op jit(solution)/shard_map/edges/pallas_call | solution.py:405
  20.3 0.0 copy-start.4
  20.4 5.1 %all-to-all-done = bf16[8,64,512]{2,1,0:T(8,128)(2,1)S(1)} async-done(((bf16[8,64,512]{2,1,0:T(8,128)(2,1)}), bf16[8,64,512]{2,1,0:T(8,128)(2,1)S(1)}, u32[]{:S(2)}, u32[]{:S(2)}) %all-to-all-start) | async-done | bytes 524320 | tf_op jit(solution)/shard_map/all_to_all | solution.py:360
  25.4 4.5 %all-to-all-start.1 = ((bf16[8,64,640]{2,1,0:T(8,128)(2,1)}), bf16[8,64,640]{2,1,0:T(8,128)(2,1)S(1)}, u32[]{:S(2)}, u32[]{:S(2)}) async-start(bf16[8,64,640]{2,1,0:T(8,128)(2,1)} %bitcast.8), calls=%async_computation.1 | async-start | bytes 1310720 | tf_op jit(solution)/shard_map/all_to_all | solution.py:417
  30.6 0.1 pad_add_fusion.place
  30.7 0.4 student.1
  31.2 0.8 copy-done.6
  31.9 15.2 %all-to-all-done.1.every = bf16[8,64,640]{2,1,0:T(8,128)(2,1)S(1)} async-done(((bf16[8,64,640]{2,1,0:T(8,128)(2,1)}), bf16[8,64,640]{2,1,0:T(8,128)(2,1)S(1)}, u32[]{:S(2)}, u32[]{:S(2)}) %all-to-all-start.1) | async-done | bytes 655392 | tf_op jit(solution)/shard_map/all_to_all | solution.py:417
  47.2 6.3 %score.1 = (bf16[32,2,40,128]{3,2,1,0:T(8,128)(2,1)S(1)}, bf16[32,2,40,128]{3,2,1,0:T(8,128)(2,1)S(1)}) custom-call(f32[512,512]{1,0:T(8,128)S(1)} %get-tuple-element.20.early, bf16[512,512]{1,0:T(8,128)(2,1)S(1)} %bitcast.17, bf16[8,64,640]{2,1,0:T(8,128)(2,1)S(1)} %all-to-all-done.1.every, bf16[128,512]{1,0:T(8,128)(2,1)S(1)} %copy-done.8, ...), custom_call_target="tpu_custom_call" | custom-call | tf_op jit(solution)/shard_map/score/pallas_call | solution.py:438
  53.5 2.9 %collective-permute-start.2 = (bf16[32,2,40,128]{3,2,1,0:T(8,128)(2,1)S(1)}, bf16[32,2,40,128]{3,2,1,0:T(8,128)(2,1)S(1)}, u32[]{:S(2)}, u32[]{:S(2)}) collective-permute-start(bf16[32,2,40,128]{3,2,1,0:T(8,128)(2,1)S(1)} %get-tuple-element.24), channel_id=1, source_target_pairs={{0,64},{64,0},{1,65},{65,1},{2,66},{66,2},{3,67},{67,3},{4,68},{68... | collective-permute-start | bytes 1966088 | tf_op jit(solution)/shard_map/ppermute | solution.py:457
  56.4 1.7 %collective-permute-done.2 = bf16[32,2,40,128]{3,2,1,0:T(8,128)(2,1)S(1)} collective-permute-done((bf16[32,2,40,128]{3,2,1,0:T(8,128)(2,1)S(1)}, bf16[32,2,40,128]{3,2,1,0:T(8,128)(2,1)S(1)}, u32[]{:S(2)}, u32[]{:S(2)}) %collective-permute-start.2) | collective-permute-done | bytes 655392 | tf_op jit(solution)/shard_map/ppermute | solution.py:457
  58.1 0.2 add_convert_fusion
  58.2 28.2 %all_to_all.20.arrived = bf16[32,2,40,128]{3,2,1,0:T(8,128)(2,1)S(1)} all-to-all(bf16[32,2,40,128]{3,2,1,0:T(8,128)(2,1)S(1)} %add_convert_fusion), channel_id=1, replica_groups=mesh['member_0'=4,'core'=2,'tile_0'=2,'tile_1'=4,'tile_2'=8] {'tile_1','..., dimensions={0} | all-to-all | bytes 1310720 | tf_op jit(solution)/shard_map/all_to_all | solution.py:459
  86.4 0.2 fold.1
  86.6 17.3 %all_to_all.21.arrived = bf16[16,40,128]{2,1,0:T(8,128)(2,1)S(1)} all-to-all(bf16[16,40,128]{2,1,0:T(8,128)(2,1)S(1)} %fold.1), channel_id=1, replica_groups=mesh['member_0'=4,'core'=2,'tile_0'=2,'tile_1'=4,'tile_2'=8] {'tile_0','..., dimensions={0} | all-to-all | bytes 327680 | tf_op jit(solution)/shard_map/all_to_all | solution.py:468
  103.9 0.6 last.1
  (17 shorter events, 0.0 us)
Async XLA Ops:
  0.6 10.4 %copy-start = (bf16[1,512,512]{2,1,0:T(8,128)(2,1)S(1)}, bf16[1,512,512]{2,1,0:T(8,128)(2,1)}, u32[]{:S(2)}) copy-start(bf16[1,512,512]{2,1,0:T(8,128)(2,1)} %param.10) | copy-start | bytes 1572868
  0.6 13.0 %copy-start.9 = (s32[8,512]{1,0:T(8,128)S(1)}, s32[8,512]{1,0:T(8,128)}, u32[]{:S(2)}) copy-start(s32[8,512]{1,0:T(8,128)} %near.3) | copy-start | bytes 49156
  0.7 13.0 %copy-start.7 = (bf16[1,512,128]{2,1,0:T(8,128)(2,1)S(1)}, bf16[1,512,128]{2,1,0:T(8,128)(2,1)}, u32[]{:S(2)}) copy-start(bf16[1,512,128]{2,1,0:T(8,128)(2,1)} %param.11) | copy-start | bytes 393220
  0.7 24.8 %all-to-all-start = ((bf16[8,64,512]{2,1,0:T(8,128)(2,1)}), bf16[8,64,512]{2,1,0:T(8,128)(2,1)S(1)}, u32[]{:S(2)}, u32[]{:S(2)}) async-start(bf16[8,64,512]{2,1,0:T(8,128)(2,1)} %bitcast.13), calls=%async_computation | async-start | bytes 1048576 | tf_op jit(solution)/shard_map/all_to_all | solution.py:360
  11.1 7.3 %collective-permute-start.1 = (bf16[64,512]{1,0:T(8,128)(2,1)S(1)}, bf16[64,512]{1,0:T(8,128)(2,1)S(1)}, u32[]{:S(2)}, u32[]{:S(2)}) collective-permute-start(bf16[64,512]{1,0:T(8,128)(2,1)S(1)} %get-tuple-element.29), channel_id=1, source_target_pairs={{0,1},{2,3},{4,5},{6,7},{8,9},{10,11},{12,13},{14,15},{16,17},{18,... | collective-permute-start | bytes 196616 | tf_op jit(solution)/shard_map/ppermute | solution.py:335
  13.0 5.4 %collective-permute-start = (bf16[64,512]{1,0:T(8,128)(2,1)S(1)}, bf16[64,512]{1,0:T(8,128)(2,1)S(1)}, u32[]{:S(2)}, u32[]{:S(2)}) collective-permute-start(bf16[64,512]{1,0:T(8,128)(2,1)S(1)} %get-tuple-element.30), channel_id=1, source_target_pairs={{1,2},{3,4},{5,6},{7,8},{9,10},{11,12},{13,14},{15,16},{17,18},{19... | collective-permute-start | bytes 196616 | tf_op jit(solution)/shard_map/ppermute | solution.py:335
  13.7 4.7 %copy-start.1 = (bf16[512,1024]{1,0:T(8,128)(2,1)S(1)}, bf16[512,1024]{1,0:T(8,128)(2,1)}, u32[]{:S(2)}) copy-start(bf16[512,1024]{1,0:T(8,128)(2,1)} %up.1) | copy-start | bytes 3145732
  13.7 4.7 %copy-start.2 = (bf16[1024,512]{1,0:T(8,128)(2,1)S(1)}, bf16[1024,512]{1,0:T(8,128)(2,1)}, u32[]{:S(2)}) copy-start(bf16[1024,512]{1,0:T(8,128)(2,1)} %down.1) | copy-start | bytes 3145732
  13.7 4.7 %copy-start.3 = (bf16[512,512]{1,0:T(8,128)(2,1)S(1)}, bf16[512,512]{1,0:T(8,128)(2,1)}, u32[]{:S(2)}) copy-start(bf16[512,512]{1,0:T(8,128)(2,1)} %msg.1) | copy-start | bytes 1572868
  20.3 10.4 %copy-start.4 = (bf16[512,512]{1,0:T(8,128)(2,1)S(1)}, bf16[512,512]{1,0:T(8,128)(2,1)}, u32[]{:S(2)}) copy-start(bf16[512,512]{1,0:T(8,128)(2,1)} %w_in.1) | copy-start | bytes 1572868
  25.4 21.7 %copy-start.5 = (bf16[512,512]{1,0:T(8,128)(2,1)S(1)}, bf16[512,512]{1,0:T(8,128)(2,1)}, u32[]{:S(2)}) copy-start(bf16[512,512]{1,0:T(8,128)(2,1)} %w_out.1) | copy-start | bytes 1572868
  25.4 21.7 %copy-start.8 = (bf16[128,512]{1,0:T(8,128)(2,1)S(1)}, bf16[128,512]{1,0:T(8,128)(2,1)}, u32[]{:S(2)}) copy-start(bf16[128,512]{1,0:T(8,128)(2,1)} %w_noise.1) | copy-start | bytes 393220
  25.4 21.7 %all-to-all-start.1 = ((bf16[8,64,640]{2,1,0:T(8,128)(2,1)}), bf16[8,64,640]{2,1,0:T(8,128)(2,1)S(1)}, u32[]{:S(2)}, u32[]{:S(2)}) async-start(bf16[8,64,640]{2,1,0:T(8,128)(2,1)} %bitcast.8), calls=%async_computation.1 | async-start | bytes 1310720 | tf_op jit(solution)/shard_map/all_to_all | solution.py:417
  31.1 0.8 copy-start.6
  53.5 4.6 %collective-permute-start.2 = (bf16[32,2,40,128]{3,2,1,0:T(8,128)(2,1)S(1)}, bf16[32,2,40,128]{3,2,1,0:T(8,128)(2,1)S(1)}, u32[]{:S(2)}, u32[]{:S(2)}) collective-permute-start(bf16[32,2,40,128]{3,2,1,0:T(8,128)(2,1)S(1)} %get-tuple-element.24), channel_id=1, source_target_pairs={{0,64},{64,0},{1,65},{65,1},{2,66},{66,2},{3,67},{67,3},{4,68},{68... | collective-permute-start | bytes 1966088 | tf_op jit(solution)/shard_map/ppermute | solution.py:457

commit v8 on v7

--- a/solution.py
+++ b/solution.py
@@ -39,12 +39,16 @@
     return count.astype(BF16)
 
 
-def teach(state, gathered, msg, up, down):
-    resid = state.astype(F32) + jnp.dot(gathered, msg, preferred_element_type=F32)
+def teach(state, gathered, msg, up, down, loads=()):
+    waits = [load.wait for load in loads] or [lambda: None] * 3
+    waits[0]()
+    resid = state.astype(F32) + jnp.dot(gathered, msg[...], preferred_element_type=F32)
     power = jnp.mean(resid * resid, axis=1, keepdims=True)
     normed = (resid * lax.rsqrt(power + 1e-06)).astype(BF16)
-    hidden = jax.nn.silu(jnp.dot(normed, up, preferred_element_type=F32)).astype(BF16)
-    return (resid + jnp.dot(hidden, down, preferred_element_type=F32)).astype(BF16)
+    waits[1]()
+    hidden = jax.nn.silu(jnp.dot(normed, up[...], preferred_element_type=F32)).astype(BF16)
+    waits[2]()
+    return (resid + jnp.dot(hidden, down[...], preferred_element_type=F32)).astype(BF16)
 
 
 def middle_kernel(
@@ -83,8 +87,6 @@
                 preferred_element_type=F32,
             ).astype(BF16)
         )
-    for copy in loads:
-        copy.wait()
     half = (CELLS - 2 * HALO) // 2
     gathered = jnp.concatenate(parts, axis=0)
     writes = []
@@ -92,9 +94,10 @@
         held[at : at + half] = teach(
             state[HALO + at : HALO + at + half],
             gathered[at : at + half],
-            msg[...],
-            up[...],
-            down[...],
+            msg,
+            up,
+            down,
+            loads if k == 0 else (),
         )
         rows = pl.ds(HALO + at, half)
         for target, wait in ((out.at[rows], 2 * k), (sent.at[rows, :D], 2 * k + 1)):
@@ -143,7 +146,7 @@
         axis=0,
     ).astype(BF16)
     ends = jnp.concatenate([state[:HALO], state[CELLS - HALO :]], axis=0)
-    held[...] = teach(ends, gathered, msg[...], up[...], down[...])
+    held[...] = teach(ends, gathered, msg, up, down)
     writes = [
         pltpu.make_async_copy(held.at[:HALO], out.at[:HALO], sem.at[0]),
         pltpu.make_async_copy(held.at[HALO:], out.at[CELLS - HALO :], sem.at[1]),
@@ -156,7 +159,8 @@
         copy.wait()
 
 
-def student_kernel(mine, w_in, early, turned):
+def student_kernel(mine, w_in, w_out, early, turned, w_out_near):
+    w_out_near[...] = w_out[...]
     rows = 256
     for at in range(0, CELLS, rows):
         state = mine[at : at + rows]
@@ -170,22 +174,18 @@
     every,
     w_noise,
     w_out,
-    turned_at,
+    turned,
     place,
     send,
-    keep,
     gst,
     gpre,
-    wide,
-    turned,
     turned_noise,
     shidden,
+    loss_rows,
+    wide,
     slope,
     student,
-    sem,
 ):
-    copy = pltpu.make_async_copy(turned_at, turned, sem)
-    copy.start()
     rows = 256
     for at in range(0, CELLS, rows):
         draws = every[at // BLOCK : (at + rows) // BLOCK, :, D:].reshape(rows, NOISE)
@@ -252,34 +252,41 @@
     spread = jnp.zeros((4, 128), F32)
     for k, piece in enumerate(three(total)):
         spread = spread + jnp.where(lane_ids == at + k * REGIONS, piece, 0.0)
-    spread = jnp.broadcast_to(spread[None], (XY, 4, 128))
-
-    copy.wait()
     back = gst[...].reshape(CELLS, D)
     pull = lax.dot_general(
         back, w_out[...], (((1,), (1,)), ((), ())), preferred_element_type=F32
     )
     gpre[...] = (pull * slope[...]).astype(BF16)
-    for k, target in enumerate((send, keep)):
-        left = pl.multiple_of(jnp.where(place[1] == k, HALF, 0), HALF)
-        d_out = jnp.dot(
-            shidden[...], gst[:, :, pl.ds(left, HALF)].reshape(CELLS, HALF), preferred_element_type=F32
-        )
-        pulled = gpre[:, pl.ds(left, HALF)]
-        d_in = jnp.dot(turned[...], pulled, preferred_element_type=F32)
-        d_noise = jnp.dot(turned_noise[...], pulled, preferred_element_type=F32)
-        for high in range(2):
-            pieces = []
-            for source, count in ((d_in, 8), (d_out, 8), (d_noise, 2)):
-                start = high * XY * count
-                for lane in (0, 128):
-                    pieces.append(
-                        source[start : start + XY * count, lane : lane + 128].reshape(
-                            XY, count, 128
-                        )
-                    )
-            pieces.append(spread)
-            target[:, high] = jnp.concatenate(pieces, axis=1).astype(BF16)
+    theirs = pl.multiple_of(jnp.where(place[1] == 0, HALF, 0), HALF)
+    half_of_grads(theirs, turned, turned_noise, shidden, gst, gpre, spread, send)
+    loss_rows[...] = spread
+
+
+def half_of_grads(left, turned, turned_noise, shidden, gst, gpre, spread, target):
+    spread = jnp.broadcast_to(spread[None], (XY, 4, 128))
+    d_out = jnp.dot(
+        shidden[...],
+        gst[:, :, pl.ds(left, HALF)].reshape(CELLS, HALF),
+        preferred_element_type=F32,
+    )
+    pulled = gpre[:, pl.ds(left, HALF)]
+    d_in = jnp.dot(turned[...], pulled, preferred_element_type=F32)
+    d_noise = jnp.dot(turned_noise[...], pulled, preferred_element_type=F32)
+    for high in range(2):
+        pieces = []
+        for source, count in ((d_in, 8), (d_out, 8), (d_noise, 2)):
+            start = high * XY * count
+            for lane in (0, 128):
+                pieces.append(
+                    source[start : start + XY * count, lane : lane + 128].reshape(XY, count, 128)
+                )
+        pieces.append(spread)
+        target[:, high] = jnp.concatenate(pieces, axis=1).astype(BF16)
+
+
+def keep_kernel(turned, turned_noise, shidden, gst, gpre, loss_rows, place, keep):
+    ours = pl.multiple_of(jnp.where(place[1] == 0, 0, HALF), HALF)
+    half_of_grads(ours, turned, turned_noise, shidden, gst, gpre, loss_rows[...], keep)
 
 
 def three(value):
@@ -427,33 +434,43 @@
         out_shape=(
             jax.ShapeDtypeStruct((CELLS, H), F32),
             jax.ShapeDtypeStruct((D, CELLS), BF16),
+            jax.ShapeDtypeStruct((H, D), BF16),
         ),
-        in_specs=[VMEM] * 2,
-        out_specs=[VMEM] * 2,
+        in_specs=[VMEM] * 3,
+        out_specs=[VMEM] * 3,
         compiler_params=PARAMS,
         name="student",
     )
-    early, turned = pupil(mine, student_in)
+    early, turned, w_out_near = pupil(mine, student_in, student_out)
     place = jnp.stack([region_map[0], lax.axis_index("core").astype(jnp.int32)])
-    send, keep = pl.pallas_call(
+    send, gst, gpre, turned_noise, shidden, loss_rows = pl.pallas_call(
         score_kernel,
-        out_shape=[jax.ShapeDtypeStruct((XY, 2, SHARE, 128), BF16)] * 2,
-        in_specs=[VMEM] * 5 + [HBM, pl.BlockSpec(memory_space=pltpu.SMEM)],
-        out_specs=[VMEM] * 2,
+        out_shape=[
+            jax.ShapeDtypeStruct((XY, 2, SHARE, 128), BF16),
+            jax.ShapeDtypeStruct((MEMBERS, BLOCK, D), BF16),
+            jax.ShapeDtypeStruct((CELLS, D), BF16),
+            jax.ShapeDtypeStruct((NOISE, CELLS), BF16),
+            jax.ShapeDtypeStruct((H, CELLS), BF16),
+            jax.ShapeDtypeStruct((4, 128), F32),
+        ],
+        in_specs=[VMEM] * 6 + [pl.BlockSpec(memory_space=pltpu.SMEM)],
+        out_specs=[VMEM] * 6,
         scratch_shapes=[
-            pltpu.VMEM((MEMBERS, BLOCK, D), BF16),
-            pltpu.VMEM((CELLS, D), BF16),
             pltpu.VMEM((16, 128), F32),
-            pltpu.VMEM((D, CELLS), BF16),
-            pltpu.VMEM((NOISE, CELLS), BF16),
-            pltpu.VMEM((H, CELLS), BF16),
             pltpu.VMEM((CELLS, H), F32),
             pltpu.VMEM((CELLS, D), BF16),
-            pltpu.SemaphoreType.DMA,
         ],
         compiler_params=PARAMS,
         name="score",
-    )(early, mine, every, student_noise, student_out, in_hbm(turned), place)
+    )(early, mine, every, student_noise, w_out_near, turned, place)
+    keep = pl.pallas_call(
+        keep_kernel,
+        out_shape=jax.ShapeDtypeStruct((XY, 2, SHARE, 128), BF16),
+        in_specs=[VMEM] * 6 + [pl.BlockSpec(memory_space=pltpu.SMEM)],
+        out_specs=VMEM,
+        compiler_params=PARAMS,
+        name="keep",
+    )(turned, turned_noise, shidden, gst, gpre, loss_rows, place)
     other = lax.ppermute(send, "core", [(0, 1), (1, 0)])
     half = (keep.astype(F32) + other.astype(F32)).astype(BF16)
     shares = lax.all_to_all(half, ("tile_1", "tile_2"), split_axis=0, concat_axis=0, tiled=True)

time: 105 us -> 106 us (level)
  local copies, waits for them, and re-layouts: 0.85 us -> 2.95 us
  waiting for transfers between devices: 22 us -> 20.6 us
    unnamed x20 -> x22, local copies, waits for them, and re-layouts: 0.84 us -> 2.94 us
    pallas_call x1 -> x2, Pallas kernels: 0.43 us -> 1.53 us  [the longest x1 1.07 us: step(): pl.pallas_call(keep_kernel, out_shape=jax.ShapeDtypeStruct((XY, 2, SHARE,...]
    all_to_all x1, waiting for transfers between devices: 15.2 us -> 14.1 us  [step(): lax.all_to_all(sent.reshape(MEMBERS, BLOCK, D + NOISE), MEMBER, split_axi...]
    ppermute x1, waiting for transfers between devices: 1.7 us -> 0.63 us  [step(): other = lax.ppermute(send, 'core', [(0, 1), (1, 0)])]
where the time goes in v8:
time: 106 us; the launch traced here: 105 us
  blocking collectives  45.5 us (43%)
  waiting for transfers between devices  20.6 us (19%)
  starting transfers between devices  20.4 us (19%)
  Pallas kernels  14 us (13%)
  local copies, waits for them, and re-layouts  2.95 us (3%)
  between operations  1.48 us (1%)
    all_to_all x1, blocking collectives, step(): lax.all_to_all(half, ('tile_1', 'tile_2'), split_axis=0, concat_axis=0, t...  28.2 us
    all_to_all x1, blocking collectives, step(): lax.all_to_all(copies, ('tile_0', 'member_0', 'core'), split_axis=0, conc...  17.3 us
    all_to_all x1, waiting for transfers between devices, step(): lax.all_to_all(sent.reshape(MEMBERS, BLOCK, D + NOISE), MEMBER, split_axi...  14.1 us
    all_to_all x1, starting transfers between devices, step(): lax.all_to_all(state.reshape(MEMBERS, BLOCK, D), MEMBER, split_axis=0, co...  10.4 us
    pallas_call x1, Pallas kernels, step(): pl.pallas_call(score_kernel, out_shape=[jax.ShapeDtypeStruct((XY, 2, SHAR...  5.81 us
    all_to_all x1, waiting for transfers between devices, step(): lax.all_to_all(state.reshape(MEMBERS, BLOCK, D), MEMBER, split_axis=0, co...  5.81 us
    all_to_all x1, starting transfers between devices, step(): lax.all_to_all(sent.reshape(MEMBERS, BLOCK, D + NOISE), MEMBER, split_axi...  4.54 us
    pallas_call x1, Pallas kernels, step(): middle(state, noise[0], neighbours, in_hbm(msg_weight), in_hbm(up_weight)...  3.91 us
  transfers between devices with their start and end apart: 5, of which 3 were waited for; matrix products, arithmetic and copies ran while one was open for 0% of the time, Pallas kernels for 7%

profile of v8, /device:TPU:1, one launch (start us, length us, event | category | flops | bytes accessed | tf_op | source)
XLA Modules:
  0.0 105.1 jit_solution(11274720487571340613)
XLA Ops:
  0.7 10.4 %all-to-all-start = ((bf16[8,64,512]{2,1,0:T(8,128)(2,1)}), bf16[8,64,512]{2,1,0:T(8,128)(2,1)S(1)}, u32[]{:S(2)}, u32[]{:S(2)}) async-start(bf16[8,64,512]{2,1,0:T(8,128)(2,1)} %bitcast.13), calls=%async_computation | async-start | bytes 1048576 | tf_op jit(solution)/shard_map/all_to_all | solution.py:367
  11.1 1.9 %collective-permute-start.1 = (bf16[64,512]{1,0:T(8,128)(2,1)S(1)}, bf16[64,512]{1,0:T(8,128)(2,1)S(1)}, u32[]{:S(2)}, u32[]{:S(2)}) collective-permute-start(bf16[64,512]{1,0:T(8,128)(2,1)S(1)} %get-tuple-element.39), channel_id=1, source_target_pairs={{0,1},{2,3},{4,5},{6,7},{8,9},{10,11},{12,13},{14,15},{16,17},{18,... | collective-permute-start | bytes 196616 | tf_op jit(solution)/shard_map/ppermute | solution.py:342
  13.0 0.7 collective-permute-start
  13.7 0.0 copy-start.1
  13.7 3.9 %middle.1 = (bf16[512,512]{1,0:T(8,128)(2,1)}, bf16[512,640]{1,0:T(8,128)(2,1)}) custom-call(bf16[512,512]{1,0:T(8,128)(2,1)S(1)} %bitcast.14, bf16[512,128]{1,0:T(8,128)(2,1)S(1)} %bitcast.18, s32[8,512]{1,0:T(8,128)S(1)} %copy-done.10, bf16[512,512]{1,0:T(8,128)(2,1)} %msg.1, bf16[512,1024]{1,0:T(8,128)(2,1)} %up.1, bf16[1024,512]{1,0:T(8,128)(2,1)} %down.1), custom_call_target="tpu_custom_call" | custom-call | tf_op jit(solution)/shard_map/middle/pallas_call | solution.py:404
  17.7 1.9 %edges.1 = (bf16[512,512]{1,0:T(8,128)(2,1)}, bf16[512,640]{1,0:T(8,128)(2,1)}) custom-call(bf16[64,512]{1,0:T(8,128)(2,1)S(1)} %collective-permute-done.odd_swap, bf16[64,512]{1,0:T(8,128)(2,1)S(1)} %collective-permute-done.1.even_swap, bf16[512,512]{1,0:T(8,128)(2,1)S(1)} %bitcast.15, ...), custom_call_target="tpu_custom_call", output_to_operand_aliasing={{0}: (7, {}), {1}: (8, {})} | custom-call | tf_op jit(solution)/shard_map/edges/pallas_call | solution.py:412
  19.6 0.0 copy-start.4
  19.6 5.8 %all-to-all-done = bf16[8,64,512]{2,1,0:T(8,128)(2,1)S(1)} async-done(((bf16[8,64,512]{2,1,0:T(8,128)(2,1)}), bf16[8,64,512]{2,1,0:T(8,128)(2,1)S(1)}, u32[]{:S(2)}, u32[]{:S(2)}) %all-to-all-start) | async-done | bytes 524320 | tf_op jit(solution)/shard_map/all_to_all | solution.py:367
  25.4 4.5 %all-to-all-start.1 = ((bf16[8,64,640]{2,1,0:T(8,128)(2,1)}), bf16[8,64,640]{2,1,0:T(8,128)(2,1)S(1)}, u32[]{:S(2)}, u32[]{:S(2)}) async-start(bf16[8,64,640]{2,1,0:T(8,128)(2,1)} %bitcast.8), calls=%async_computation.1 | async-start | bytes 1310720 | tf_op jit(solution)/shard_map/all_to_all | solution.py:424
  30.6 0.1 pad_add_fusion.place
  30.7 1.0 copy-done.5
  31.7 0.5 student.1
  32.2 0.8 copy-done.6
  33.0 14.1 %all-to-all-done.1.every = bf16[8,64,640]{2,1,0:T(8,128)(2,1)S(1)} async-done(((bf16[8,64,640]{2,1,0:T(8,128)(2,1)}), bf16[8,64,640]{2,1,0:T(8,128)(2,1)S(1)}, u32[]{:S(2)}, u32[]{:S(2)}) %all-to-all-start.1) | async-done | bytes 655392 | tf_op jit(solution)/shard_map/all_to_all | solution.py:424
  47.2 1.0 copy-done.7
  48.2 5.8 %score.1 = (bf16[32,2,40,128]{3,2,1,0:T(8,128)(2,1)S(1)}, bf16[8,64,512]{2,1,0:T(8,128)(2,1)S(1)}, bf16[512,512]{1,0:T(8,128)(2,1)S(1)}, bf16[128,512]{1,0:T(8,1...) custom-call(f32[512,512]{1,0:T(8,128)S(1)} %get-tuple-element.26.early, bf16[512,512]{1,0:T(8,128)(2,1)S(1)} %bitcast.17, ...), custom_call_target="tpu_custom_call" | custom-call | tf_op jit(solution)/shard_map/score/pallas_call | solution.py:446
  54.0 2.9 %collective-permute-start.2 = (bf16[32,2,40,128]{3,2,1,0:T(8,128)(2,1)S(1)}, bf16[32,2,40,128]{3,2,1,0:T(8,128)(2,1)S(1)}, u32[]{:S(2)}, u32[]{:S(2)}) collective-permute-start(bf16[32,2,40,128]{3,2,1,0:T(8,128)(2,1)S(1)} %get-tuple-element.34), channel_id=1, source_target_pairs={{0,64},{64,0},{1,65},{65,1},{2,66},{66,2},{3,67},{67,3},{4,68},{68... | collective-permute-start | bytes 1966088 | tf_op jit(solution)/shard_map/ppermute | solution.py:474
  56.9 1.1 %keep.1 = bf16[32,2,40,128]{3,2,1,0:T(8,128)(2,1)S(1)} custom-call(bf16[512,512]{1,0:T(8,128)(2,1)S(1)} %get-tuple-element.25.turned, bf16[128,512]{1,0:T(8,128)(2,1)S(1)} %get-tuple-element.29.turned_noise, bf16[512,512]{1,0:T(8,128)(2,1)S(1)} %get-tuple-element.30.shidden, bf16[8,64,512]{2,1,0:T(8,128)(2,1)S(1)} %get-tuple-element.31.gst, ...), custom_call_target="tpu_custom_call" | custom-call | tf_op jit(solution)/shard_map/keep/pallas_call | solution.py:466
  58.0 0.6 collective-permute-done.2
  58.6 0.2 add_convert_fusion
  58.8 28.2 %all_to_all.20.arrived = bf16[32,2,40,128]{3,2,1,0:T(8,128)(2,1)S(1)} all-to-all(bf16[32,2,40,128]{3,2,1,0:T(8,128)(2,1)S(1)} %add_convert_fusion), channel_id=1, replica_groups=mesh['member_0'=4,'core'=2,'tile_0'=2,'tile_1'=4,'tile_2'=8] {'tile_1','..., dimensions={0} | all-to-all | bytes 1310720 | tf_op jit(solution)/shard_map/all_to_all | solution.py:476
  87.0 0.2 fold.1
  87.2 17.3 %all_to_all.21.arrived = bf16[16,40,128]{2,1,0:T(8,128)(2,1)S(1)} all-to-all(bf16[16,40,128]{2,1,0:T(8,128)(2,1)S(1)} %fold.1), channel_id=1, replica_groups=mesh['member_0'=4,'core'=2,'tile_0'=2,'tile_1'=4,'tile_2'=8] {'tile_0','..., dimensions={0} | all-to-all | bytes 327680 | tf_op jit(solution)/shard_map/all_to_all | solution.py:485
  104.5 0.6 last.1
  (20 shorter events, 0.1 us)
Async XLA Ops:
  0.6 10.4 %copy-start = (bf16[1,512,512]{2,1,0:T(8,128)(2,1)S(1)}, bf16[1,512,512]{2,1,0:T(8,128)(2,1)}, u32[]{:S(2)}) copy-start(bf16[1,512,512]{2,1,0:T(8,128)(2,1)} %param.10) | copy-start | bytes 1572868
  0.6 13.0 %copy-start.10 = (s32[8,512]{1,0:T(8,128)S(1)}, s32[8,512]{1,0:T(8,128)}, u32[]{:S(2)}) copy-start(s32[8,512]{1,0:T(8,128)} %near.3) | copy-start | bytes 49156
  0.7 13.0 %copy-start.8 = (bf16[1,512,128]{2,1,0:T(8,128)(2,1)S(1)}, bf16[1,512,128]{2,1,0:T(8,128)(2,1)}, u32[]{:S(2)}) copy-start(bf16[1,512,128]{2,1,0:T(8,128)(2,1)} %param.11) | copy-start | bytes 393220
  0.7 24.8 %all-to-all-start = ((bf16[8,64,512]{2,1,0:T(8,128)(2,1)}), bf16[8,64,512]{2,1,0:T(8,128)(2,1)S(1)}, u32[]{:S(2)}, u32[]{:S(2)}) async-start(bf16[8,64,512]{2,1,0:T(8,128)(2,1)} %bitcast.13), calls=%async_computation | async-start | bytes 1048576 | tf_op jit(solution)/shard_map/all_to_all | solution.py:367
  11.1 6.6 %collective-permute-start.1 = (bf16[64,512]{1,0:T(8,128)(2,1)S(1)}, bf16[64,512]{1,0:T(8,128)(2,1)S(1)}, u32[]{:S(2)}, u32[]{:S(2)}) collective-permute-start(bf16[64,512]{1,0:T(8,128)(2,1)S(1)} %get-tuple-element.39), channel_id=1, source_target_pairs={{0,1},{2,3},{4,5},{6,7},{8,9},{10,11},{12,13},{14,15},{16,17},{18,... | collective-permute-start | bytes 196616 | tf_op jit(solution)/shard_map/ppermute | solution.py:342
  13.0 4.7 %collective-permute-start = (bf16[64,512]{1,0:T(8,128)(2,1)S(1)}, bf16[64,512]{1,0:T(8,128)(2,1)S(1)}, u32[]{:S(2)}, u32[]{:S(2)}) collective-permute-start(bf16[64,512]{1,0:T(8,128)(2,1)S(1)} %get-tuple-element.40), channel_id=1, source_target_pairs={{1,2},{3,4},{5,6},{7,8},{9,10},{11,12},{13,14},{15,16},{17,18},{19... | collective-permute-start | bytes 196616 | tf_op jit(solution)/shard_map/ppermute | solution.py:342
  13.7 4.0 %copy-start.1 = (bf16[512,1024]{1,0:T(8,128)(2,1)S(1)}, bf16[512,1024]{1,0:T(8,128)(2,1)}, u32[]{:S(2)}) copy-start(bf16[512,1024]{1,0:T(8,128)(2,1)} %up.1) | copy-start | bytes 3145732
  13.7 4.0 %copy-start.2 = (bf16[1024,512]{1,0:T(8,128)(2,1)S(1)}, bf16[1024,512]{1,0:T(8,128)(2,1)}, u32[]{:S(2)}) copy-start(bf16[1024,512]{1,0:T(8,128)(2,1)} %down.1) | copy-start | bytes 3145732
  13.7 4.0 %copy-start.3 = (bf16[512,512]{1,0:T(8,128)(2,1)S(1)}, bf16[512,512]{1,0:T(8,128)(2,1)}, u32[]{:S(2)}) copy-start(bf16[512,512]{1,0:T(8,128)(2,1)} %msg.1) | copy-start | bytes 1572868
  19.6 11.1 %copy-start.4 = (bf16[512,512]{1,0:T(8,128)(2,1)S(1)}, bf16[512,512]{1,0:T(8,128)(2,1)}, u32[]{:S(2)}) copy-start(bf16[512,512]{1,0:T(8,128)(2,1)} %w_in.1) | copy-start | bytes 1572868
  25.4 21.7 %copy-start.9 = (bf16[128,512]{1,0:T(8,128)(2,1)S(1)}, bf16[128,512]{1,0:T(8,128)(2,1)}, u32[]{:S(2)}) copy-start(bf16[128,512]{1,0:T(8,128)(2,1)} %w_noise.1) | copy-start | bytes 393220
  25.4 21.7 %all-to-all-start.1 = ((bf16[8,64,640]{2,1,0:T(8,128)(2,1)}), bf16[8,64,640]{2,1,0:T(8,128)(2,1)S(1)}, u32[]{:S(2)}, u32[]{:S(2)}) async-start(bf16[8,64,640]{2,1,0:T(8,128)(2,1)} %bitcast.8), calls=%async_computation.1 | async-start | bytes 1310720 | tf_op jit(solution)/shard_map/all_to_all | solution.py:424
  30.7 1.0 copy-start.5
  32.2 0.8 copy-start.6
  47.2 1.0 copy-start.7
  54.0 4.6 %collective-permute-start.2 = (bf16[32,2,40,128]{3,2,1,0:T(8,128)(2,1)S(1)}, bf16[32,2,40,128]{3,2,1,0:T(8,128)(2,1)S(1)}, u32[]{:S(2)}, u32[]{:S(2)}) collective-permute-start(bf16[32,2,40,128]{3,2,1,0:T(8,128)(2,1)S(1)} %get-tuple-element.34), channel_id=1, source_target_pairs={{0,64},{64,0},{1,65},{65,1},{2,66},{66,2},{3,67},{67,3},{4,68},{68... | collective-permute-start | bytes 1966088 | tf_op jit(solution)/shard_map/ppermute | solution.py:474

commit v9 on v8

--- a/solution.py
+++ b/solution.py
@@ -159,8 +159,7 @@
         copy.wait()
 
 
-def student_kernel(mine, w_in, w_out, early, turned, w_out_near):
-    w_out_near[...] = w_out[...]
+def student_kernel(mine, w_in, early, turned):
     rows = 256
     for at in range(0, CELLS, rows):
         state = mine[at : at + rows]
@@ -173,19 +172,29 @@
     mine,
     every,
     w_noise,
-    w_out,
-    turned,
+    w_out_at,
+    turned_at,
     place,
     send,
     gst,
     gpre,
+    turned,
     turned_noise,
     shidden,
     loss_rows,
     wide,
     slope,
     student,
+    hidden,
+    w_out,
+    sem,
 ):
+    copies = [
+        pltpu.make_async_copy(w_out_at, w_out, sem.at[0]),
+        pltpu.make_async_copy(turned_at, turned, sem.at[1]),
+    ]
+    for copy in copies:
+        copy.start()
     rows = 256
     for at in range(0, CELLS, rows):
         draws = every[at // BLOCK : (at + rows) // BLOCK, :, D:].reshape(rows, NOISE)
@@ -194,13 +203,16 @@
         )
         sig = jax.nn.sigmoid(preact)
         hid = (preact * sig).astype(BF16)
+        hidden[at : at + rows] = hid
         slope[at : at + rows] = sig * (1.0 + preact * (1.0 - sig))
+        shidden[:, at : at + rows] = hid.T
+        turned_noise[:, at : at + rows] = draws.T
+    copies[0].wait()
+    for at in range(0, CELLS, rows):
         student[at : at + rows] = (
             mine[at : at + rows].astype(F32)
-            + jnp.dot(hid, w_out[...], preferred_element_type=F32)
+            + jnp.dot(hidden[at : at + rows], w_out[...], preferred_element_type=F32)
         ).astype(BF16)
-        shidden[:, at : at + rows] = hid.T
-        turned_noise[:, at : at + rows] = draws.T
 
     step = 16
     wide[...] = jnp.zeros_like(wide)
@@ -252,6 +264,7 @@
     spread = jnp.zeros((4, 128), F32)
     for k, piece in enumerate(three(total)):
         spread = spread + jnp.where(lane_ids == at + k * REGIONS, piece, 0.0)
+    copies[1].wait()
     back = gst[...].reshape(CELLS, D)
     pull = lax.dot_general(
         back, w_out[...], (((1,), (1,)), ((), ())), preferred_element_type=F32
@@ -434,35 +447,38 @@
         out_shape=(
             jax.ShapeDtypeStruct((CELLS, H), F32),
             jax.ShapeDtypeStruct((D, CELLS), BF16),
-            jax.ShapeDtypeStruct((H, D), BF16),
         ),
-        in_specs=[VMEM] * 3,
-        out_specs=[VMEM] * 3,
+        in_specs=[VMEM] * 2,
+        out_specs=[VMEM] * 2,
         compiler_params=PARAMS,
         name="student",
     )
-    early, turned, w_out_near = pupil(mine, student_in, student_out)
+    early, turned_far = pupil(mine, student_in)
     place = jnp.stack([region_map[0], lax.axis_index("core").astype(jnp.int32)])
-    send, gst, gpre, turned_noise, shidden, loss_rows = pl.pallas_call(
+    send, gst, gpre, turned, turned_noise, shidden, loss_rows = pl.pallas_call(
         score_kernel,
         out_shape=[
             jax.ShapeDtypeStruct((XY, 2, SHARE, 128), BF16),
             jax.ShapeDtypeStruct((MEMBERS, BLOCK, D), BF16),
             jax.ShapeDtypeStruct((CELLS, D), BF16),
+            jax.ShapeDtypeStruct((D, CELLS), BF16),
             jax.ShapeDtypeStruct((NOISE, CELLS), BF16),
             jax.ShapeDtypeStruct((H, CELLS), BF16),
             jax.ShapeDtypeStruct((4, 128), F32),
         ],
-        in_specs=[VMEM] * 6 + [pl.BlockSpec(memory_space=pltpu.SMEM)],
-        out_specs=[VMEM] * 6,
+        in_specs=[VMEM] * 4 + [HBM] * 2 + [pl.BlockSpec(memory_space=pltpu.SMEM)],
+        out_specs=[VMEM] * 7,
         scratch_shapes=[
             pltpu.VMEM((16, 128), F32),
             pltpu.VMEM((CELLS, H), F32),
             pltpu.VMEM((CELLS, D), BF16),
+            pltpu.VMEM((CELLS, H), BF16),
+            pltpu.VMEM((H, D), BF16),
+            pltpu.SemaphoreType.DMA((2,)),
         ],
         compiler_params=PARAMS,
         name="score",
-    )(early, mine, every, student_noise, w_out_near, turned, place)
+    )(early, mine, every, student_noise, in_hbm(student_out), in_hbm(turned_far), place)
     keep = pl.pallas_call(
         keep_kernel,
         out_shape=jax.ShapeDtypeStruct((XY, 2, SHARE, 128), BF16),

time: 106 us -> 105 us (level)
  local copies, waits for them, and re-layouts: 2.95 us -> 0.86 us
    unnamed x22 -> x18, local copies, waits for them, and re-layouts: 2.94 us -> 0.85 us
    all_to_all x1, waiting for transfers between devices: 14.1 us -> 15.2 us  [step(): lax.all_to_all(sent.reshape(MEMBERS, BLOCK, D + NOISE), MEMBER, split_axi...]
where the time goes in v9:
time: 105 us
  blocking collectives  45.5 us (43%)
  waiting for transfers between devices  21.6 us (21%)
  starting transfers between devices  20.4 us (19%)
  Pallas kernels  14.8 us (14%)
  between operations  1.48 us (1%)
    all_to_all x1, blocking collectives, step(): lax.all_to_all(half, ('tile_1', 'tile_2'), split_axis=0, concat_axis=0, t...  28.2 us
    all_to_all x1, blocking collectives, step(): lax.all_to_all(copies, ('tile_0', 'member_0', 'core'), split_axis=0, conc...  17.3 us
    all_to_all x1, waiting for transfers between devices, step(): lax.all_to_all(sent.reshape(MEMBERS, BLOCK, D + NOISE), MEMBER, split_axi...  15.2 us
    all_to_all x1, starting transfers between devices, step(): lax.all_to_all(state.reshape(MEMBERS, BLOCK, D), MEMBER, split_axis=0, co...  10.4 us
    pallas_call x1, Pallas kernels, step(): pl.pallas_call(score_kernel, out_shape=[jax.ShapeDtypeStruct((XY, 2, SHAR...  6.64 us
    all_to_all x1, waiting for transfers between devices, step(): lax.all_to_all(state.reshape(MEMBERS, BLOCK, D), MEMBER, split_axis=0, co...  5.8 us
    all_to_all x1, starting transfers between devices, step(): lax.all_to_all(sent.reshape(MEMBERS, BLOCK, D + NOISE), MEMBER, split_axi...  4.54 us
    pallas_call x1, Pallas kernels, step(): middle(state, noise[0], neighbours, in_hbm(msg_weight), in_hbm(up_weight)...  3.92 us
  transfers between devices with their start and end apart: 5, of which 3 were waited for; matrix products, arithmetic and copies ran while one was open for 0% of the time, Pallas kernels for 7%

profile of v9, /device:TPU:1, one launch (start us, length us, event | category | flops | bytes accessed | tf_op | source)
XLA Modules:
  0.0 104.9 jit_solution(16123618045998548118)
XLA Ops:
  0.7 10.4 %all-to-all-start = ((bf16[8,64,512]{2,1,0:T(8,128)(2,1)}), bf16[8,64,512]{2,1,0:T(8,128)(2,1)S(1)}, u32[]{:S(2)}, u32[]{:S(2)}) async-start(bf16[8,64,512]{2,1,0:T(8,128)(2,1)} %bitcast.13), calls=%async_computation | async-start | bytes 1048576 | tf_op jit(solution)/shard_map/all_to_all | solution.py:380
  11.1 1.9 %collective-permute-start.1 = (bf16[64,512]{1,0:T(8,128)(2,1)S(1)}, bf16[64,512]{1,0:T(8,128)(2,1)S(1)}, u32[]{:S(2)}, u32[]{:S(2)}) collective-permute-start(bf16[64,512]{1,0:T(8,128)(2,1)S(1)} %get-tuple-element.39), channel_id=1, source_target_pairs={{0,1},{2,3},{4,5},{6,7},{8,9},{10,11},{12,13},{14,15},{16,17},{18,... | collective-permute-start | bytes 196616 | tf_op jit(solution)/shard_map/ppermute | solution.py:355
  13.0 0.7 collective-permute-start
  13.7 0.0 copy-start.1
  13.7 0.0 copy-start.2
  13.7 0.0 copy-start.3
  13.7 3.9 %middle.1 = (bf16[512,512]{1,0:T(8,128)(2,1)}, bf16[512,640]{1,0:T(8,128)(2,1)}) custom-call(bf16[512,512]{1,0:T(8,128)(2,1)S(1)} %bitcast.14, bf16[512,128]{1,0:T(8,128)(2,1)S(1)} %bitcast.18, s32[8,512]{1,0:T(8,128)S(1)} %copy-done.8, bf16[512,512]{1,0:T(8,128)(2,1)} %msg.1, bf16[512,1024]{1,0:T(8,128)(2,1)} %up.1, bf16[1024,512]{1,0:T(8,128)(2,1)} %down.1), custom_call_target="tpu_custom_call" | custom-call | tf_op jit(solution)/shard_map/middle/pallas_call | solution.py:417
  17.7 1.9 %edges.1 = (bf16[512,512]{1,0:T(8,128)(2,1)}, bf16[512,640]{1,0:T(8,128)(2,1)}) custom-call(bf16[64,512]{1,0:T(8,128)(2,1)S(1)} %collective-permute-done.odd_swap, bf16[64,512]{1,0:T(8,128)(2,1)S(1)} %collective-permute-done.1.even_swap, bf16[512,512]{1,0:T(8,128)(2,1)S(1)} %bitcast.15, ...), custom_call_target="tpu_custom_call", output_to_operand_aliasing={{0}: (7, {}), {1}: (8, {})} | custom-call | tf_op jit(solution)/shard_map/edges/pallas_call | solution.py:425
  19.6 0.0 copy-start.4
  19.6 5.8 %all-to-all-done = bf16[8,64,512]{2,1,0:T(8,128)(2,1)S(1)} async-done(((bf16[8,64,512]{2,1,0:T(8,128)(2,1)}), bf16[8,64,512]{2,1,0:T(8,128)(2,1)S(1)}, u32[]{:S(2)}, u32[]{:S(2)}) %all-to-all-start) | async-done | bytes 524320 | tf_op jit(solution)/shard_map/all_to_all | solution.py:380
  25.4 4.5 %all-to-all-start.1 = ((bf16[8,64,640]{2,1,0:T(8,128)(2,1)}), bf16[8,64,640]{2,1,0:T(8,128)(2,1)S(1)}, u32[]{:S(2)}, u32[]{:S(2)}) async-start(bf16[8,64,640]{2,1,0:T(8,128)(2,1)} %bitcast.8), calls=%async_computation.1 | async-start | bytes 1310720 | tf_op jit(solution)/shard_map/all_to_all | solution.py:437
  30.6 0.1 pad_add_fusion.place
  30.7 0.4 student.1
  31.2 0.8 copy-done.5
  32.0 15.2 %all-to-all-done.1.every = bf16[8,64,640]{2,1,0:T(8,128)(2,1)S(1)} async-done(((bf16[8,64,640]{2,1,0:T(8,128)(2,1)}), bf16[8,64,640]{2,1,0:T(8,128)(2,1)S(1)}, u32[]{:S(2)}, u32[]{:S(2)}) %all-to-all-start.1) | async-done | bytes 655392 | tf_op jit(solution)/shard_map/all_to_all | solution.py:437
  47.2 6.6 %score.1 = (bf16[32,2,40,128]{3,2,1,0:T(8,128)(2,1)S(1)}, bf16[8,64,512]{2,1,0:T(8,128)(2,1)S(1)}, bf16[512,512]{1,0:T(8,128)(2,1)S(1)}, bf16[512,512]{1,0:T(8,1...) custom-call(f32[512,512]{1,0:T(8,128)S(1)} %get-tuple-element.25.early, ...), custom_call_target="tpu_custom_call" | custom-call | tf_op jit(solution)/shard_map/score/pallas_call | solution.py:458
  53.8 2.9 %collective-permute-start.2 = (bf16[32,2,40,128]{3,2,1,0:T(8,128)(2,1)S(1)}, bf16[32,2,40,128]{3,2,1,0:T(8,128)(2,1)S(1)}, u32[]{:S(2)}, u32[]{:S(2)}) collective-permute-start(bf16[32,2,40,128]{3,2,1,0:T(8,128)(2,1)S(1)} %get-tuple-element.34), channel_id=1, source_target_pairs={{0,64},{64,0},{1,65},{65,1},{2,66},{66,2},{3,67},{67,3},{4,68},{68... | collective-permute-start | bytes 1966088 | tf_op jit(solution)/shard_map/ppermute | solution.py:490
  56.7 1.1 %keep.1 = bf16[32,2,40,128]{3,2,1,0:T(8,128)(2,1)S(1)} custom-call(bf16[512,512]{1,0:T(8,128)(2,1)S(1)} %get-tuple-element.28.turned, bf16[128,512]{1,0:T(8,128)(2,1)S(1)} %get-tuple-element.29.turned_noise, bf16[512,512]{1,0:T(8,128)(2,1)S(1)} %get-tuple-element.30.shidden, bf16[8,64,512]{2,1,0:T(8,128)(2,1)S(1)} %get-tuple-element.31.gst, ...), custom_call_target="tpu_custom_call" | custom-call | tf_op jit(solution)/shard_map/keep/pallas_call | solution.py:482
  57.8 0.6 collective-permute-done.2
  58.4 0.2 add_convert_fusion
  58.6 28.2 %all_to_all.20.arrived = bf16[32,2,40,128]{3,2,1,0:T(8,128)(2,1)S(1)} all-to-all(bf16[32,2,40,128]{3,2,1,0:T(8,128)(2,1)S(1)} %add_convert_fusion), channel_id=1, replica_groups=mesh['member_0'=4,'core'=2,'tile_0'=2,'tile_1'=4,'tile_2'=8] {'tile_1','..., dimensions={0} | all-to-all | bytes 1310720 | tf_op jit(solution)/shard_map/all_to_all | solution.py:492
  86.8 0.2 fold.1
  87.0 17.3 %all_to_all.21.arrived = bf16[16,40,128]{2,1,0:T(8,128)(2,1)S(1)} all-to-all(bf16[16,40,128]{2,1,0:T(8,128)(2,1)S(1)} %fold.1), channel_id=1, replica_groups=mesh['member_0'=4,'core'=2,'tile_0'=2,'tile_1'=4,'tile_2'=8] {'tile_0','..., dimensions={0} | all-to-all | bytes 327680 | tf_op jit(solution)/shard_map/all_to_all | solution.py:501
  104.2 0.6 last.1
  (16 shorter events, 0.0 us)
Async XLA Ops:
  0.6 10.4 %copy-start = (bf16[1,512,512]{2,1,0:T(8,128)(2,1)S(1)}, bf16[1,512,512]{2,1,0:T(8,128)(2,1)}, u32[]{:S(2)}) copy-start(bf16[1,512,512]{2,1,0:T(8,128)(2,1)} %param.10) | copy-start | bytes 1572868
  0.6 13.0 %copy-start.8 = (s32[8,512]{1,0:T(8,128)S(1)}, s32[8,512]{1,0:T(8,128)}, u32[]{:S(2)}) copy-start(s32[8,512]{1,0:T(8,128)} %near.3) | copy-start | bytes 49156
  0.7 13.0 %copy-start.6 = (bf16[1,512,128]{2,1,0:T(8,128)(2,1)S(1)}, bf16[1,512,128]{2,1,0:T(8,128)(2,1)}, u32[]{:S(2)}) copy-start(bf16[1,512,128]{2,1,0:T(8,128)(2,1)} %param.11) | copy-start | bytes 393220
  0.7 24.8 %all-to-all-start = ((bf16[8,64,512]{2,1,0:T(8,128)(2,1)}), bf16[8,64,512]{2,1,0:T(8,128)(2,1)S(1)}, u32[]{:S(2)}, u32[]{:S(2)}) async-start(bf16[8,64,512]{2,1,0:T(8,128)(2,1)} %bitcast.13), calls=%async_computation | async-start | bytes 1048576 | tf_op jit(solution)/shard_map/all_to_all | solution.py:380
  11.1 6.6 %collective-permute-start.1 = (bf16[64,512]{1,0:T(8,128)(2,1)S(1)}, bf16[64,512]{1,0:T(8,128)(2,1)S(1)}, u32[]{:S(2)}, u32[]{:S(2)}) collective-permute-start(bf16[64,512]{1,0:T(8,128)(2,1)S(1)} %get-tuple-element.39), channel_id=1, source_target_pairs={{0,1},{2,3},{4,5},{6,7},{8,9},{10,11},{12,13},{14,15},{16,17},{18,... | collective-permute-start | bytes 196616 | tf_op jit(solution)/shard_map/ppermute | solution.py:355
  13.0 4.7 %collective-permute-start = (bf16[64,512]{1,0:T(8,128)(2,1)S(1)}, bf16[64,512]{1,0:T(8,128)(2,1)S(1)}, u32[]{:S(2)}, u32[]{:S(2)}) collective-permute-start(bf16[64,512]{1,0:T(8,128)(2,1)S(1)} %get-tuple-element.40), channel_id=1, source_target_pairs={{1,2},{3,4},{5,6},{7,8},{9,10},{11,12},{13,14},{15,16},{17,18},{19... | collective-permute-start | bytes 196616 | tf_op jit(solution)/shard_map/ppermute | solution.py:355
  13.7 4.0 %copy-start.1 = (bf16[512,1024]{1,0:T(8,128)(2,1)S(1)}, bf16[512,1024]{1,0:T(8,128)(2,1)}, u32[]{:S(2)}) copy-start(bf16[512,1024]{1,0:T(8,128)(2,1)} %up.1) | copy-start | bytes 3145732
  13.7 4.0 %copy-start.2 = (bf16[1024,512]{1,0:T(8,128)(2,1)S(1)}, bf16[1024,512]{1,0:T(8,128)(2,1)}, u32[]{:S(2)}) copy-start(bf16[1024,512]{1,0:T(8,128)(2,1)} %down.1) | copy-start | bytes 3145732
  13.7 4.0 %copy-start.3 = (bf16[512,512]{1,0:T(8,128)(2,1)S(1)}, bf16[512,512]{1,0:T(8,128)(2,1)}, u32[]{:S(2)}) copy-start(bf16[512,512]{1,0:T(8,128)(2,1)} %msg.1) | copy-start | bytes 1572868
  19.6 11.1 %copy-start.4 = (bf16[512,512]{1,0:T(8,128)(2,1)S(1)}, bf16[512,512]{1,0:T(8,128)(2,1)}, u32[]{:S(2)}) copy-start(bf16[512,512]{1,0:T(8,128)(2,1)} %w_in.1) | copy-start | bytes 1572868
  25.4 21.7 %copy-start.7 = (bf16[128,512]{1,0:T(8,128)(2,1)S(1)}, bf16[128,512]{1,0:T(8,128)(2,1)}, u32[]{:S(2)}) copy-start(bf16[128,512]{1,0:T(8,128)(2,1)} %w_noise.1) | copy-start | bytes 393220
  25.4 21.7 %all-to-all-start.1 = ((bf16[8,64,640]{2,1,0:T(8,128)(2,1)}), bf16[8,64,640]{2,1,0:T(8,128)(2,1)S(1)}, u32[]{:S(2)}, u32[]{:S(2)}) async-start(bf16[8,64,640]{2,1,0:T(8,128)(2,1)} %bitcast.8), calls=%async_computation.1 | async-start | bytes 1310720 | tf_op jit(solution)/shard_map/all_to_all | solution.py:437
  31.1 0.8 copy-start.5
  53.8 4.6 %collective-permute-start.2 = (bf16[32,2,40,128]{3,2,1,0:T(8,128)(2,1)S(1)}, bf16[32,2,40,128]{3,2,1,0:T(8,128)(2,1)S(1)}, u32[]{:S(2)}, u32[]{:S(2)}) collective-permute-start(bf16[32,2,40,128]{3,2,1,0:T(8,128)(2,1)S(1)} %get-tuple-element.34), channel_id=1, source_target_pairs={{0,64},{64,0},{1,65},{65,1},{2,66},{66,2},{3,67},{67,3},{4,68},{68... | collective-permute-start | bytes 1966088 | tf_op jit(solution)/shard_map/ppermute | solution.py:490

commit v10 on v7

--- a/solution.py
+++ b/solution.py
@@ -39,12 +39,16 @@
     return count.astype(BF16)
 
 
-def teach(state, gathered, msg, up, down):
-    resid = state.astype(F32) + jnp.dot(gathered, msg, preferred_element_type=F32)
+def teach(state, gathered, msg, up, down, loads=()):
+    waits = [load.wait for load in loads] or [lambda: None] * 3
+    waits[0]()
+    resid = state.astype(F32) + jnp.dot(gathered, msg[...], preferred_element_type=F32)
     power = jnp.mean(resid * resid, axis=1, keepdims=True)
     normed = (resid * lax.rsqrt(power + 1e-06)).astype(BF16)
-    hidden = jax.nn.silu(jnp.dot(normed, up, preferred_element_type=F32)).astype(BF16)
-    return (resid + jnp.dot(hidden, down, preferred_element_type=F32)).astype(BF16)
+    waits[1]()
+    hidden = jax.nn.silu(jnp.dot(normed, up[...], preferred_element_type=F32)).astype(BF16)
+    waits[2]()
+    return (resid + jnp.dot(hidden, down[...], preferred_element_type=F32)).astype(BF16)
 
 
 def middle_kernel(
@@ -83,8 +87,6 @@
                 preferred_element_type=F32,
             ).astype(BF16)
         )
-    for copy in loads:
-        copy.wait()
     half = (CELLS - 2 * HALO) // 2
     gathered = jnp.concatenate(parts, axis=0)
     writes = []
@@ -92,9 +94,10 @@
         held[at : at + half] = teach(
             state[HALO + at : HALO + at + half],
             gathered[at : at + half],
-            msg[...],
-            up[...],
-            down[...],
+            msg,
+            up,
+            down,
+            loads if k == 0 else (),
         )
         rows = pl.ds(HALO + at, half)
         for target, wait in ((out.at[rows], 2 * k), (sent.at[rows, :D], 2 * k + 1)):
@@ -143,7 +146,7 @@
         axis=0,
     ).astype(BF16)
     ends = jnp.concatenate([state[:HALO], state[CELLS - HALO :]], axis=0)
-    held[...] = teach(ends, gathered, msg[...], up[...], down[...])
+    held[...] = teach(ends, gathered, msg, up, down)
     writes = [
         pltpu.make_async_copy(held.at[:HALO], out.at[:HALO], sem.at[0]),
         pltpu.make_async_copy(held.at[HALO:], out.at[CELLS - HALO :], sem.at[1]),

time: 105 us -> 105 us (level)
  transfers between devices with their start and end apart: 5 -> 5, of which waited for: 3 -> 3; matrix products, arithmetic and copies ran while one was open for 0% -> 0% of each run, Pallas kernels for 7% -> 6%
where the time goes in v10:
time: 105 us
  blocking collectives  45.5 us (43%)
  waiting for transfers between devices  22.7 us (22%)
  starting transfers between devices  20.4 us (19%)
  Pallas kernels  13.4 us (13%)
  between operations  1.47 us (1%)
    all_to_all x1, blocking collectives, step(): lax.all_to_all(half, ('tile_1', 'tile_2'), split_axis=0, concat_axis=0, t...  28.2 us
    all_to_all x1, blocking collectives, step(): lax.all_to_all(copies, ('tile_0', 'member_0', 'core'), split_axis=0, conc...  17.3 us
    all_to_all x1, waiting for transfers between devices, step(): lax.all_to_all(sent.reshape(MEMBERS, BLOCK, D + NOISE), MEMBER, split_axi...  15.2 us
    all_to_all x1, starting transfers between devices, step(): lax.all_to_all(state.reshape(MEMBERS, BLOCK, D), MEMBER, split_axis=0, co...  10.4 us
    pallas_call x1, Pallas kernels, step(): pl.pallas_call(score_kernel, out_shape=[jax.ShapeDtypeStruct((XY, 2, SHAR...  6.28 us
    all_to_all x1, waiting for transfers between devices, step(): lax.all_to_all(state.reshape(MEMBERS, BLOCK, D), MEMBER, split_axis=0, co...  5.8 us
    all_to_all x1, starting transfers between devices, step(): lax.all_to_all(sent.reshape(MEMBERS, BLOCK, D + NOISE), MEMBER, split_axi...  4.54 us
    pallas_call x1, Pallas kernels, step(): middle(state, noise[0], neighbours, in_hbm(msg_weight), in_hbm(up_weight)...  3.92 us
  transfers between devices with their start and end apart: 5, of which 3 were waited for; matrix products, arithmetic and copies ran while one was open for 0% of the time, Pallas kernels for 6%

profile of v10, /device:TPU:1, one launch (start us, length us, event | category | flops | bytes accessed | tf_op | source)
XLA Modules:
  0.0 104.5 jit_solution(15432045158479070964)
XLA Ops:
  0.7 10.4 %all-to-all-start = ((bf16[8,64,512]{2,1,0:T(8,128)(2,1)}), bf16[8,64,512]{2,1,0:T(8,128)(2,1)S(1)}, u32[]{:S(2)}, u32[]{:S(2)}) async-start(bf16[8,64,512]{2,1,0:T(8,128)(2,1)} %bitcast.13), calls=%async_computation | async-start | bytes 1048576 | tf_op jit(solution)/shard_map/all_to_all | solution.py:363
  11.1 1.9 %collective-permute-start.1 = (bf16[64,512]{1,0:T(8,128)(2,1)S(1)}, bf16[64,512]{1,0:T(8,128)(2,1)S(1)}, u32[]{:S(2)}, u32[]{:S(2)}) collective-permute-start(bf16[64,512]{1,0:T(8,128)(2,1)S(1)} %get-tuple-element.29), channel_id=1, source_target_pairs={{0,1},{2,3},{4,5},{6,7},{8,9},{10,11},{12,13},{14,15},{16,17},{18,... | collective-permute-start | bytes 196616 | tf_op jit(solution)/shard_map/ppermute | solution.py:338
  13.0 0.7 collective-permute-start
  13.7 0.0 copy-start.1
  13.7 0.0 copy-start.2
  13.7 0.0 copy-start.3
  13.7 3.9 %middle.1 = (bf16[512,512]{1,0:T(8,128)(2,1)}, bf16[512,640]{1,0:T(8,128)(2,1)}) custom-call(bf16[512,512]{1,0:T(8,128)(2,1)S(1)} %bitcast.14, bf16[512,128]{1,0:T(8,128)(2,1)S(1)} %bitcast.18, s32[8,512]{1,0:T(8,128)S(1)} %copy-done.9, bf16[512,512]{1,0:T(8,128)(2,1)} %msg.1, bf16[512,1024]{1,0:T(8,128)(2,1)} %up.1, bf16[1024,512]{1,0:T(8,128)(2,1)} %down.1), custom_call_target="tpu_custom_call" | custom-call | tf_op jit(solution)/shard_map/middle/pallas_call | solution.py:400
  17.6 0.0 collective-permute-done.1.even_swap
  17.7 1.9 %edges.1 = (bf16[512,512]{1,0:T(8,128)(2,1)}, bf16[512,640]{1,0:T(8,128)(2,1)}) custom-call(bf16[64,512]{1,0:T(8,128)(2,1)S(1)} %collective-permute-done.odd_swap, bf16[64,512]{1,0:T(8,128)(2,1)S(1)} %collective-permute-done.1.even_swap, bf16[512,512]{1,0:T(8,128)(2,1)S(1)} %bitcast.15, ...), custom_call_target="tpu_custom_call", output_to_operand_aliasing={{0}: (7, {}), {1}: (8, {})} | custom-call | tf_op jit(solution)/shard_map/edges/pallas_call | solution.py:408
  19.6 0.0 copy-start.4
  19.6 5.8 %all-to-all-done = bf16[8,64,512]{2,1,0:T(8,128)(2,1)S(1)} async-done(((bf16[8,64,512]{2,1,0:T(8,128)(2,1)}), bf16[8,64,512]{2,1,0:T(8,128)(2,1)S(1)}, u32[]{:S(2)}, u32[]{:S(2)}) %all-to-all-start) | async-done | bytes 524320 | tf_op jit(solution)/shard_map/all_to_all | solution.py:363
  25.4 4.5 %all-to-all-start.1 = ((bf16[8,64,640]{2,1,0:T(8,128)(2,1)}), bf16[8,64,640]{2,1,0:T(8,128)(2,1)S(1)}, u32[]{:S(2)}, u32[]{:S(2)}) async-start(bf16[8,64,640]{2,1,0:T(8,128)(2,1)} %bitcast.8), calls=%async_computation.1 | async-start | bytes 1310720 | tf_op jit(solution)/shard_map/all_to_all | solution.py:420
  30.6 0.1 pad_add_fusion.place
  30.7 0.4 student.1
  31.2 0.8 copy-done.6
  31.9 15.2 %all-to-all-done.1.every = bf16[8,64,640]{2,1,0:T(8,128)(2,1)S(1)} async-done(((bf16[8,64,640]{2,1,0:T(8,128)(2,1)}), bf16[8,64,640]{2,1,0:T(8,128)(2,1)S(1)}, u32[]{:S(2)}, u32[]{:S(2)}) %all-to-all-start.1) | async-done | bytes 655392 | tf_op jit(solution)/shard_map/all_to_all | solution.py:420
  47.2 6.3 %score.1 = (bf16[32,2,40,128]{3,2,1,0:T(8,128)(2,1)S(1)}, bf16[32,2,40,128]{3,2,1,0:T(8,128)(2,1)S(1)}) custom-call(f32[512,512]{1,0:T(8,128)S(1)} %get-tuple-element.20.early, bf16[512,512]{1,0:T(8,128)(2,1)S(1)} %bitcast.17, bf16[8,64,640]{2,1,0:T(8,128)(2,1)S(1)} %all-to-all-done.1.every, bf16[128,512]{1,0:T(8,128)(2,1)S(1)} %copy-done.8, ...), custom_call_target="tpu_custom_call" | custom-call | tf_op jit(solution)/shard_map/score/pallas_call | solution.py:441
  53.5 2.9 %collective-permute-start.2 = (bf16[32,2,40,128]{3,2,1,0:T(8,128)(2,1)S(1)}, bf16[32,2,40,128]{3,2,1,0:T(8,128)(2,1)S(1)}, u32[]{:S(2)}, u32[]{:S(2)}) collective-permute-start(bf16[32,2,40,128]{3,2,1,0:T(8,128)(2,1)S(1)} %get-tuple-element.24), channel_id=1, source_target_pairs={{0,64},{64,0},{1,65},{65,1},{2,66},{66,2},{3,67},{67,3},{4,68},{68... | collective-permute-start | bytes 1966088 | tf_op jit(solution)/shard_map/ppermute | solution.py:460
  56.4 1.7 %collective-permute-done.2 = bf16[32,2,40,128]{3,2,1,0:T(8,128)(2,1)S(1)} collective-permute-done((bf16[32,2,40,128]{3,2,1,0:T(8,128)(2,1)S(1)}, bf16[32,2,40,128]{3,2,1,0:T(8,128)(2,1)S(1)}, u32[]{:S(2)}, u32[]{:S(2)}) %collective-permute-start.2) | collective-permute-done | bytes 655392 | tf_op jit(solution)/shard_map/ppermute | solution.py:460
  58.1 0.2 add_convert_fusion
  58.2 28.2 %all_to_all.20.arrived = bf16[32,2,40,128]{3,2,1,0:T(8,128)(2,1)S(1)} all-to-all(bf16[32,2,40,128]{3,2,1,0:T(8,128)(2,1)S(1)} %add_convert_fusion), channel_id=1, replica_groups=mesh['member_0'=4,'core'=2,'tile_0'=2,'tile_1'=4,'tile_2'=8] {'tile_1','..., dimensions={0} | all-to-all | bytes 1310720 | tf_op jit(solution)/shard_map/all_to_all | solution.py:462
  86.4 0.2 fold.1
  86.6 17.3 %all_to_all.21.arrived = bf16[16,40,128]{2,1,0:T(8,128)(2,1)S(1)} all-to-all(bf16[16,40,128]{2,1,0:T(8,128)(2,1)S(1)} %fold.1), channel_id=1, replica_groups=mesh['member_0'=4,'core'=2,'tile_0'=2,'tile_1'=4,'tile_2'=8] {'tile_0','..., dimensions={0} | all-to-all | bytes 327680 | tf_op jit(solution)/shard_map/all_to_all | solution.py:471
  103.9 0.6 last.1
  (17 shorter events, 0.0 us)
Async XLA Ops:
  0.6 10.4 %copy-start = (bf16[1,512,512]{2,1,0:T(8,128)(2,1)S(1)}, bf16[1,512,512]{2,1,0:T(8,128)(2,1)}, u32[]{:S(2)}) copy-start(bf16[1,512,512]{2,1,0:T(8,128)(2,1)} %param.10) | copy-start | bytes 1572868
  0.6 13.0 %copy-start.9 = (s32[8,512]{1,0:T(8,128)S(1)}, s32[8,512]{1,0:T(8,128)}, u32[]{:S(2)}) copy-start(s32[8,512]{1,0:T(8,128)} %near.3) | copy-start | bytes 49156
  0.7 13.0 %copy-start.7 = (bf16[1,512,128]{2,1,0:T(8,128)(2,1)S(1)}, bf16[1,512,128]{2,1,0:T(8,128)(2,1)}, u32[]{:S(2)}) copy-start(bf16[1,512,128]{2,1,0:T(8,128)(2,1)} %param.11) | copy-start | bytes 393220
  0.7 24.8 %all-to-all-start = ((bf16[8,64,512]{2,1,0:T(8,128)(2,1)}), bf16[8,64,512]{2,1,0:T(8,128)(2,1)S(1)}, u32[]{:S(2)}, u32[]{:S(2)}) async-start(bf16[8,64,512]{2,1,0:T(8,128)(2,1)} %bitcast.13), calls=%async_computation | async-start | bytes 1048576 | tf_op jit(solution)/shard_map/all_to_all | solution.py:363
  11.1 6.6 %collective-permute-start.1 = (bf16[64,512]{1,0:T(8,128)(2,1)S(1)}, bf16[64,512]{1,0:T(8,128)(2,1)S(1)}, u32[]{:S(2)}, u32[]{:S(2)}) collective-permute-start(bf16[64,512]{1,0:T(8,128)(2,1)S(1)} %get-tuple-element.29), channel_id=1, source_target_pairs={{0,1},{2,3},{4,5},{6,7},{8,9},{10,11},{12,13},{14,15},{16,17},{18,... | collective-permute-start | bytes 196616 | tf_op jit(solution)/shard_map/ppermute | solution.py:338
  13.0 4.7 %collective-permute-start = (bf16[64,512]{1,0:T(8,128)(2,1)S(1)}, bf16[64,512]{1,0:T(8,128)(2,1)S(1)}, u32[]{:S(2)}, u32[]{:S(2)}) collective-permute-start(bf16[64,512]{1,0:T(8,128)(2,1)S(1)} %get-tuple-element.30), channel_id=1, source_target_pairs={{1,2},{3,4},{5,6},{7,8},{9,10},{11,12},{13,14},{15,16},{17,18},{19... | collective-permute-start | bytes 196616 | tf_op jit(solution)/shard_map/ppermute | solution.py:338
  13.7 4.0 %copy-start.1 = (bf16[512,1024]{1,0:T(8,128)(2,1)S(1)}, bf16[512,1024]{1,0:T(8,128)(2,1)}, u32[]{:S(2)}) copy-start(bf16[512,1024]{1,0:T(8,128)(2,1)} %up.1) | copy-start | bytes 3145732
  13.7 4.0 %copy-start.2 = (bf16[1024,512]{1,0:T(8,128)(2,1)S(1)}, bf16[1024,512]{1,0:T(8,128)(2,1)}, u32[]{:S(2)}) copy-start(bf16[1024,512]{1,0:T(8,128)(2,1)} %down.1) | copy-start | bytes 3145732
  13.7 4.0 %copy-start.3 = (bf16[512,512]{1,0:T(8,128)(2,1)S(1)}, bf16[512,512]{1,0:T(8,128)(2,1)}, u32[]{:S(2)}) copy-start(bf16[512,512]{1,0:T(8,128)(2,1)} %msg.1) | copy-start | bytes 1572868
  19.6 11.1 %copy-start.4 = (bf16[512,512]{1,0:T(8,128)(2,1)S(1)}, bf16[512,512]{1,0:T(8,128)(2,1)}, u32[]{:S(2)}) copy-start(bf16[512,512]{1,0:T(8,128)(2,1)} %w_in.1) | copy-start | bytes 1572868
  25.4 21.7 %copy-start.5 = (bf16[512,512]{1,0:T(8,128)(2,1)S(1)}, bf16[512,512]{1,0:T(8,128)(2,1)}, u32[]{:S(2)}) copy-start(bf16[512,512]{1,0:T(8,128)(2,1)} %w_out.1) | copy-start | bytes 1572868
  25.4 21.7 %copy-start.8 = (bf16[128,512]{1,0:T(8,128)(2,1)S(1)}, bf16[128,512]{1,0:T(8,128)(2,1)}, u32[]{:S(2)}) copy-start(bf16[128,512]{1,0:T(8,128)(2,1)} %w_noise.1) | copy-start | bytes 393220
  25.4 21.7 %all-to-all-start.1 = ((bf16[8,64,640]{2,1,0:T(8,128)(2,1)}), bf16[8,64,640]{2,1,0:T(8,128)(2,1)S(1)}, u32[]{:S(2)}, u32[]{:S(2)}) async-start(bf16[8,64,640]{2,1,0:T(8,128)(2,1)} %bitcast.8), calls=%async_computation.1 | async-start | bytes 1310720 | tf_op jit(solution)/shard_map/all_to_all | solution.py:420
  31.1 0.8 copy-start.6
  53.5 4.6 %collective-permute-start.2 = (bf16[32,2,40,128]{3,2,1,0:T(8,128)(2,1)S(1)}, bf16[32,2,40,128]{3,2,1,0:T(8,128)(2,1)S(1)}, u32[]{:S(2)}, u32[]{:S(2)}) collective-permute-start(bf16[32,2,40,128]{3,2,1,0:T(8,128)(2,1)S(1)} %get-tuple-element.24), channel_id=1, source_target_pairs={{0,64},{64,0},{1,65},{65,1},{2,66},{66,2},{3,67},{67,3},{4,68},{68... | collective-permute-start | bytes 1966088 | tf_op jit(solution)/shard_map/ppermute | solution.py:460
